TPU v7x, 256 devices: a whole 4x4x8 slice. The times are simulated.
256 devices in a mesh: seq: 64 (over x, z, core), head: 4 (over y).
Axes of the slice: x: 4, y: 4, z: 8, core: 2. Of those that a mesh axis runs over, the one named last changes fastest.
Arguments:
- tokens: bfloat16 [65536, 2048], P('seq', 'head'), may hold values from -6 to 6
- w_qkv: bfloat16 [2048, 6144], P(None, 'head'), may hold values from -1 to 1
- item_at: int32 [4, 2048], P('head'), may hold values from 0 to 2047, as said below
- rand_cols: int32 [16, 512, 4], P('head'), may hold values from 0 to 511, as said below
- rand_used: int32 [16, 512], P('head'), may hold values from 0 to 4, as said below
Outputs:
- attended: bfloat16 [4, 2048, 128, 128], P('head', 'seq')
Inputs may be any that keep to these rules, and one draw needn't show every extreme that they name: In head group g, item e * 512 + r stands for head g * 4 + e at block row r, and every item appears exactly once in item_at[g]. Positions j * 32 to (j + 1) * 32 - 1 hold the items placed at device j of seq. Of the items whose block rows lie on one device of seq, at most 1 of one group are placed at any one device, and exactly 1 at some. `rand_cols`: take all 128 candidates (used or not) of the items placed at one device in one head group, or of the items of one group whose block rows lie on one device: at most 2 of them lie in the block rows of any one device of seq, and exactly 2 in some. A candidate may equal a window block or block 0. `rand_used`: in each head group the counts of the 32 items placed at one device sum to exactly 64; the sums over the items whose block rows lie on one device vary.
All inputs are finite; a program needn't handle non-finite values.
Results may differ from a plain program's by a relative error of at most 0.019.
Values may be sent and summed in bfloat16 or wider, within the bound.
No kernel may reach another device: no remote copies, remote signals or barrier semaphores. Data moves between devices by JAX's collectives and lax.ppermute only.
A program may use at most 128 MiB of HBM per device.

v0:
```python
import math

import jax
import jax.numpy as jnp
from jax import lax
from jax.sharding import PartitionSpec as P

neg_large = -1e30


def extended(block, sides, width):
    for axis, dim in sides:
        count = lax.axis_size(axis)
        forward = [(i, i + 1) for i in range(count - 1)]
        backward = [(target, source) for source, target in forward]
        low = lax.ppermute(
            lax.slice_in_dim(block, block.shape[dim] - width, None, axis=dim), axis, forward
        )
        high = lax.ppermute(lax.slice_in_dim(block, 0, width, axis=dim), axis, backward)
        block = jnp.concatenate([low, block, high], axis=dim)
    return block


def broadcast(block, axis, owner):
    block = jnp.where(lax.axis_index(axis) == owner, block, jnp.zeros_like(block))
    return lax.psum(block, axis)


def packed_attend(
    queries, near_keys, near_values, near_usable, rand_keys, rand_values, slot_item, factor
):
    item_count = queries.shape[0]
    near_scores = (
        jnp.einsum("ibe,ijke->ibjk", queries, near_keys, preferred_element_type=jnp.float32)
        * factor
    )
    near_scores = jnp.where(near_usable[:, None, :, None], near_scores, neg_large)
    rand_scores = (
        jnp.einsum(
            "kbe,kce->kbc", queries[slot_item], rand_keys, preferred_element_type=jnp.float32
        )
        * factor
    )
    member = slot_item[None, :] == jnp.arange(item_count, dtype=jnp.int32)[:, None]
    slot_max = jnp.max(rand_scores, axis=2)
    rand_max = jnp.max(jnp.where(member[:, :, None], slot_max[None], neg_large), axis=1)
    row_max = jnp.maximum(jnp.max(near_scores, axis=(2, 3)), rand_max)
    near_expo = jnp.exp(near_scores - row_max[:, :, None, None])
    rand_expo = jnp.exp(rand_scores - row_max[slot_item][:, :, None])
    slot_total = jnp.sum(rand_expo, axis=2)
    row_sum = jnp.sum(near_expo, axis=(2, 3)) + jnp.sum(
        jnp.where(member[:, :, None], slot_total[None], 0.0), axis=1
    )
    summed = jnp.einsum(
        "ibjk,ijke->ibe",
        near_expo.astype(jnp.bfloat16),
        near_values,
        preferred_element_type=jnp.float32,
    )
    slot_out = jnp.einsum(
        "kbc,kce->kbe",
        rand_expo.astype(jnp.bfloat16),
        rand_values,
        preferred_element_type=jnp.float32,
    )
    summed = summed + jnp.einsum(
        "ik,kbe->ibe", member.astype(jnp.float32), slot_out, precision=lax.Precision.HIGHEST
    )
    return (summed, row_max, row_sum)


def rank_among(homes):
    count = homes.shape[-1]
    earlier = jnp.tril(jnp.ones((count, count), bool), -1)
    same_home = homes[..., :, None] == homes[..., None, :]
    return jnp.sum(same_home & earlier, axis=-1)


def pack_live(counts, rand_count, live_total):
    slot_total = counts.shape[0] * rand_count
    slot_ids = jnp.arange(slot_total, dtype=jnp.int32)
    live = slot_ids % rand_count < jnp.repeat(counts, rand_count)
    live_rank = jnp.cumsum(live.astype(jnp.int32)) - 1
    picks = live[:, None] & (live_rank[:, None] == jnp.arange(live_total, dtype=jnp.int32)[None, :])
    return jnp.sum(jnp.where(picks, slot_ids[:, None], 0), axis=0)


def local(tokens, w_qkv, item_at, rand_cols, rand_used):
    seq_count = lax.axis_size("seq")
    my_seq = lax.axis_index("seq")
    heads_dev, nblocks, rand_count = rand_cols.shape
    tokens_dev = tokens.shape[0]
    head_dim = w_qkv.shape[1] // (3 * heads_dev)
    block_len = tokens_dev * seq_count // nblocks
    rows_dev = tokens_dev // block_len
    items_dev = heads_dev * rows_dev
    slot_count = items_dev * rand_count
    live_total = slot_count // 2
    cap_items = max(1, items_dev // seq_count)
    cap_tiles = max(1, slot_count // seq_count)
    factor = 1.0 / math.sqrt(head_dim)
    projected = jnp.dot(
        lax.all_gather(tokens, "head", axis=1, tiled=True),
        w_qkv,
        preferred_element_type=jnp.float32,
    )
    projected = projected.astype(jnp.bfloat16).reshape(rows_dev, block_len, 3, heads_dev, head_dim)
    query_tiles = projected[:, :, 0].transpose(2, 0, 1, 3).reshape(items_dev, block_len, head_dim)
    pair_rows = projected[:, :, 1:].reshape(tokens_dev, 2, heads_dev, head_dim)
    widened = extended(pair_rows, (("seq", 0),), block_len)
    pair_tiles = widened.reshape(rows_dev + 2, block_len, 2, heads_dev, head_dim).transpose(
        3, 0, 2, 1, 4
    )
    own_tiles = pair_tiles[:, 1 : rows_dev + 1].reshape(items_dev, 2, block_len, head_dim)
    first_tiles = broadcast(pair_tiles[:, 1], "seq", 0)
    window_tiles = jnp.stack(
        [
            pair_tiles[:, 0:rows_dev],
            pair_tiles[:, 1 : rows_dev + 1],
            pair_tiles[:, 2 : rows_dev + 2],
        ],
        axis=2,
    )
    window_tiles = window_tiles.reshape(items_dev, 3, 2, block_len, head_dim)
    placed = item_at[0].reshape(seq_count, items_dev)
    placed_head = placed // nblocks
    placed_row = placed % nblocks
    placed_home = placed_row // rows_dev
    local_index = placed_head * rows_dev + placed_row % rows_dev
    is_mine = placed_home == my_seq
    rank_mine = jnp.cumsum(is_mine.astype(jnp.int32), axis=1) - 1
    slot_ids = jnp.arange(cap_items, dtype=jnp.int32)
    slot_hit = is_mine[:, :, None] & (rank_mine[:, :, None] == slot_ids)
    send_index = jnp.sum(jnp.where(slot_hit, local_index[:, :, None], 0), axis=1).reshape(-1)
    my_items = lax.dynamic_index_in_dim(placed, my_seq, 0, keepdims=False)
    item_head = my_items // nblocks
    item_row = my_items % nblocks
    item_home = item_row // rows_dev
    recv_slot = item_home * cap_items + rank_among(item_home)
    my_random = rand_cols[item_head, item_row].reshape(-1)
    tile_home = my_random // rows_dev
    tile_rank = rank_among(tile_home)
    tile_slot = tile_home * cap_tiles + tile_rank
    tile_ids = jnp.arange(cap_tiles, dtype=jnp.int32)
    peer_ids = jnp.arange(seq_count, dtype=jnp.int32)
    slot_head = jnp.repeat(item_head, rand_count)
    tile_local = slot_head * rows_dev + my_random % rows_dev
    wanted = (tile_home[None, :, None] == peer_ids[:, None, None]) & (
        tile_rank[None, :, None] == tile_ids[None, None, :]
    )
    requests = jnp.sum(jnp.where(wanted, tile_local[None, :, None], 0), axis=1)
    asked = lax.all_to_all(requests, "seq", split_axis=0, concat_axis=0, tiled=True)
    picked = own_tiles[asked.reshape(-1)].reshape(asked.shape + own_tiles.shape[1:])
    fetched = lax.all_to_all(picked, "seq", split_axis=0, concat_axis=0, tiled=True)
    gathered = fetched.reshape(seq_count * cap_tiles, 2, block_len, head_dim)[tile_slot]
    random_tiles = gathered.reshape(items_dev, rand_count, 2, block_len, head_dim)
    item_counts = rand_used[item_head, item_row]
    live_slots = pack_live(item_counts, rand_count, live_total)
    packed_tiles = random_tiles.reshape(slot_count, 2, block_len, head_dim)[live_slots]
    slot_item = live_slots // rand_count
    global_tiles = first_tiles[item_head][:, None]
    sent_query = query_tiles[send_index].reshape(seq_count, cap_items, block_len, head_dim)
    sent_window = window_tiles[send_index].reshape(seq_count, cap_items, 3, 2, block_len, head_dim)
    got_query, got_window = (
        lax.all_to_all(sent_query, "seq", split_axis=0, concat_axis=0, tiled=True),
        lax.all_to_all(sent_window, "seq", split_axis=0, concat_axis=0, tiled=True),
    )
    queries = got_query.reshape(seq_count * cap_items, block_len, head_dim)[recv_slot]
    windows = got_window.reshape(seq_count * cap_items, 3, 2, block_len, head_dim)[recv_slot]
    near_tiles = jnp.concatenate([windows, global_tiles], axis=1)
    near_usable = jnp.concatenate(
        [
            (item_row >= 1)[:, None],
            jnp.ones((items_dev, 1), bool),
            (item_row + 1 < nblocks)[:, None],
            jnp.ones((items_dev, 1), bool),
        ],
        axis=1,
    )
    summed, row_max, row_sum = packed_attend(
        queries,
        near_tiles[:, :, 0],
        near_tiles[:, :, 1],
        near_usable,
        packed_tiles[:, 0],
        packed_tiles[:, 1],
        slot_item,
        factor,
    )
    result = (summed / row_sum[:, :, None]).astype(jnp.bfloat16)
    return result.reshape(1, items_dev, block_len, head_dim)


def solution(mesh):
    return jax.shard_map(
        local,
        mesh=mesh,
        in_specs=(
            P("seq", "head"),
            P(None, "head"),
            P("head", None),
            P("head", None, None),
            P("head", None),
        ),
        out_specs=P("head", "seq", None, None),
        check_vma=False,
    )
```

profile of v0, /device:TPU:1, one launch (start us, length us, event | category | flops | bytes accessed | tf_op | source)
XLA Modules:
  0.0 679.1 jit_solution(8968216010016144075)
XLA Ops:
  6.5 0.7 all-gather.2.cloned.1.call-update
  7.3 0.5 broadcast.1180
  7.8 1.3 reduce.15
  9.2 1.1 copy.117
  10.4 0.2 convert_reduce_fusion.1
  10.6 0.6 fusion.78
  11.2 0.7 gather_fusion.7
  12.2 0.2 convert_reduce_fusion
  12.5 0.7 copy.118
  13.3 13.0 %all-to-all-start.2 = ((s32[64,1,2]{2,1,0:T(1,128)}), s32[64,1,2]{2,1,0:T(1,128)S(1)}, u32[]{:S(2)}, u32[]{:S(2)}) async-start(s32[64,1,2]{2,1,0:T(1,128)} %copy.118), calls=%async_computation.2 | async-start | bytes 65536 | tf_op jit(solution)/shard_map/all_to_all | solution.py:152
  26.3 0.2 reduce_window_sum.18
  26.5 0.8 reshape_squeeze.6
  27.5 36.4 %all-gather.2.cloned.1.call-done = bf16[1024,2048]{1,0:T(8,128)(2,1)} async-done(((bf16[1024,512]{1,0:T(8,128)(2,1)}), bf16[1024,2048]{1,0:T(8,128)(2,1)}) %all-gather.2.cloned.1.call-update) | async-done | bytes 4194320 | tf_op jit(solution)/shard_map/all_gather | solution.py:103
  63.8 11.2 %convolution_convert_fusion = bf16[1024,1536]{1,0:T(8,128)(2,1)} fusion(bf16[1024,2048]{1,0:T(8,128)(2,1)} %all-gather.2.cloned.1.call-done, bf16[2048,1536]{1,0:T(8,128)(2,1)} %param.6), kind=kOutput, calls=%fused_computation.35 | convolution fusion | flops 6444023808 | bytes 13631488 | tf_op jit(solution)/shard_map/dot_general | solution.py:102
  75.0 5.0 reshape.931
  80.0 0.4 slice.83
  80.4 1.2 copy.137
  81.6 3.3 gather_fusion
  85.0 10.9 %all-to-all-start = ((bf16[64,1,128,128]{3,2,1,0:T(8,128)(2,1)}), bf16[64,1,128,128]{3,2,1,0:T(8,128)(2,1)}, u32[]{:S(2)}, u32[]{:S(2)}) async-start(bf16[64,1,128,128]{3,2,1,0:T(8,128)(2,1)} %bitcast.166), calls=%async_computation | async-start | bytes 4194304 | tf_op jit(solution)/shard_map/all_to_all | solution.py:165
  95.9 0.2 fusion.85
  96.0 0.7 copy.160
  96.8 3.5 collective-permute-start
  100.3 0.7 copy.159
  101.1 2.1 collective-permute-start.1
  103.2 0.7 reduce.16
  104.1 0.7 slice.85
  104.8 0.5 copy.106
  105.3 38.3 %collective-permute-done = bf16[128,2,4,128]{3,0,2,1:T(8,128)(2,1)S(1)} collective-permute-done((bf16[128,2,4,128]{3,0,2,1:T(8,128)(2,1)}, bf16[128,2,4,128]{3,0,2,1:T(8,128)(2,1)S(1)}, u32[]{:S(2)}, u32[]{:S(2)}) %collective-permute-start) | collective-permute-done | bytes 262176 | tf_op jit(solution)/shard_map/ppermute | solution.py:16
  143.6 2.4 collective-permute-done.1
  146.0 1.1 pad_maximum_fusion.2
  147.1 0.3 copy.157
  147.5 3.7 fusion.86
  151.4 6.7 gather_fusion.8
  158.0 9.4 %all-to-all-start.3 = ((bf16[64,2,2,128,128]{4,3,2,1,0:T(8,128)(2,1)}), bf16[64,2,2,128,128]{4,3,2,1,0:T(8,128)(2,1)}, u32[]{:S(2)}, u32[]{:S(2)}) async-start(bf16[64,2,2,128,128]{4,3,2,1,0:T(8,128)(2,1)} %bitcast.161), calls=%async_computation.3 | async-start | bytes 16777216 | tf_op jit(solution)/shard_map/all_to_all | solution.py:154
  167.4 1.9 copy.109
  169.3 0.3 copy-done.5
  169.6 0.2 copy.111
  169.8 3.3 pad_maximum_fusion
  173.1 10.0 %gather_fusion.2 = bf16[64,3,2,128,128]{4,3,2,1,0:T(8,128)(2,1)} fusion(bf16[32,3,2,128,128]{4,3,2,0,1:T(8,128)(2,1)} %pad_maximum_fusion, s32[1024]{0:T(1024)S(1)} %pad_clamp_fusion.6), kind=kCustom, calls=%fused_computation.2 | custom fusion | bytes 25166080 | tf_op jit(solution)/shard_map/gather | solution.py:163
  183.1 170.0 %all-to-all-done.3 = bf16[64,2,2,128,128]{4,3,2,1,0:T(8,128)(2,1)} async-done(((bf16[64,2,2,128,128]{4,3,2,1,0:T(8,128)(2,1)}), bf16[64,2,2,128,128]{4,3,2,1,0:T(8,128)(2,1)}, u32[]{:S(2)}, u32[]{:S(2)}) %all-to-all-start.3) | async-done | bytes 8388640 | tf_op jit(solution)/shard_map/all_to_all | solution.py:154
  353.1 6.2 all-to-all-start.1
  359.3 0.3 all-reduce.2.cloned.1.call-start
  359.7 0.8 gather_fusion.5
  361.5 1.7 fusion.37
  363.4 221.4 %all-reduce.2.cloned.1.call-done = bf16[4,2,128,128]{3,2,1,0:T(8,128)(2,1)} async-done(((bf16[4,2,128,128]{3,2,1,0:T(8,128)(2,1)}), bf16[4,2,128,128]{3,2,1,0:T(8,128)(2,1)}) %all-reduce.2.cloned.1.call-update) | async-done | bytes 262160 | tf_op jit(solution)/shard_map/psum | solution.py:26
  584.7 1.9 gather_fusion.4
  586.6 1.5 copy.158
  588.1 2.3 gather_fusion.1
  590.5 1.0 gather_fusion.6
  591.4 10.0 %gather_fusion.9 = bf16[128,2,128,128]{3,2,1,0:T(8,128)(2,1)} fusion(bf16[128,2,128,128]{3,2,1,0:T(8,128)(2,1)} %bitcast.37, s32[1024]{0:T(1024)S(1)} %pad_clamp_fusion.1), kind=kCustom, calls=%fused_computation.9 | custom fusion | bytes 16777728 | tf_op jit(solution)/shard_map/gather | solution.py:155
  601.4 6.4 gather_fusion.10
  607.8 5.2 multiply_reduce_fusion
  613.1 0.4 select_reduce_fusion.1
  613.4 24.8 %all-to-all-done.1 = bf16[64,1,3,2,128,128]{5,4,3,2,1,0:T(8,128)(2,1)} async-done(((bf16[64,1,3,2,128,128]{5,4,3,2,1,0:T(8,128)(2,1)}), bf16[64,1,3,2,128,128]{5,4,3,2,1,0:T(8,128)(2,1)}, u32[]{:S(2)}, u32[]{:S(2)}) %all-to-all-start.1) | async-done | bytes 12582944 | tf_op jit(solution)/shard_map/all_to_all | solution.py:166
  638.3 8.7 %gather_fusion.3 = bf16[32,3,2,128,128]{4,3,2,1,0:T(8,128)(2,1)} fusion(bf16[64,3,2,128,128]{4,3,2,1,0:T(8,128)(2,1)} %bitcast.26, s32[1024]{0:T(1024)S(1)} %pad_clamp_fusion.5), kind=kCustom, calls=%fused_computation.3 | custom fusion | bytes 12583040 | tf_op jit(solution)/shard_map/gather | solution.py:169
  647.0 5.5 fusion
  652.5 0.6 gather_fusion.11
  653.1 3.3 fusion.18
  656.6 2.7 fusion.20
  659.3 0.4 select_reduce_fusion
  659.7 0.9 copy-done.4
  660.6 2.1 fusion.1
  662.7 4.1 fusion.12
  666.8 5.5 fusion.31
  (68 shorter events, 2.5 us)
Async XLA Ops:
  6.5 353.2 %copy-start = (s32[4,512]{1,0:T(4,128)S(1)}, s32[4,512]{1,0:T(4,128)}, u32[]{:S(2)}) copy-start(s32[4,512]{1,0:T(4,128)} %param.9) | copy-start | bytes 24580
  6.5 57.3 %all-gather.2.cloned.1.call-start = ((), (), s32[]{:S(2)}) async-start(), calls=%async_computation.4 | async-start | bytes 5242880 | tf_op jit(solution)/shard_map/all_gather | solution.py:103
  13.3 71.7 %all-to-all-start.2 = ((s32[64,1,2]{2,1,0:T(1,128)}), s32[64,1,2]{2,1,0:T(1,128)S(1)}, u32[]{:S(2)}, u32[]{:S(2)}) async-start(s32[64,1,2]{2,1,0:T(1,128)} %copy.118), calls=%async_computation.2 | async-start | bytes 65536 | tf_op jit(solution)/shard_map/all_to_all | solution.py:152
  85.0 73.0 %all-to-all-start = ((bf16[64,1,128,128]{3,2,1,0:T(8,128)(2,1)}), bf16[64,1,128,128]{3,2,1,0:T(8,128)(2,1)}, u32[]{:S(2)}, u32[]{:S(2)}) async-start(bf16[64,1,128,128]{3,2,1,0:T(8,128)(2,1)} %bitcast.166), calls=%async_computation | async-start | bytes 4194304 | tf_op jit(solution)/shard_map/all_to_all | solution.py:165
  96.8 46.8 %collective-permute-start = (bf16[128,2,4,128]{3,0,2,1:T(8,128)(2,1)}, bf16[128,2,4,128]{3,0,2,1:T(8,128)(2,1)S(1)}, u32[]{:S(2)}, u32[]{:S(2)}) collective-permute-start(bf16[128,2,4,128]{3,0,2,1:T(8,128)(2,1)} %bitcast.157), channel_id=1, source_target_pairs={{0,4},{4,8},{8,12},{12,16},{16,20},{20,24},{24,28},{28,32},{32,36}... | collective-permute-start | bytes 786440 | tf_op jit(solution)/shard_map/ppermute | solution.py:16
  101.1 44.9 %collective-permute-start.1 = (bf16[128,2,4,128]{3,0,2,1:T(8,128)(2,1)}, bf16[128,2,4,128]{3,0,2,1:T(8,128)(2,1)}, u32[]{:S(2)}, u32[]{:S(2)}) collective-permute-start(bf16[128,2,4,128]{3,0,2,1:T(8,128)(2,1)} %bitcast.156), channel_id=1, source_target_pairs={{4,0},{8,4},{12,8},{16,12},{20,16},{24,20},{28,24},{32,28},{36,32}... | collective-permute-start | bytes 786440 | tf_op jit(solution)/shard_map/ppermute | solution.py:19
  147.5 3.8 copy-start.3
  158.0 195.1 %all-to-all-start.3 = ((bf16[64,2,2,128,128]{4,3,2,1,0:T(8,128)(2,1)}), bf16[64,2,2,128,128]{4,3,2,1,0:T(8,128)(2,1)}, u32[]{:S(2)}, u32[]{:S(2)}) async-start(bf16[64,2,2,128,128]{4,3,2,1,0:T(8,128)(2,1)} %bitcast.161), calls=%async_computation.3 | async-start | bytes 16777216 | tf_op jit(solution)/shard_map/all_to_all | solution.py:154
  167.4 2.2 copy-start.5
  353.1 7.9 %copy-start.7 = (s32[32]{0:T(128)S(1)}, s32[32]{0:T(128)}, u32[]{:S(2)}) copy-start(s32[32]{0:T(128)} %get-tuple-element.21) | copy-start | bytes 388
  353.1 285.1 %all-to-all-start.1 = ((bf16[64,1,3,2,128,128]{5,4,3,2,1,0:T(8,128)(2,1)}), bf16[64,1,3,2,128,128]{5,4,3,2,1,0:T(8,128)(2,1)}, u32[]{:S(2)}, u32[]{:S(2)}) async-start(bf16[64,1,3,2,128,128]{5,4,3,2,1,0:T(8,128)(2,1)} %bitcast.160), calls=%async_computation.1 | async-start | bytes 25165824 | tf_op jit(solution)/shard_map/all_to_all | solution.py:166
  359.3 225.4 %all-reduce.2.cloned.1.call-start = ((), (), s32[]{:S(2)}) async-start(), calls=%async_computation.5 | async-start | bytes 524288 | tf_op jit(solution)/shard_map/psum | solution.py:26
  638.3 8.7 %copy-start.6 = (bf16[32,2,128,128]{3,2,0,1:T(8,128)(2,1)S(1)}, bf16[32,2,128,128]{3,2,0,1:T(8,128)(2,1)}, u32[]{:S(2)}) copy-start(bf16[32,2,128,128]{3,2,0,1:T(8,128)(2,1)} %copy.158) | copy-start | bytes 6291460
  653.1 3.4 copy-start.2
  656.6 4.0 copy-start.4
  656.6 10.2 %slice-start = ((s8[6291456]{0:T(1024)(128)(4,1)}), s8[4194304]{0:T(1024)(128)(4,1)S(1)}, s32[]{:S(2)}) async-start(s8[6291456]{0:T(1024)(128)(4,1)} %bitcast.170), calls=%async_computation.6 | async-start | bytes 8388608
  660.6 6.2 slice-start.1
  666.8 5.5 copy-start.1
Sparse Core Ops, SparseCore 0:
  9.2 54.5 all-gather.1
  363.7 221.0 all-reduce.1
where the time goes:
time: 680 us; the launch traced here: 679 us
  waiting for transfers between devices  494 us (73%)
  local copies, waits for them, and re-layouts  75.2 us (11%)
  starting transfers between devices  45.3 us (7%)
  matrix products  34.2 us (5%)
  other arithmetic  16.5 us (2%)
  between operations  13.8 us (2%)
    psum x1, waiting for transfers between devices, broadcast(): return lax.psum(block, axis)  221 us
    all_to_all x1, waiting for transfers between devices, local(): lax.all_to_all(picked, 'seq', split_axis=0, concat_axis=0, tiled=True)  170 us
    ppermute x1, waiting for transfers between devices, extended(): lax.ppermute(lax.slice_in_dim(block, block.shape[dim] - width, None, axis...  38.3 us
    all_gather x1, waiting for transfers between devices, local(): lax.all_gather(tokens, 'head', axis=1, tiled=True)  36.4 us
    all_to_all x1, waiting for transfers between devices, local(): lax.all_to_all(sent_window, 'seq', split_axis=0, concat_axis=0, tiled=True)  24.8 us
  transfers between devices with their start and end apart: 8, of which 6 were waited for; matrix products, arithmetic and copies ran while one was open for 14% of the time, Pallas kernels for 0%

commit v1 on v0

v1 whole, which is shorter than its diff:
```python
import math

import jax
import jax.numpy as jnp
from jax import lax
from jax.experimental import pallas as pl
from jax.experimental.pallas import tpu as pltpu
from jax.sharding import PartitionSpec as P

NEG = -1e30
BF = jnp.bfloat16
F32 = jnp.float32
VMEM_BYTES = 48 << 20


def dot_t(a, b):
    return lax.dot_general(a, b, (((1,), (1,)), ((), ())), preferred_element_type=F32)


def pack_tiles(index, proj, slots, rows, heads, blk, hd):
    step = 8

    def kernel(index_ref, k_ref, v_ref, out_ref):
        first = pl.program_id(0) * step
        for j in range(step):
            tile = index_ref[first + j]
            row = pl.ds(pl.multiple_of((tile % rows) * blk, blk), blk)
            col = pl.ds(pl.multiple_of((tile // rows) * hd, hd), hd)
            out_ref[j, 0] = k_ref[row, col]
            out_ref[j, 1] = v_ref[row, col]

    tokens, width = proj.shape[0], heads * hd
    return pl.pallas_call(
        kernel,
        out_shape=jax.ShapeDtypeStruct((slots, 2, blk, hd), BF),
        grid_spec=pltpu.PrefetchScalarGridSpec(
            num_scalar_prefetch=1,
            grid=(slots // step,),
            in_specs=[
                pl.BlockSpec((tokens, width), lambda i, s: (0, 1)),
                pl.BlockSpec((tokens, width), lambda i, s: (0, 2)),
            ],
            out_specs=pl.BlockSpec((step, 2, blk, hd), lambda i, s: (i, 0, 0, 0)),
        ),
        compiler_params=pltpu.CompilerParams(vmem_limit_bytes=VMEM_BYTES),
        name="pack_tiles",
    )(index, proj, proj)


def near_attend(edges, proj, around, first, rows, heads, blk, hd, factor):
    width = heads * hd

    def kernel(edge_ref, q_ref, kv_ref, first_ref, acc_ref, stat_ref):
        r = pl.program_id(0)
        window = pl.ds(pl.multiple_of(r * blk, blk), 3 * blk)
        lane = lax.broadcasted_iota(jnp.int32, (blk, 3 * blk), 1)
        low = jnp.where((r == 0) & (edge_ref[0] == 1), blk, 0)
        high = jnp.where((r == rows - 1) & (edge_ref[1] == 1), 2 * blk, 3 * blk)
        usable = (lane >= low) & (lane < high)
        half = lax.broadcasted_iota(jnp.int32, (blk, hd), 1) < hd // 2
        for e in range(heads):
            cols = slice(e * hd, (e + 1) * hd)
            vcols = slice(width + e * hd, width + (e + 1) * hd)
            q = q_ref[:, cols]
            near = jnp.where(usable, dot_t(q, kv_ref[window, cols]) * factor, NEG)
            glob = dot_t(q, first_ref[:, cols]) * factor
            top = jnp.maximum(
                jnp.max(near, axis=1, keepdims=True), jnp.max(glob, axis=1, keepdims=True)
            )
            near = jnp.exp(near - top)
            glob = jnp.exp(glob - top)
            total = jnp.sum(near, axis=1, keepdims=True) + jnp.sum(glob, axis=1, keepdims=True)
            acc_ref[e] = jnp.dot(
                near.astype(BF), kv_ref[window, vcols], preferred_element_type=F32
            ) + jnp.dot(glob.astype(BF), first_ref[:, vcols], preferred_element_type=F32)
            stat_ref[e] = jnp.where(half, top, total)

    out = jax.ShapeDtypeStruct((rows * heads, blk, hd), F32)
    return pl.pallas_call(
        kernel,
        out_shape=(out, out),
        grid_spec=pltpu.PrefetchScalarGridSpec(
            num_scalar_prefetch=1,
            grid=(rows,),
            in_specs=[
                pl.BlockSpec((blk, width), lambda r, s: (r, 0)),
                pl.BlockSpec(around.shape, lambda r, s: (0, 0)),
                pl.BlockSpec(first.shape, lambda r, s: (0, 0)),
            ],
            out_specs=(
                pl.BlockSpec((heads, blk, hd), lambda r, s: (r, 0, 0)),
                pl.BlockSpec((heads, blk, hd), lambda r, s: (r, 0, 0)),
            ),
        ),
        compiler_params=pltpu.CompilerParams(vmem_limit_bytes=VMEM_BYTES),
        name="near_attend",
    )(edges, proj, around, first)


def rand_attend(slot, count, target, proj, tiles, acc, stat, rows, heads, blk, hd, rand, peers, factor):
    items = rows * heads

    def kernel(slot_ref, count_ref, target_ref, q_ref, *refs):
        kv = refs[:rand]
        acc_ref, stat_ref, out_ref = refs[rand:]
        used = count_ref[pl.program_id(0)]
        q = q_ref[...]
        stats = stat_ref[0]
        top0, total0 = stats[:, 0:1], stats[:, hd // 2 : hd // 2 + 1]
        scores = [
            jnp.where(j < used, dot_t(q, kv[j][0, 0]) * factor, NEG) for j in range(rand)
        ]
        best = scores[0]
        for s in scores[1:]:
            best = jnp.maximum(best, s)
        top = jnp.maximum(jnp.max(best, axis=1, keepdims=True), top0)
        keep = jnp.exp(top0 - top)
        summed = acc_ref[0] * keep
        sums = None
        for j in range(rand):
            w = jnp.exp(scores[j] - top)
            sums = w if sums is None else sums + w
            summed += jnp.dot(w.astype(BF), kv[j][0, 1], preferred_element_type=F32)
        total = total0 * keep + jnp.sum(sums, axis=1, keepdims=True)
        out_ref[0] = (summed / total).astype(BF)

    def tile_spec(j):
        return pl.BlockSpec((1, 2, blk, hd), lambda i, s, c, t: (s[i * rand + j], 0, 0, 0))

    return pl.pallas_call(
        kernel,
        out_shape=jax.ShapeDtypeStruct((peers, blk, hd), BF),
        grid_spec=pltpu.PrefetchScalarGridSpec(
            num_scalar_prefetch=3,
            grid=(items,),
            in_specs=[
                pl.BlockSpec((blk, hd), lambda i, s, c, t: (i // heads, i % heads)),
                *[tile_spec(j) for j in range(rand)],
                pl.BlockSpec((1, blk, hd), lambda i, s, c, t: (i, 0, 0)),
                pl.BlockSpec((1, blk, hd), lambda i, s, c, t: (i, 0, 0)),
            ],
            out_specs=pl.BlockSpec((1, blk, hd), lambda i, s, c, t: (t[i], 0, 0)),
        ),
        compiler_params=pltpu.CompilerParams(vmem_limit_bytes=VMEM_BYTES),
        name="rand_attend",
    )(slot, count, target, proj, *[tiles] * rand, acc, stat)


def take_tiles(index, tiles):
    count = index.shape[0]

    def kernel(index_ref, in_ref, out_ref, sems):
        copies = [
            pltpu.make_async_copy(in_ref.at[index_ref[i]], out_ref.at[i], sems.at[i])
            for i in range(count)
        ]
        for copy in copies:
            copy.start()
        for copy in copies:
            copy.wait()

    return pl.pallas_call(
        kernel,
        out_shape=jax.ShapeDtypeStruct((count, *tiles.shape[1:]), tiles.dtype),
        grid_spec=pltpu.PrefetchScalarGridSpec(
            num_scalar_prefetch=1,
            grid=(1,),
            in_specs=[pl.BlockSpec(memory_space=pl.ANY)],
            out_specs=pl.BlockSpec(memory_space=pl.ANY),
            scratch_shapes=[pltpu.SemaphoreType.DMA((count,))],
        ),
        name="take_tiles",
    )(index, tiles)


def local(tokens, w_qkv, item_at, rand_cols, rand_used):
    peers = lax.axis_size("seq")
    me = lax.axis_index("seq")
    heads, nblocks, rand = rand_cols.shape
    rows = nblocks // peers
    blk = tokens.shape[0] // rows
    hd = w_qkv.shape[1] // (3 * heads)
    width = heads * hd
    items = heads * rows
    factor = 1.0 / math.sqrt(hd)

    asked = rand_cols.reshape(heads, peers, rows, rand).transpose(1, 2, 0, 3)
    asked = asked.reshape(peers, items * rand)
    head_of = (jnp.arange(items * rand, dtype=jnp.int32) // rand) % heads
    order = jnp.arange(items * rand, dtype=jnp.int32)
    code = order * items + head_of * rows + asked % rows
    mine = asked // rows == me
    low = jnp.min(jnp.where(mine, code, jnp.int32(1 << 30)), axis=1) % items
    high = jnp.max(jnp.where(mine, code, 0), axis=1) % items
    send_tile = jnp.stack([low, high], axis=1).reshape(-1)
    wanted = lax.dynamic_index_in_dim(asked, me, 0, keepdims=False)
    source = wanted // rows
    again = jnp.sum(
        ((source[:, None] == source[None, :]) & (order[None, :] < order[:, None])).astype(jnp.int32),
        axis=1,
    )
    slot = source * 2 + again
    my_used = lax.dynamic_slice_in_dim(rand_used, me * rows, rows, axis=1).T.reshape(-1)
    number = jnp.arange(items, dtype=jnp.int32)
    my_item = (number % heads) * nblocks + me * rows + number // heads
    place = jnp.arange(peers * items, dtype=jnp.int32)
    target = jnp.sum(
        jnp.where(item_at[0][None, :] == my_item[:, None], place[None, :] // items, 0), axis=1
    )
    home = (lax.dynamic_slice_in_dim(item_at[0], me * items, items) % nblocks) // rows
    edges = jnp.stack([me == 0, me == peers - 1]).astype(jnp.int32)

    proj = jnp.dot(
        lax.all_gather(tokens, "head", axis=1, tiled=True), w_qkv, preferred_element_type=F32
    ).astype(BF)
    sent = pack_tiles(send_tile, proj, 2 * peers, rows, heads, blk, hd)
    up = [(i, i + 1) for i in range(peers - 1)]
    down = [(b, a) for a, b in up]
    pair = proj[:, width:]
    before = lax.ppermute(pair[-blk:], "seq", up)
    after = lax.ppermute(pair[:blk], "seq", down)
    first = pair[:blk]
    first = lax.psum(jnp.where(me == 0, first, jnp.zeros_like(first)), "seq")
    around = jnp.concatenate([before, pair, after], axis=0)

    tiles = lax.all_to_all(sent, "seq", split_axis=0, concat_axis=0, tiled=True)
    acc, stat = near_attend(edges, proj, around, first, rows, heads, blk, hd, factor)
    done = rand_attend(
        slot, my_used, target, proj, tiles, acc, stat, rows, heads, blk, hd, rand, peers, factor
    )
    back = lax.all_to_all(done, "seq", split_axis=0, concat_axis=0, tiled=True)
    return take_tiles(home, back)[None]


def solution(mesh):
    return jax.shard_map(
        local,
        mesh=mesh,
        in_specs=(
            P("seq", "head"),
            P(None, "head"),
            P("head", None),
            P("head", None, None),
            P("head", None),
        ),
        out_specs=P("head", "seq", None, None),
        check_vma=False,
    )
```

time: 680 us -> 461 us (0.68)
  waiting for transfers between devices: 494 us -> 313 us
  Pallas kernels: 0 us -> 84.5 us
  local copies, waits for them, and re-layouts: 75.2 us -> 8.06 us
  matrix products: 34.2 us -> 10 us
  starting transfers between devices: 45.3 us -> 23.2 us
  other arithmetic: 16.5 us -> 6.45 us
    psum x1, waiting for transfers between devices: 221 us -> 29.9 us  [local(): first = lax.psum(jnp.where(me == 0, first, jnp.zeros_like(first)), 'seq')]
    all_to_all x4 -> x2, waiting for transfers between devices: 195 us -> 50.6 us  [the longest x1 50.6 us: local(): back = lax.all_to_all(done, 'seq', split_axis=0, concat_axis=0, tiled=True)]
    ppermute x2, waiting for transfers between devices: 40.7 us -> 177 us  [the longest x1 177 us: local(): after = lax.ppermute(pair[:blk], 'seq', down)]
    pallas_call x0 -> x4, Pallas kernels: none -> 84.5 us  [the longest x1 33.8 us: take_tiles(): pl.pallas_call(kernel, out_shape=jax.ShapeDtypeStruct((count, *tiles.shap...]
    gather x13 -> x0, local copies, waits for them, and re-layouts: 53.9 us -> none  [the longest x1 9.99 us: local(): window_tiles[send_index]]
    dot_general x5 -> x0, matrix products: 23 us -> none  [the longest x1 5.5 us: packed_attend(): jnp.einsum('ibe,ijke->ibjk', queries, near_keys, preferred_element_type=j...]
    all_to_all x4 -> x2, starting transfers between devices: 39.4 us -> 17.6 us  [the longest x1 11 us: local(): tiles = lax.all_to_all(sent, 'seq', split_axis=0, concat_axis=0, tiled=True)]
    all_gather x1, waiting for transfers between devices: 36.4 us -> 54.4 us  [local(): lax.all_gather(tokens, 'head', axis=1, tiled=True)]
  transfers between devices with their start and end apart: 8 -> 6, of which waited for: 6 -> 4; matrix products, arithmetic and copies ran while one was open for 14% -> 2% of each run, Pallas kernels for 0% -> 3%
where the time goes in v1:
time: 461 us; the launch traced here: 459 us
  waiting for transfers between devices  313 us (68%)
  Pallas kernels  84.5 us (18%)
  starting transfers between devices  23.2 us (5%)
  between operations  13.6 us (3%)
  matrix products  10 us (2%)
  local copies, waits for them, and re-layouts  8.06 us (2%)
  other arithmetic  6.45 us (1%)
    ppermute x1, waiting for transfers between devices, local(): after = lax.ppermute(pair[:blk], 'seq', down)  177 us
    all_gather x1, waiting for transfers between devices, local(): lax.all_gather(tokens, 'head', axis=1, tiled=True)  54.4 us
    all_to_all x1, waiting for transfers between devices, local(): back = lax.all_to_all(done, 'seq', split_axis=0, concat_axis=0, tiled=True)  50.6 us
    pallas_call x1, Pallas kernels, take_tiles(): pl.pallas_call(kernel, out_shape=jax.ShapeDtypeStruct((count, *tiles.shap...  33.8 us
    psum x1, waiting for transfers between devices, local(): first = lax.psum(jnp.where(me == 0, first, jnp.zeros_like(first)), 'seq')  29.9 us
    pallas_call x1, Pallas kernels, rand_attend(): pl.pallas_call(kernel, out_shape=jax.ShapeDtypeStruct((peers, blk, hd), B...  28.8 us
    pallas_call x1, Pallas kernels, near_attend(): pl.pallas_call(kernel, out_shape=(out, out), grid_spec=pltpu.PrefetchScal...  13.4 us
    all_to_all x1, starting transfers between devices, local(): tiles = lax.all_to_all(sent, 'seq', split_axis=0, concat_axis=0, tiled=True)  11 us
  transfers between devices with their start and end apart: 6, of which 4 were waited for; matrix products, arithmetic and copies ran while one was open for 2% of the time, Pallas kernels for 3%

profile of v1, /device:TPU:1, one launch (start us, length us, event | category | flops | bytes accessed | tf_op | source)
XLA Modules:
  0.0 458.6 jit_solution(17985269326258732789)
XLA Ops:
  6.5 0.0 copy-start
  6.5 0.0 all-gather.2.cloned.1.call-start
  6.5 0.7 all-gather.2.cloned.1.call-update
  7.3 1.1 reshape.217
  8.3 0.0 copy-start.5
  8.4 0.7 select_reduce_fusion.1
  9.1 0.1 copy.17
  9.2 0.1 reshape.220.index_ref
  9.4 0.0 copy-done.5
  9.4 54.4 %all-gather.2.cloned.1.call-done = bf16[1024,2048]{1,0:T(8,128)(2,1)} async-done(((bf16[1024,512]{1,0:T(8,128)(2,1)}), bf16[1024,2048]{1,0:T(8,128)(2,1)}) %all-gather.2.cloned.1.call-update) | async-done | bytes 4194320 | tf_op jit(solution)/shard_map/all_gather | solution.py:214
  63.8 10.0 %convolution_convert_fusion.k_ref.v_ref.q_ref = bf16[1024,1536]{1,0:T(8,128)(2,1)S(1)} fusion(bf16[1024,2048]{1,0:T(8,128)(2,1)} %all-gather.2.cloned.1.call-done, bf16[2048,1536]{1,0:T(8,128)(2,1)} %param.6), kind=kOutput, calls=%fused_computation | convolution fusion | flops 6444023808 | bytes 13631488 | tf_op jit(solution)/shard_map/dot_general | solution.py:213
  73.8 0.0 copy-start.1
  73.8 8.6 %pack_tiles.1 = bf16[128,2,128,128]{3,2,1,0:T(8,128)(2,1)} custom-call(s32[128]{0:T(128)S(1)} %reshape.220.index_ref, bf16[1024,1536]{1,0:T(8,128)(2,1)S(1)} %convolution_convert_fusion.k_ref.v_ref.q_ref, bf16[1024,1536]{1,0:T(8,128)(2,1)S(1)} %convolution_convert_fusion.k_ref.v_ref.q_ref), custom_call_target="tpu_custom_call" | custom-call | tf_op jit(solution)/shard_map/pack_tiles/pallas_call | solution.py:33
  82.4 0.0 copy-start.6
  82.4 11.0 %all-to-all-start = ((bf16[128,2,128,128]{3,2,1,0:T(8,128)(2,1)}), bf16[128,2,128,128]{3,2,1,0:T(8,128)(2,1)}, u32[]{:S(2)}, u32[]{:S(2)}) async-start(bf16[128,2,128,128]{3,2,1,0:T(8,128)(2,1)} %pack_tiles.1), calls=%async_computation | async-start | bytes 16777216 | tf_op jit(solution)/shard_map/all_to_all | solution.py:226
  93.5 0.0 all-reduce.2.cloned.1.call-start
  93.5 1.2 copy.15
  94.8 0.2 dynamic-slice_reduce_fusion
  95.0 0.0 copy-done
  95.0 0.1 dynamic-slice_bitcast_fusion
  95.1 0.2 convert_reduce_fusion
  95.3 0.0 copy-done.6
  95.3 0.2 select_reduce_fusion.2.target_ref
  95.5 0.8 broadcast_select_fusion
  96.3 2.4 collective-permute-start.1
  98.8 3.1 collective-permute-start
  101.9 0.1 add_convert_fusion.edge_ref
  102.0 0.1 copy.16
  102.0 0.1 reshape.219.count_ref
  102.1 0.0 copy-done.1
  102.2 1.6 slice.16
  103.8 0.0 all-reduce.2.cloned.1.call-update
  103.8 177.1 %collective-permute-done.1 = bf16[128,1024]{1,0:T(8,128)(2,1)} collective-permute-done((bf16[128,1024]{1,0:T(8,128)(2,1)}, bf16[128,1024]{1,0:T(8,128)(2,1)}, u32[]{:S(2)}, u32[]{:S(2)}) %collective-permute-start.1) | collective-permute-done | bytes 262176 | tf_op jit(solution)/shard_map/ppermute | solution.py:221
  281.0 0.0 collective-permute-done
  281.0 3.5 pad_maximum_fusion.kv_ref
  284.4 29.9 %all-reduce.2.cloned.1.call-done.first_ref = bf16[128,1024]{1,0:T(8,128)(2,1)} async-done(((bf16[128,1024]{1,0:T(8,128)(2,1)}), bf16[128,1024]{1,0:T(8,128)(2,1)}) %all-reduce.2.cloned.1.call-update) | async-done | bytes 262160 | tf_op jit(solution)/shard_map/psum | solution.py:223
  314.4 0.0 copy-start.3
  314.4 0.9 copy-done.3
  315.3 13.4 %near_attend.1 = (f32[32,128,128]{2,1,0:T(8,128)S(1)}, f32[32,128,128]{2,1,0:T(8,128)S(1)}) custom-call(s32[2]{0:T(128)S(1)} %add_convert_fusion.edge_ref, bf16[1024,1536]{1,0:T(8,128)(2,1)} %copy-done.1, bf16[1280,1024]{1,0:T(8,128)(2,1)} %pad_maximum_fusion.kv_ref, bf16[128,1024]{1,0:T(8,128)(2,1)S(1)} %copy-done.3), custom_call_target="tpu_custom_call" | custom-call | tf_op jit(solution)/shard_map/near_attend/pallas_call | solution.py:79
  328.7 0.0 copy-start.2
  328.7 1.3 copy-done.2
  330.0 0.0 all-to-all-done.refs_0_.refs_1_.refs_2_.refs_3_
  330.0 28.8 %rand_attend.1 = bf16[64,128,128]{2,1,0:T(8,128)(2,1)} custom-call(s32[128]{0:T(128)S(1)} %multiply_add_fusion.1.slot_ref, s32[32]{0:T(128)S(1)} %reshape.219.count_ref, s32[32]{0:T(128)S(1)} %select_reduce_fusion.2.target_ref, bf16[1024,1536]{1,0:T(8,128)(2,1)} %copy-done.1, bf16[128,2,128,128]{3,2,1,0:T(8,128)(2,1)} %all-to-all-done.refs_0_.refs_1_.refs_2_.refs_3_, ...), custom_call_target="tpu_custom_call" | custom-call | tf_op jit(solution)/shard_map/rand_attend/pallas_call | solution.py:130
  358.8 6.5 %all-to-all-start.1 = ((bf16[64,128,128]{2,1,0:T(8,128)(2,1)}), bf16[64,128,128]{2,1,0:T(8,128)(2,1)S(1)}, u32[]{:S(2)}, u32[]{:S(2)}) async-start(bf16[64,128,128]{2,1,0:T(8,128)(2,1)} %rand_attend.1), calls=%async_computation.1 | async-start | bytes 4194304 | tf_op jit(solution)/shard_map/all_to_all | solution.py:231
  365.3 0.7 and_select_fusion.5.index_ref
  366.0 50.6 %all-to-all-done.1.in_ref = bf16[64,128,128]{2,1,0:T(8,128)(2,1)S(1)} async-done(((bf16[64,128,128]{2,1,0:T(8,128)(2,1)}), bf16[64,128,128]{2,1,0:T(8,128)(2,1)S(1)}, u32[]{:S(2)}, u32[]{:S(2)}) %all-to-all-start.1) | async-done | bytes 2097184 | tf_op jit(solution)/shard_map/all_to_all | solution.py:231
  416.6 0.0 copy-start.4
  416.6 1.3 copy-done.4
  417.9 33.8 %take_tiles.1 = bf16[32,128,128]{2,1,0:T(8,128)(2,1)} custom-call(s32[32]{0:T(128)} %and_select_fusion.5.index_ref, bf16[64,128,128]{2,1,0:T(8,128)(2,1)} %copy-done.4), custom_call_target="tpu_custom_call" | custom-call | tf_op jit(solution)/shard_map/take_tiles/pallas_call | solution.py:162
  (7 shorter events, 0.1 us)
Async XLA Ops:
  6.5 88.4 %copy-start = (s32[4,512]{1,0:T(4,128)S(1)}, s32[4,512]{1,0:T(4,128)}, u32[]{:S(2)}) copy-start(s32[4,512]{1,0:T(4,128)} %param.9) | copy-start | bytes 24580
  6.5 57.3 %all-gather.2.cloned.1.call-start = ((), (), s32[]{:S(2)}) async-start(), calls=%async_computation.2 | async-start | bytes 5242880 | tf_op jit(solution)/shard_map/all_gather | solution.py:214
  8.3 1.0 copy-start.5
  73.8 28.3 %copy-start.1 = (bf16[1024,1536]{1,0:T(8,128)(2,1)}, bf16[1024,1536]{1,0:T(8,128)(2,1)S(1)}, u32[]{:S(2)}) copy-start(bf16[1024,1536]{1,0:T(8,128)(2,1)S(1)} %convolution_convert_fusion.k_ref.v_ref.q_ref) | copy-start | bytes 9437188
  82.4 12.8 %copy-start.6 = (s32[1,2048]{1,0:T(1,128)S(1)}, s32[1,2048]{1,0:T(1,128)}, u32[]{:S(2)}) copy-start(s32[1,2048]{1,0:T(1,128)} %param.7) | copy-start | bytes 24580
  82.4 247.6 %all-to-all-start = ((bf16[128,2,128,128]{3,2,1,0:T(8,128)(2,1)}), bf16[128,2,128,128]{3,2,1,0:T(8,128)(2,1)}, u32[]{:S(2)}, u32[]{:S(2)}) async-start(bf16[128,2,128,128]{3,2,1,0:T(8,128)(2,1)} %pack_tiles.1), calls=%async_computation | async-start | bytes 16777216 | tf_op jit(solution)/shard_map/all_to_all | solution.py:226
  93.5 220.9 %all-reduce.2.cloned.1.call-start = ((), (), s32[]{:S(2)}) async-start(), calls=%async_computation.3 | async-start | bytes 524288 | tf_op jit(solution)/shard_map/psum | solution.py:223
  96.3 184.6 %collective-permute-start.1 = (bf16[128,1024]{1,0:T(8,128)(2,1)}, bf16[128,1024]{1,0:T(8,128)(2,1)}, u32[]{:S(2)}, u32[]{:S(2)}) collective-permute-start(bf16[128,1024]{1,0:T(8,128)(2,1)} %get-tuple-element.14), channel_id=1, source_target_pairs={{4,0},{8,4},{12,8},{16,12},{20,16},{24,20},{28,24},{32,28},{36,32}... | collective-permute-start | bytes 786440 | tf_op jit(solution)/shard_map/ppermute | solution.py:221
  98.8 182.2 %collective-permute-start = (bf16[128,1024]{1,0:T(8,128)(2,1)S(1)}, bf16[128,1024]{1,0:T(8,128)(2,1)}, u32[]{:S(2)}, u32[]{:S(2)}) collective-permute-start(bf16[128,1024]{1,0:T(8,128)(2,1)S(1)} %get-tuple-element.15), channel_id=1, source_target_pairs={{0,4},{4,8},{8,12},{12,16},{16,20},{20,24},{24,28},{28,32},{32,36}... | collective-permute-start | bytes 786440 | tf_op jit(solution)/shard_map/ppermute | solution.py:220
  314.4 0.9 copy-start.3
  328.7 1.4 copy-start.2
  358.8 57.8 %all-to-all-start.1 = ((bf16[64,128,128]{2,1,0:T(8,128)(2,1)}), bf16[64,128,128]{2,1,0:T(8,128)(2,1)S(1)}, u32[]{:S(2)}, u32[]{:S(2)}) async-start(bf16[64,128,128]{2,1,0:T(8,128)(2,1)} %rand_attend.1), calls=%async_computation.1 | async-start | bytes 4194304 | tf_op jit(solution)/shard_map/all_to_all | solution.py:231
  416.6 1.3 copy-start.4
Sparse Core Ops, SparseCore 0:
  9.2 54.5 all-gather.1
  103.9 210.3 all-reduce.1

commit v2 on v1

v2 whole, which is shorter than its diff:
```python
import math

import jax
import jax.numpy as jnp
from jax import lax
from jax.experimental import pallas as pl
from jax.experimental.pallas import tpu as pltpu
from jax.sharding import PartitionSpec as P

NEG = -1e30
BF = jnp.bfloat16
F32 = jnp.float32
VMEM_BYTES = 48 << 20


def dot(a, b):
    return jnp.dot(a, b, preferred_element_type=F32)


def dot_t(a, b):
    return lax.dot_general(a, b, (((1,), (1,)), ((), ())), preferred_element_type=F32)


def params():
    return pltpu.CompilerParams(vmem_limit_bytes=VMEM_BYTES)


def pack_tiles(index, pair, slots, rows, blk, wide):
    def kernel(index_ref, pair_ref, out_ref, sems):
        def copy(s):
            tile = index_ref[s]
            row = pl.ds(pl.multiple_of((tile % rows) * blk, blk), blk)
            col = pl.ds(pl.multiple_of((tile // rows) * wide, wide), wide)
            return pltpu.make_async_copy(pair_ref.at[row, col], out_ref.at[s], sems.at[s])

        for s in range(slots):
            copy(s).start()
        for s in range(slots):
            copy(s).wait()

    return pl.pallas_call(
        kernel,
        out_shape=jax.ShapeDtypeStruct((slots, blk, wide), BF),
        grid_spec=pltpu.PrefetchScalarGridSpec(
            num_scalar_prefetch=1,
            grid=(1,),
            in_specs=[pl.BlockSpec(memory_space=pltpu.VMEM)],
            out_specs=pl.BlockSpec(memory_space=pl.ANY),
            scratch_shapes=[pltpu.SemaphoreType.DMA((slots,))],
        ),
        compiler_params=params(),
        name="pack_tiles",
    )(index, pair)


def take_tiles(index, tiles):
    count = index.shape[0]

    def kernel(index_ref, in_ref, out_ref, sems):
        def copy(i):
            return pltpu.make_async_copy(in_ref.at[index_ref[i]], out_ref.at[i], sems.at[i])

        for i in range(count):
            copy(i).start()
        for i in range(count):
            copy(i).wait()

    return pl.pallas_call(
        kernel,
        out_shape=jax.ShapeDtypeStruct((count, *tiles.shape[1:]), tiles.dtype),
        grid_spec=pltpu.PrefetchScalarGridSpec(
            num_scalar_prefetch=1,
            grid=(1,),
            in_specs=[pl.BlockSpec(memory_space=pltpu.VMEM)],
            out_specs=pl.BlockSpec(memory_space=pl.ANY),
            scratch_shapes=[pltpu.SemaphoreType.DMA((count,))],
        ),
        compiler_params=params(),
        name="take_tiles",
    )(index, tiles)


def near_attend(edges, query, around, first, rows, heads, blk, hd, factor):
    def kernel(edge_ref, q_ref, kv_ref, first_ref, acc_ref, stat_ref):
        r = pl.program_id(0)
        window = pl.ds(pl.multiple_of(r * blk, blk), 3 * blk)
        lane = lax.broadcasted_iota(jnp.int32, (blk, 3 * blk), 1)
        low = jnp.where((r == 0) & (edge_ref[0] == 1), blk, 0)
        high = jnp.where((r == rows - 1) & (edge_ref[1] == 1), 2 * blk, 3 * blk)
        usable = (lane >= low) & (lane < high)
        half = lax.broadcasted_iota(jnp.int32, (blk, hd), 1) < hd // 2
        for e in range(heads):
            keys = slice(2 * e * hd, (2 * e + 1) * hd)
            values = slice((2 * e + 1) * hd, (2 * e + 2) * hd)
            q = q_ref[:, e * hd : (e + 1) * hd]
            near = jnp.where(usable, dot_t(q, kv_ref[window, keys]) * factor, NEG)
            glob = dot_t(q, first_ref[:, keys]) * factor
            top = jnp.maximum(
                jnp.max(near, axis=1, keepdims=True), jnp.max(glob, axis=1, keepdims=True)
            )
            near = jnp.exp2(near - top)
            glob = jnp.exp2(glob - top)
            total = jnp.sum(near, axis=1, keepdims=True) + jnp.sum(glob, axis=1, keepdims=True)
            acc_ref[e] = dot(near.astype(BF), kv_ref[window, values]) + dot(
                glob.astype(BF), first_ref[:, values]
            )
            stat_ref[e] = jnp.where(half, top, total)

    out = jax.ShapeDtypeStruct((rows * heads, blk, hd), F32)
    return pl.pallas_call(
        kernel,
        out_shape=(out, out),
        grid_spec=pltpu.PrefetchScalarGridSpec(
            num_scalar_prefetch=1,
            grid=(rows,),
            in_specs=[
                pl.BlockSpec((blk, heads * hd), lambda r, s: (r, 0)),
                pl.BlockSpec(around.shape, lambda r, s: (0, 0)),
                pl.BlockSpec(first.shape, lambda r, s: (0, 0)),
            ],
            out_specs=(
                pl.BlockSpec((heads, blk, hd), lambda r, s: (r, 0, 0)),
                pl.BlockSpec((heads, blk, hd), lambda r, s: (r, 0, 0)),
            ),
        ),
        compiler_params=params(),
        name="near_attend",
    )(edges, query, around, first)


def rand_attend(slot, count, target, query, tiles, acc, stat, rows, heads, blk, hd, rand, peers, factor):
    items = rows * heads
    parts = heads * rand

    def kernel(slot_ref, count_ref, target_ref, q_ref, *refs):
        kv = refs[:parts]
        acc_ref, stat_ref, out_ref, done_ref, sems = refs[parts:]
        r = pl.program_id(0)
        for e in range(heads):
            used = count_ref[r * heads + e]
            q = q_ref[:, e * hd : (e + 1) * hd]
            top0 = stat_ref[e, :, 0:1]
            total0 = stat_ref[e, :, hd // 2 : hd // 2 + 1]
            scores = [
                jnp.where(j < used, dot_t(q, kv[e * rand + j][0, :, :hd]) * factor, NEG)
                for j in range(rand)
            ]
            best = scores[0]
            for s in scores[1:]:
                best = jnp.maximum(best, s)
            top = jnp.maximum(jnp.max(best, axis=1, keepdims=True), top0)
            keep = jnp.exp2(top0 - top)
            summed = acc_ref[e] * keep
            sums = None
            for j in range(rand):
                w = jnp.exp2(scores[j] - top)
                sums = w if sums is None else sums + w
                summed += dot(w.astype(BF), kv[e * rand + j][0, :, hd:])
            total = total0 * keep + jnp.sum(sums, axis=1, keepdims=True)
            i = r * heads + e
            done_ref[i] = (summed / total).astype(BF)
            pltpu.make_async_copy(
                done_ref.at[i], out_ref.at[target_ref[i]], sems.at[i]
            ).start()

        @pl.when(r == rows - 1)
        def _():
            for i in range(items):
                pltpu.make_async_copy(
                    done_ref.at[i], out_ref.at[target_ref[i]], sems.at[i]
                ).wait()

    def tile_spec(n):
        return pl.BlockSpec((1, blk, 2 * hd), lambda r, s, c, t: (s[r * parts + n], 0, 0))

    return pl.pallas_call(
        kernel,
        out_shape=jax.ShapeDtypeStruct((peers, blk, hd), BF),
        grid_spec=pltpu.PrefetchScalarGridSpec(
            num_scalar_prefetch=3,
            grid=(rows,),
            in_specs=[
                pl.BlockSpec((blk, heads * hd), lambda r, s, c, t: (r, 0)),
                *[tile_spec(n) for n in range(parts)],
                pl.BlockSpec((heads, blk, hd), lambda r, s, c, t: (r, 0, 0)),
                pl.BlockSpec((heads, blk, hd), lambda r, s, c, t: (r, 0, 0)),
            ],
            out_specs=pl.BlockSpec(memory_space=pl.ANY),
            scratch_shapes=[pltpu.VMEM((items, blk, hd), BF), pltpu.SemaphoreType.DMA((items,))],
        ),
        compiler_params=params(),
        name="rand_attend",
    )(slot, count, target, query, *[tiles] * parts, acc, stat)


def local(tokens, w_qkv, item_at, rand_cols, rand_used):
    peers = lax.axis_size("seq")
    me = lax.axis_index("seq")
    groups = lax.axis_size("head")
    mine_y = lax.axis_index("head")
    heads, nblocks, rand = rand_cols.shape
    rows = nblocks // peers
    count, depth = tokens.shape
    blk = count // rows
    hd = w_qkv.shape[1] // (3 * heads)
    width = heads * hd
    items = heads * rows
    factor = math.log2(math.e) / math.sqrt(hd)

    first_part = tokens[:blk]
    first_part = lax.psum(jnp.where(me == 0, first_part, jnp.zeros_like(first_part)), "seq")
    first_all = lax.all_gather(first_part, "head", axis=1, tiled=True)

    asked = rand_cols.reshape(heads, peers, rows, rand).transpose(1, 2, 0, 3)
    asked = asked.reshape(peers, items * rand)
    order = jnp.arange(items * rand, dtype=jnp.int32)
    head_of = (order // rand) % heads
    code = order * items + head_of * rows + asked % rows
    mine = asked // rows == me
    low = jnp.min(jnp.where(mine, code, jnp.int32(1 << 30)), axis=1) % items
    high = jnp.max(jnp.where(mine, code, 0), axis=1) % items
    send_tile = jnp.stack([low, high], axis=1).reshape(-1)
    wanted = lax.dynamic_index_in_dim(asked, me, 0, keepdims=False)
    source = wanted // rows
    again = jnp.sum(
        ((source[:, None] == source[None, :]) & (order[None, :] < order[:, None])).astype(jnp.int32),
        axis=1,
    )
    slot = source * 2 + again
    my_used = lax.dynamic_slice_in_dim(rand_used, me * rows, rows, axis=1).T.reshape(-1)
    number = jnp.arange(items, dtype=jnp.int32)
    my_item = (number % heads) * nblocks + me * rows + number // heads
    place = jnp.arange(peers * items, dtype=jnp.int32)
    target = jnp.sum(
        jnp.where(item_at[0][None, :] == my_item[:, None], place[None, :] // items, 0), axis=1
    )
    home = (lax.dynamic_slice_in_dim(item_at[0], me * items, items) % nblocks) // rows
    edges = jnp.stack([me == 0, me == peers - 1]).astype(jnp.int32)

    w_query = w_qkv[:, :width]
    w_pair = w_qkv[:, width:].reshape(-1, 2, heads, hd).transpose(0, 2, 1, 3).reshape(-1, 2 * width)

    def weight(table, shift):
        return lax.dynamic_slice_in_dim(table, (mine_y + shift) % groups * depth, depth, axis=0)

    onward = [(i, (i + 1) % groups) for i in range(groups)]
    backward = [(b, a) for a, b in onward]
    middle = count // 2
    from_low = lax.ppermute(tokens, "head", onward)
    from_high = lax.ppermute(tokens, "head", backward)
    far_top = lax.ppermute(from_low[:middle], "head", onward)
    far_bottom = lax.ppermute(from_high[middle:], "head", backward)

    total = dot(tokens, weight(w_pair, 0))
    total += dot(from_low, weight(w_pair, 3))
    total += dot(from_high, weight(w_pair, 1))
    w_far = weight(w_pair, 2)
    pair = jnp.concatenate(
        [
            (total[:middle] + dot(far_top, w_far)).astype(BF),
            (total[middle:] + dot(far_bottom, w_far)).astype(BF),
        ],
        axis=0,
    )
    sent = pack_tiles(send_tile, pair, 2 * peers, rows, blk, 2 * hd)
    up = [(i, i + 1) for i in range(peers - 1)]
    down = [(b, a) for a, b in up]
    before = lax.ppermute(pair[-blk:], "seq", up)
    after = lax.ppermute(pair[:blk], "seq", down)
    sent, before, after, first_all, far_top, far_bottom = lax.optimization_barrier(
        (sent, before, after, first_all, far_top, far_bottom)
    )
    tiles = lax.all_to_all(sent, "seq", split_axis=0, concat_axis=0, tiled=True)

    around = jnp.concatenate([before, pair, after], axis=0)
    first = dot(first_all, w_pair).astype(BF)
    far = jnp.concatenate([far_top, far_bottom], axis=0)
    query = dot(tokens, weight(w_query, 0)) + dot(from_low, weight(w_query, 3))
    query = query + dot(from_high, weight(w_query, 1)) + dot(far, weight(w_query, 2))
    query = query.astype(BF)
    acc, stat = near_attend(edges, query, around, first, rows, heads, blk, hd, factor)
    done = rand_attend(
        slot, my_used, target, query, tiles, acc, stat, rows, heads, blk, hd, rand, peers, factor
    )
    back = lax.all_to_all(done, "seq", split_axis=0, concat_axis=0, tiled=True)
    return take_tiles(home, back)[None]


def solution(mesh):
    return jax.shard_map(
        local,
        mesh=mesh,
        in_specs=(
            P("seq", "head"),
            P(None, "head"),
            P("head", None),
            P("head", None, None),
            P("head", None),
        ),
        out_specs=P("head", "seq", None, None),
        check_vma=False,
    )
```

time: 461 us -> 488 us (1.059)
  Pallas kernels: 84.5 us -> 39.6 us
  waiting for transfers between devices: 313 us -> 345 us
  local copies, waits for them, and re-layouts: 8.06 us -> 25.3 us
  blocking collectives: 0 us -> 14 us
  starting transfers between devices: 23.2 us -> 30.8 us
    ppermute x1, waiting for transfers between devices: 177 us -> 0.01 us  [local(): after = lax.ppermute(pair[:blk], 'seq', down)]
    all_to_all x1, waiting for transfers between devices: 0.01 us -> 156 us  [local(): tiles = lax.all_to_all(sent, 'seq', split_axis=0, concat_axis=0, tiled=True)]
    psum x1, waiting for transfers between devices: 29.9 us -> 132 us  [local(): lax.psum(jnp.where(me == 0, first_part, jnp.zeros_like(first_part)), 'seq')]
    all_gather x1 -> x0, waiting for transfers between devices: 54.4 us -> none  [local(): lax.all_gather(tokens, 'head', axis=1, tiled=True)]
    pallas_call x1, Pallas kernels: 33.8 us -> 1.77 us  [take_tiles(): pl.pallas_call(kernel, out_shape=jax.ShapeDtypeStruct((count, *tiles.shap...]
    all_gather x0 -> x1, blocking collectives: none -> 14 us  [local(): first_all = lax.all_gather(first_part, 'head', axis=1, tiled=True)]
    pallas_call x1, Pallas kernels: 28.8 us -> 19.5 us  [rand_attend(): pl.pallas_call(kernel, out_shape=jax.ShapeDtypeStruct((peers, blk, hd), B...]
    slice x1 -> x6, local copies, waits for them, and re-layouts: 1.64 us -> 9.15 us  [the longest x1 4.59 us: local(): w_qkv[:, width:].reshape(-1, 2, heads, hd).transpose(0, 2, 1, 3)]
  transfers between devices with their start and end apart: 6 -> 9, of which waited for: 4 -> 4; matrix products, arithmetic and copies ran while one was open for 2% -> 8% of each run, Pallas kernels for 3% -> 4%
where the time goes in v2:
time: 488 us; the launch traced here: 487 us
  waiting for transfers between devices  345 us (71%)
  Pallas kernels  39.6 us (8%)
  starting transfers between devices  30.8 us (6%)
  local copies, waits for them, and re-layouts  25.3 us (5%)
  blocking collectives  14 us (3%)
  between operations  13.8 us (3%)
  matrix products  13 us (3%)
  other arithmetic  5.94 us (1%)
    all_to_all x1, waiting for transfers between devices, local(): tiles = lax.all_to_all(sent, 'seq', split_axis=0, concat_axis=0, tiled=True)  156 us
    psum x1, waiting for transfers between devices, local(): lax.psum(jnp.where(me == 0, first_part, jnp.zeros_like(first_part)), 'seq')  132 us
    all_to_all x1, waiting for transfers between devices, local(): back = lax.all_to_all(done, 'seq', split_axis=0, concat_axis=0, tiled=True)  51.1 us
    pallas_call x1, Pallas kernels, rand_attend(): pl.pallas_call(kernel, out_shape=jax.ShapeDtypeStruct((peers, blk, hd), B...  19.5 us
    all_gather x1, blocking collectives, local(): first_all = lax.all_gather(first_part, 'head', axis=1, tiled=True)  14 us
    pallas_call x1, Pallas kernels, near_attend(): pl.pallas_call(kernel, out_shape=(out, out), grid_spec=pltpu.PrefetchScal...  13.4 us
    dot_general x10, matrix products, dot(): return jnp.dot(a, b, preferred_element_type=F32)  13 us
  transfers between devices with their start and end apart: 9, of which 4 were waited for; matrix products, arithmetic and copies ran while one was open for 8% of the time, Pallas kernels for 4%

profile of v2, /device:TPU:1, one launch (start us, length us, event | category | flops | bytes accessed | tf_op | source)
XLA Modules:
  0.0 487.1 jit_solution(8543746935105962637)
XLA Ops:
  6.5 2.1 collective-permute-start
  8.7 1.4 collective-permute-start.1
  10.1 1.6 slice_select_fusion
  11.7 0.0 all-reduce.2.cloned.1.call-update
  11.8 4.6 slice.28
  16.4 6.5 %copy.37 = bf16[2048,1024]{0,1:T(8,128)(2,1)} copy(bf16[2048,1024]{1,0:T(8,128)(2,1)} %slice.28) | data formatting | bytes 8388608
  22.9 4.7 copy.33
  27.7 0.3 reshape.222
  28.0 0.7 select_reduce_fusion.1
  28.8 0.1 copy.31
  28.9 0.1 reshape.225.index_ref
  29.0 3.0 fusion.10
  32.0 0.0 collective-permute-done
  32.0 0.0 copy-start.6
  32.1 0.8 collective-permute-start.2
  32.9 0.0 collective-permute-done.1
  33.0 2.0 collective-permute-start.3
  35.0 1.3 fusion.8
  36.3 1.3 add_bitcast_fusion
  37.6 6.3 %collective-permute-done.2 = bf16[512,512]{1,0:T(8,128)(2,1)S(1)} collective-permute-done((bf16[512,512]{1,0:T(8,128)(2,1)S(1)}, bf16[512,512]{1,0:T(8,128)(2,1)S(1)}, u32[]{:S(2)}, u32[]{:S(2)}) %collective-permute-start.2) | collective-permute-done | bytes 524320 | tf_op jit(solution)/shard_map/ppermute | solution.py:251
  43.9 0.7 fusion.1
  44.6 0.7 slice.41
  45.4 5.7 %collective-permute-start.5 = (bf16[128,1024]{1,0:T(8,128)(2,1)}, bf16[128,1024]{1,0:T(8,128)(2,1)S(1)}, u32[]{:S(2)}, u32[]{:S(2)}) collective-permute-start(bf16[128,1024]{1,0:T(8,128)(2,1)} %slice.41), channel_id=1, source_target_pairs={{4,0},{8,4},{12,8},{16,12},{20,16},{24,20},{28,24},{32,28},{36,32}... | collective-permute-start | bytes 786440 | tf_op jit(solution)/shard_map/ppermute | solution.py:269
  51.1 0.0 collective-permute-done.3
  51.1 0.8 fusion
  51.9 0.7 slice.40
  52.6 4.3 collective-permute-start.4
  56.9 131.5 %all-reduce.2.cloned.1.call-done = bf16[128,512]{1,0:T(8,128)(2,1)} async-done(((bf16[128,512]{1,0:T(8,128)(2,1)}), bf16[128,512]{1,0:T(8,128)(2,1)}) %all-reduce.2.cloned.1.call-update) | async-done | bytes 131088 | tf_op jit(solution)/shard_map/psum | solution.py:211
  188.5 14.0 %all_gather.3 = bf16[128,2048]{1,0:T(8,128)(2,1)} all-gather(bf16[128,512]{1,0:T(8,128)(2,1)} %all-reduce.2.cloned.1.call-done), channel_id=1, replica_groups=mesh['seq'=64,'head'=4] {'head'}, dimensions={1}, use_global_device_ids=true | all-gather | bytes 655360 | tf_op jit(solution)/shard_map/all_gather | solution.py:212
  202.4 0.2 pad_maximum_fusion.1.pair_ref
  202.6 4.9 %pack_tiles.1 = bf16[128,128,256]{2,1,0:T(8,128)(2,1)} custom-call(s32[128]{0:T(128)S(1)} %reshape.225.index_ref, bf16[1024,1024]{1,0:T(8,128)(2,1)S(1)} %pad_maximum_fusion.1.pair_ref), custom_call_target="tpu_custom_call" | custom-call | tf_op jit(solution)/shard_map/pack_tiles/pallas_call | solution.py:41
  207.5 0.0 collective-permute-done.5
  207.5 8.4 %all-to-all-start = ((bf16[128,128,256]{2,1,0:T(8,128)(2,1)}), bf16[128,128,256]{2,1,0:T(8,128)(2,1)}, u32[]{:S(2)}, u32[]{:S(2)}) async-start(bf16[128,128,256]{2,1,0:T(8,128)(2,1)} %pack_tiles.1), calls=%async_computation | async-start | bytes 16777216 | tf_op jit(solution)/shard_map/all_to_all | solution.py:273
  216.0 0.0 copy-start.15
  216.0 3.0 slice.27
  219.0 1.2 copy.26
  220.3 0.1 fusion.44
  220.3 0.1 copy.27
  220.4 0.1 reshape.224.count_ref
  220.5 0.2 dynamic-slice_reduce_fusion
  220.7 0.1 add_convert_fusion.edge_ref
  220.8 0.2 convert_reduce_fusion
  221.0 0.2 select_reduce_fusion.2.target_ref
  221.2 0.0 copy-start.7
  221.3 2.2 fusion.20
  223.5 0.1 copy-done.7
  223.6 0.7 fusion.18
  224.3 0.3 copy-done.11
  224.6 0.2 copy-done.13
  224.8 0.7 fusion.3
  225.5 0.6 copy-done.4
  226.1 0.3 copy-done.9
  226.4 1.6 convolution_convert_fusion.first_ref
  227.9 2.6 pad_maximum_fusion.kv_ref
  230.6 0.7 fusion.2.q_ref
  231.3 13.4 %near_attend.1 = (f32[32,128,128]{2,1,0:T(8,128)S(1)}, f32[32,128,128]{2,1,0:T(8,128)S(1)}) custom-call(s32[2]{0:T(128)S(1)} %add_convert_fusion.edge_ref, bf16[1024,512]{1,0:T(8,128)(2,1)S(1)} %fusion.2.q_ref, bf16[1280,1024]{1,0:T(8,128)(2,1)} %pad_maximum_fusion.kv_ref, bf16[128,1024]{1,0:T(8,128)(2,1)S(1)} %convolution_convert_fusion.first_ref), custom_call_target="tpu_custom_call" | custom-call | tf_op jit(solution)/shard_map/near_attend/pallas_call | solution.py:110
  244.7 1.3 copy-done.2
  246.0 155.8 %all-to-all-done.refs_0_.refs_1_.refs_2_.refs_3_.refs_4_.refs_5_.refs_6_.refs_7_.refs_8_.refs_9_.refs_10_.refs_11_.refs_12_.refs_13_.refs_14_.refs_15_ = bf16[128,128,256]{2,1,0:T(8,128)(2,1)} async-done(((bf16[128,128,256]{2,1,0:T(8,128)(2,1)}), bf16[128,128,256]{2,1,0:T(8,128)(2,1)}, u32[]{:S(2)}, u32[]{:S(2)}) %all-to-all-start) | async-done | bytes 8388640 | tf_op jit(solution)/shard_map/all_to_all | solution.py:273
  401.7 19.5 %rand_attend.1 = bf16[64,128,128]{2,1,0:T(8,128)(2,1)} custom-call(s32[128]{0:T(128)S(1)} %multiply_add_fusion.1.slot_ref, s32[32]{0:T(128)S(1)} %reshape.224.count_ref, s32[32]{0:T(128)S(1)} %select_reduce_fusion.2.target_ref, bf16[1024,512]{1,0:T(8,128)(2,1)S(1)} %fusion.2.q_ref, ...), custom_call_target="tpu_custom_call" | custom-call | tf_op jit(solution)/shard_map/rand_attend/pallas_call | solution.py:176
  421.3 5.9 %all-to-all-start.1 = ((bf16[64,128,128]{2,1,0:T(8,128)(2,1)}), bf16[64,128,128]{2,1,0:T(8,128)(2,1)S(1)}, u32[]{:S(2)}, u32[]{:S(2)}) async-start(bf16[64,128,128]{2,1,0:T(8,128)(2,1)} %rand_attend.1), calls=%async_computation.1 | async-start | bytes 4194304 | tf_op jit(solution)/shard_map/all_to_all | solution.py:285
  427.2 0.0 copy-start.1
  427.2 0.1 and_select_fusion.5.index_ref
  427.3 51.1 %all-to-all-done.1.in_ref = bf16[64,128,128]{2,1,0:T(8,128)(2,1)S(1)} async-done(((bf16[64,128,128]{2,1,0:T(8,128)(2,1)}), bf16[64,128,128]{2,1,0:T(8,128)(2,1)S(1)}, u32[]{:S(2)}, u32[]{:S(2)}) %all-to-all-start.1) | async-done | bytes 2097184 | tf_op jit(solution)/shard_map/all_to_all | solution.py:285
  478.4 1.8 take_tiles.1
  (33 shorter events, 0.2 us)
Async XLA Ops:
  6.5 213.7 %copy-start = (s32[4,512]{1,0:T(4,128)S(1)}, s32[4,512]{1,0:T(4,128)}, u32[]{:S(2)}) copy-start(s32[4,512]{1,0:T(4,128)} %param.9) | copy-start | bytes 24580
  6.5 181.9 %all-reduce.2.cloned.1.call-start = ((), (), s32[]{:S(2)}) async-start(), calls=%async_computation.2 | async-start | bytes 262144 | tf_op jit(solution)/shard_map/psum | solution.py:211
  6.5 25.5 %collective-permute-start = (bf16[1024,512]{1,0:T(8,128)(2,1)}, bf16[1024,512]{1,0:T(8,128)(2,1)S(1)}, u32[]{:S(2)}, u32[]{:S(2)}) collective-permute-start(bf16[1024,512]{1,0:T(8,128)(2,1)} %param.5), channel_id=1, source_target_pairs={{0,1},{1,2},{2,3},{3,0},{4,5},{5,6},{6,7},{7,4},{8,9},{9,10},{10,1... | collective-permute-start | bytes 3145736 | tf_op jit(solution)/shard_map/ppermute | solution.py:249
  8.7 24.3 %collective-permute-start.1 = (bf16[1024,512]{1,0:T(8,128)(2,1)}, bf16[1024,512]{1,0:T(8,128)(2,1)S(1)}, u32[]{:S(2)}, u32[]{:S(2)}) collective-permute-start(bf16[1024,512]{1,0:T(8,128)(2,1)} %param.5), channel_id=1, source_target_pairs={{1,0},{2,1},{3,2},{0,3},{5,4},{6,5},{7,6},{4,7},{9,8},{10,9},{11,1... | collective-permute-start | bytes 3145736 | tf_op jit(solution)/shard_map/ppermute | solution.py:250
  22.9 4.7 copy-start.14
  28.0 4.1 copy-start.8
  29.0 6.0 %copy-start.3 = (bf16[2048,4,2,128]{0,3,2,1:T(8,128)(2,1)S(1)}, bf16[2048,4,2,128]{0,3,2,1:T(8,128)(2,1)}, u32[]{:S(2)}) copy-start(bf16[2048,4,2,128]{0,3,2,1:T(8,128)(2,1)} %copy.33) | copy-start | bytes 12582916
  32.0 4.2 copy-start.6
  32.1 11.8 %collective-permute-start.2 = (bf16[512,512]{1,0:T(8,128)(2,1)S(1)}, bf16[512,512]{1,0:T(8,128)(2,1)S(1)}, u32[]{:S(2)}, u32[]{:S(2)}) collective-permute-start(bf16[512,512]{1,0:T(8,128)(2,1)S(1)} %slice.37), channel_id=1, source_target_pairs={{0,1},{1,2},{2,3},{3,0},{4,5},{5,6},{6,7},{7,4},{8,9},{9,10},{10,1... | collective-permute-start | bytes 1572872 | tf_op jit(solution)/shard_map/ppermute | solution.py:251
  33.0 18.1 %collective-permute-start.3 = (bf16[512,512]{1,0:T(8,128)(2,1)S(1)}, bf16[512,512]{1,0:T(8,128)(2,1)S(1)}, u32[]{:S(2)}, u32[]{:S(2)}) collective-permute-start(bf16[512,512]{1,0:T(8,128)(2,1)S(1)} %slice.39), channel_id=1, source_target_pairs={{1,0},{2,1},{3,2},{0,3},{5,4},{6,5},{7,6},{4,7},{9,8},{10,9},{11,1... | collective-permute-start | bytes 1572872 | tf_op jit(solution)/shard_map/ppermute | solution.py:252
  43.9 1.5 copy-start.10
  45.4 162.2 %collective-permute-start.5 = (bf16[128,1024]{1,0:T(8,128)(2,1)}, bf16[128,1024]{1,0:T(8,128)(2,1)S(1)}, u32[]{:S(2)}, u32[]{:S(2)}) collective-permute-start(bf16[128,1024]{1,0:T(8,128)(2,1)} %slice.41), channel_id=1, source_target_pairs={{4,0},{8,4},{12,8},{16,12},{20,16},{24,20},{28,24},{32,28},{36,32}... | collective-permute-start | bytes 786440 | tf_op jit(solution)/shard_map/ppermute | solution.py:269
  51.1 1.5 copy-start.12
  52.6 154.9 %collective-permute-start.4 = (bf16[128,1024]{1,0:T(8,128)(2,1)}, bf16[128,1024]{1,0:T(8,128)(2,1)}, u32[]{:S(2)}, u32[]{:S(2)}) collective-permute-start(bf16[128,1024]{1,0:T(8,128)(2,1)} %slice.40), channel_id=1, source_target_pairs={{0,4},{4,8},{8,12},{12,16},{16,20},{20,24},{24,28},{28,32},{32,36}... | collective-permute-start | bytes 786440 | tf_op jit(solution)/shard_map/ppermute | solution.py:268
  207.5 194.2 %all-to-all-start = ((bf16[128,128,256]{2,1,0:T(8,128)(2,1)}), bf16[128,128,256]{2,1,0:T(8,128)(2,1)}, u32[]{:S(2)}, u32[]{:S(2)}) async-start(bf16[128,128,256]{2,1,0:T(8,128)(2,1)} %pack_tiles.1), calls=%async_computation | async-start | bytes 16777216 | tf_op jit(solution)/shard_map/all_to_all | solution.py:273
  216.0 5.0 %copy-start.15 = (s32[1,2048]{1,0:T(1,128)S(1)}, s32[1,2048]{1,0:T(1,128)}, u32[]{:S(2)}) copy-start(s32[1,2048]{1,0:T(1,128)} %param.7) | copy-start | bytes 24580
  221.2 2.2 copy-start.5
  221.2 2.3 copy-start.7
  223.6 1.0 copy-start.11
  223.6 1.2 copy-start.13
  223.6 2.5 copy-start.4
  224.8 1.6 copy-start.9
  244.7 1.3 copy-start.2
  421.3 57.2 %all-to-all-start.1 = ((bf16[64,128,128]{2,1,0:T(8,128)(2,1)}), bf16[64,128,128]{2,1,0:T(8,128)(2,1)S(1)}, u32[]{:S(2)}, u32[]{:S(2)}) async-start(bf16[64,128,128]{2,1,0:T(8,128)(2,1)} %rand_attend.1), calls=%async_computation.1 | async-start | bytes 4194304 | tf_op jit(solution)/shard_map/all_to_all | solution.py:285
  427.2 53.0 %copy-start.1 = (s32[4,512]{1,0:T(4,128)S(1)}, s32[4,512]{1,0:T(4,128)}, u32[]{:S(2)}) copy-start(s32[4,512]{1,0:T(4,128)} %param.9) | copy-start | bytes 24580
Sparse Core Ops, SparseCore 0:
  11.9 176.5 all-reduce.1

commit v3 on v2

--- a/solution.py
+++ b/solution.py
@@ -25,32 +25,55 @@
     return pltpu.CompilerParams(vmem_limit_bytes=VMEM_BYTES)
 
 
-def pack_tiles(index, pair, slots, rows, blk, wide):
-    def kernel(index_ref, pair_ref, out_ref, sems):
+def finish_pack(index, total, far_top, far_bottom, weight, slots, rows, heads, blk, hd):
+    width, wide = heads * hd, 2 * hd
+    half = far_top.shape[0] // blk
+
+    def kernel(index_ref, total_ref, top_ref, bottom_ref, w_ref, out_ref, pair_ref, query_ref, sems):
+        def far(r):
+            ref, at = (top_ref, r) if r < half else (bottom_ref, r - half)
+            return ref[at * blk : (at + 1) * blk]
+
         def copy(s):
             tile = index_ref[s]
             row = pl.ds(pl.multiple_of((tile % rows) * blk, blk), blk)
             col = pl.ds(pl.multiple_of((tile // rows) * wide, wide), wide)
             return pltpu.make_async_copy(pair_ref.at[row, col], out_ref.at[s], sems.at[s])
 
+        for r in range(rows):
+            at = slice(r * blk, (r + 1) * blk)
+            both = (dot(far(r), w_ref[:, width:]) + total_ref[at, width:]).astype(BF)
+            for e in range(heads):
+                for c in range(2):
+                    pair_ref[at, e * wide + c * hd : e * wide + (c + 1) * hd] = both[
+                        :, c * width + e * hd : c * width + (e + 1) * hd
+                    ]
         for s in range(slots):
             copy(s).start()
+        for r in range(rows):
+            at = slice(r * blk, (r + 1) * blk)
+            query_ref[at] = (dot(far(r), w_ref[:, :width]) + total_ref[at, :width]).astype(BF)
         for s in range(slots):
             copy(s).wait()
 
+    vmem = pl.BlockSpec(memory_space=pltpu.VMEM)
     return pl.pallas_call(
         kernel,
-        out_shape=jax.ShapeDtypeStruct((slots, blk, wide), BF),
+        out_shape=(
+            jax.ShapeDtypeStruct((slots, blk, wide), BF),
+            jax.ShapeDtypeStruct((rows * blk, 2 * width), BF),
+            jax.ShapeDtypeStruct((rows * blk, width), BF),
+        ),
         grid_spec=pltpu.PrefetchScalarGridSpec(
             num_scalar_prefetch=1,
             grid=(1,),
-            in_specs=[pl.BlockSpec(memory_space=pltpu.VMEM)],
-            out_specs=pl.BlockSpec(memory_space=pl.ANY),
+            in_specs=[vmem] * 4,
+            out_specs=(pl.BlockSpec(memory_space=pl.ANY), vmem, vmem),
             scratch_shapes=[pltpu.SemaphoreType.DMA((slots,))],
         ),
         compiler_params=params(),
-        name="pack_tiles",
-    )(index, pair)
+        name="finish_pack",
+    )(index, total, far_top, far_bottom, weight)
 
 
 def take_tiles(index, tiles):
@@ -94,7 +117,7 @@
             values = slice((2 * e + 1) * hd, (2 * e + 2) * hd)
             q = q_ref[:, e * hd : (e + 1) * hd]
             near = jnp.where(usable, dot_t(q, kv_ref[window, keys]) * factor, NEG)
-            glob = dot_t(q, first_ref[:, keys]) * factor
+            glob = dot_t(q, first_ref[:, e * hd : (e + 1) * hd]) * factor
             top = jnp.maximum(
                 jnp.max(near, axis=1, keepdims=True), jnp.max(glob, axis=1, keepdims=True)
             )
@@ -102,7 +125,7 @@
             glob = jnp.exp2(glob - top)
             total = jnp.sum(near, axis=1, keepdims=True) + jnp.sum(glob, axis=1, keepdims=True)
             acc_ref[e] = dot(near.astype(BF), kv_ref[window, values]) + dot(
-                glob.astype(BF), first_ref[:, values]
+                glob.astype(BF), first_ref[:, (heads + e) * hd : (heads + e + 1) * hd]
             )
             stat_ref[e] = jnp.where(half, top, total)
 
@@ -130,67 +153,72 @@
 
 def rand_attend(slot, count, target, query, tiles, acc, stat, rows, heads, blk, hd, rand, peers, factor):
     items = rows * heads
-    parts = heads * rand
-
-    def kernel(slot_ref, count_ref, target_ref, q_ref, *refs):
-        kv = refs[:parts]
-        acc_ref, stat_ref, out_ref, done_ref, sems = refs[parts:]
-        r = pl.program_id(0)
-        for e in range(heads):
-            used = count_ref[r * heads + e]
-            q = q_ref[:, e * hd : (e + 1) * hd]
-            top0 = stat_ref[e, :, 0:1]
-            total0 = stat_ref[e, :, hd // 2 : hd // 2 + 1]
+    slots = items * rand
+
+    def kernel(
+        slot_ref, count_ref, target_ref, q_ref, acc_ref, stat_ref, tiles_ref, out_ref,
+        buffer, done, in_sems, out_sems,
+    ):
+        def fetch(n):
+            return pltpu.make_async_copy(tiles_ref.at[slot_ref[n]], buffer.at[n], in_sems.at[n])
+
+        def deliver(i):
+            return pltpu.make_async_copy(done.at[i], out_ref.at[target_ref[i]], out_sems.at[i])
+
+        for n in range(slots):
+            fetch(n).start()
+        lane = lax.broadcasted_iota(jnp.int32, (blk, rand * blk), 1)
+
+        def step(r, carry):
+            first = r * heads
+            for n in range(heads * rand):
+                fetch(first * rand + n).wait()
+            at = pl.ds(pl.multiple_of(r * blk, blk), blk)
+            each = range(heads)
+            tile_ids = [pl.ds((first + e) * rand, rand) for e in each]
+            keys = [buffer[tile_ids[e], :, :hd].reshape(rand * blk, hd) for e in each]
+            scores = [dot_t(q_ref[at, e * hd : (e + 1) * hd], keys[e]) for e in each]
             scores = [
-                jnp.where(j < used, dot_t(q, kv[e * rand + j][0, :, :hd]) * factor, NEG)
-                for j in range(rand)
+                jnp.where(lane < count_ref[first + e] * blk, scores[e] * factor, NEG) for e in each
             ]
-            best = scores[0]
-            for s in scores[1:]:
-                best = jnp.maximum(best, s)
-            top = jnp.maximum(jnp.max(best, axis=1, keepdims=True), top0)
-            keep = jnp.exp2(top0 - top)
-            summed = acc_ref[e] * keep
-            sums = None
-            for j in range(rand):
-                w = jnp.exp2(scores[j] - top)
-                sums = w if sums is None else sums + w
-                summed += dot(w.astype(BF), kv[e * rand + j][0, :, hd:])
-            total = total0 * keep + jnp.sum(sums, axis=1, keepdims=True)
-            i = r * heads + e
-            done_ref[i] = (summed / total).astype(BF)
-            pltpu.make_async_copy(
-                done_ref.at[i], out_ref.at[target_ref[i]], sems.at[i]
-            ).start()
-
-        @pl.when(r == rows - 1)
-        def _():
-            for i in range(items):
-                pltpu.make_async_copy(
-                    done_ref.at[i], out_ref.at[target_ref[i]], sems.at[i]
-                ).wait()
-
-    def tile_spec(n):
-        return pl.BlockSpec((1, blk, 2 * hd), lambda r, s, c, t: (s[r * parts + n], 0, 0))
-
+            top0 = [stat_ref[first + e, :, 0:1] for e in each]
+            total0 = [stat_ref[first + e, :, hd // 2 : hd // 2 + 1] for e in each]
+            top = [jnp.maximum(jnp.max(scores[e], axis=1, keepdims=True), top0[e]) for e in each]
+            keep = [jnp.exp2(top0[e] - top[e]) for e in each]
+            expo = [jnp.exp2(scores[e] - top[e]) for e in each]
+            total = [total0[e] * keep[e] + jnp.sum(expo[e], axis=1, keepdims=True) for e in each]
+            values = [buffer[tile_ids[e], :, hd:].reshape(rand * blk, hd) for e in each]
+            summed = [acc_ref[first + e] * keep[e] + dot(expo[e].astype(BF), values[e]) for e in each]
+            for e in each:
+                done[first + e] = (summed[e] / total[e]).astype(BF)
+            for e in each:
+                deliver(first + e).start()
+            return carry
+
+        lax.fori_loop(0, rows, step, 0)
+        for i in range(items):
+            deliver(i).wait()
+
+    vmem = pl.BlockSpec(memory_space=pltpu.VMEM)
+    anywhere = pl.BlockSpec(memory_space=pl.ANY)
     return pl.pallas_call(
         kernel,
         out_shape=jax.ShapeDtypeStruct((peers, blk, hd), BF),
         grid_spec=pltpu.PrefetchScalarGridSpec(
             num_scalar_prefetch=3,
-            grid=(rows,),
-            in_specs=[
-                pl.BlockSpec((blk, heads * hd), lambda r, s, c, t: (r, 0)),
-                *[tile_spec(n) for n in range(parts)],
-                pl.BlockSpec((heads, blk, hd), lambda r, s, c, t: (r, 0, 0)),
-                pl.BlockSpec((heads, blk, hd), lambda r, s, c, t: (r, 0, 0)),
+            grid=(1,),
+            in_specs=[vmem, vmem, vmem, anywhere],
+            out_specs=anywhere,
+            scratch_shapes=[
+                pltpu.VMEM((slots, blk, 2 * hd), BF),
+                pltpu.VMEM((items, blk, hd), BF),
+                pltpu.SemaphoreType.DMA((slots,)),
+                pltpu.SemaphoreType.DMA((items,)),
             ],
-            out_specs=pl.BlockSpec(memory_space=pl.ANY),
-            scratch_shapes=[pltpu.VMEM((items, blk, hd), BF), pltpu.SemaphoreType.DMA((items,))],
         ),
         compiler_params=params(),
         name="rand_attend",
-    )(slot, count, target, query, *[tiles] * parts, acc, stat)
+    )(slot, count, target, query, acc, stat, tiles)
 
 
 def local(tokens, w_qkv, item_at, rand_cols, rand_used):
@@ -208,8 +236,18 @@
     factor = math.log2(math.e) / math.sqrt(hd)
 
     first_part = tokens[:blk]
-    first_part = lax.psum(jnp.where(me == 0, first_part, jnp.zeros_like(first_part)), "seq")
-    first_all = lax.all_gather(first_part, "head", axis=1, tiled=True)
+    first_part = jnp.where(me == 0, first_part, jnp.zeros_like(first_part))
+    stride = peers
+    while stride > 1:
+        fan = min(4, stride)
+        stride //= fan
+        holders = range(0, peers, stride * fan)
+        got = [
+            lax.ppermute(first_part, "seq", [(h, h + k * stride) for h in holders])
+            for k in range(1, fan)
+        ]
+        for other in got:
+            first_part = first_part + other
 
     asked = rand_cols.reshape(heads, peers, rows, rand).transpose(1, 2, 0, 3)
     asked = asked.reshape(peers, items * rand)
@@ -237,47 +275,38 @@
     home = (lax.dynamic_slice_in_dim(item_at[0], me * items, items) % nblocks) // rows
     edges = jnp.stack([me == 0, me == peers - 1]).astype(jnp.int32)
 
-    w_query = w_qkv[:, :width]
-    w_pair = w_qkv[:, width:].reshape(-1, 2, heads, hd).transpose(0, 2, 1, 3).reshape(-1, 2 * width)
-
-    def weight(table, shift):
-        return lax.dynamic_slice_in_dim(table, (mine_y + shift) % groups * depth, depth, axis=0)
+    def weight(shift):
+        return lax.dynamic_slice_in_dim(w_qkv, (mine_y + shift) % groups * depth, depth, axis=0)
 
     onward = [(i, (i + 1) % groups) for i in range(groups)]
     backward = [(b, a) for a, b in onward]
+    across = [(i, (i + 2) % groups) for i in range(groups)]
     middle = count // 2
     from_low = lax.ppermute(tokens, "head", onward)
     from_high = lax.ppermute(tokens, "head", backward)
     far_top = lax.ppermute(from_low[:middle], "head", onward)
     far_bottom = lax.ppermute(from_high[middle:], "head", backward)
-
-    total = dot(tokens, weight(w_pair, 0))
-    total += dot(from_low, weight(w_pair, 3))
-    total += dot(from_high, weight(w_pair, 1))
-    w_far = weight(w_pair, 2)
-    pair = jnp.concatenate(
-        [
-            (total[:middle] + dot(far_top, w_far)).astype(BF),
-            (total[middle:] + dot(far_bottom, w_far)).astype(BF),
-        ],
-        axis=0,
-    )
-    sent = pack_tiles(send_tile, pair, 2 * peers, rows, blk, 2 * hd)
+    first_low = lax.ppermute(first_part, "head", onward)
+    first_high = lax.ppermute(first_part, "head", backward)
+    first_far = lax.ppermute(first_part, "head", across)
+
+    total = dot(tokens, weight(0)) + dot(from_low, weight(3)) + dot(from_high, weight(1))
+    sent, pair, query = finish_pack(
+        send_tile, total, far_top, far_bottom, weight(2), 2 * peers, rows, heads, blk, hd
+    )
     up = [(i, i + 1) for i in range(peers - 1)]
     down = [(b, a) for a, b in up]
     before = lax.ppermute(pair[-blk:], "seq", up)
     after = lax.ppermute(pair[:blk], "seq", down)
-    sent, before, after, first_all, far_top, far_bottom = lax.optimization_barrier(
-        (sent, before, after, first_all, far_top, far_bottom)
+    sent, before, after, first_low, first_high, first_far = lax.optimization_barrier(
+        (sent, before, after, first_low, first_high, first_far)
     )
     tiles = lax.all_to_all(sent, "seq", split_axis=0, concat_axis=0, tiled=True)
 
     around = jnp.concatenate([before, pair, after], axis=0)
-    first = dot(first_all, w_pair).astype(BF)
-    far = jnp.concatenate([far_top, far_bottom], axis=0)
-    query = dot(tokens, weight(w_query, 0)) + dot(from_low, weight(w_query, 3))
-    query = query + dot(from_high, weight(w_query, 1)) + dot(far, weight(w_query, 2))
-    query = query.astype(BF)
+    first = dot(first_part, weight(0)[:, width:]) + dot(first_low, weight(3)[:, width:])
+    first += dot(first_high, weight(1)[:, width:]) + dot(first_far, weight(2)[:, width:])
+    first = first.astype(BF)
     acc, stat = near_attend(edges, query, around, first, rows, heads, blk, hd, factor)
     done = rand_attend(
         slot, my_used, target, query, tiles, acc, stat, rows, heads, blk, hd, rand, peers, factor

time: 488 us -> 353 us (0.72)
  waiting for transfers between devices: 345 us -> 217 us
  starting transfers between devices: 30.8 us -> 48.4 us
  local copies, waits for them, and re-layouts: 25.3 us -> 11.3 us
  blocking collectives: 14 us -> 0 us
  between operations: 13.8 us -> 0.55 us
  matrix products: 13 us -> 21.9 us
    psum x1 -> x0, waiting for transfers between devices: 132 us -> none  [local(): lax.psum(jnp.where(me == 0, first_part, jnp.zeros_like(first_part)), 'seq')]
    all_gather x1 -> x0, blocking collectives: 14 us -> none  [local(): first_all = lax.all_gather(first_part, 'head', axis=1, tiled=True)]
    ppermute x0 -> x12, starting transfers between devices: none -> 10.3 us  [the longest x9 8.05 us: local(): lax.ppermute(first_part, 'seq', [(h, h + k * stride) for h in holders])]
    dot_general x10 -> x7, matrix products: 13 us -> 21.9 us  [dot(): return jnp.dot(a, b, preferred_element_type=F32)]
    slice x3 -> x0, local copies, waits for them, and re-layouts: 8.37 us -> none  [the longest x1 4.59 us: local(): w_qkv[:, width:].reshape(-1, 2, heads, hd).transpose(0, 2, 1, 3)]
    ppermute x1, starting transfers between devices: 5.74 us -> 14 us  [local(): after = lax.ppermute(pair[:blk], 'seq', down)]
    ppermute x0 -> x12, waiting for transfers between devices: none -> 6.76 us  [the longest x1 3.4 us: local(): first_far = lax.ppermute(first_part, 'head', across)]
    ppermute x1, waiting for transfers between devices: 6.28 us -> 0.01 us  [local(): far_top = lax.ppermute(from_low[:middle], 'head', onward)]
  transfers between devices with their start and end apart: 9 -> 20, of which waited for: 4 -> 5; matrix products, arithmetic and copies ran while one was open for 8% -> 10% of each run, Pallas kernels for 4% -> 6%
where the time goes in v3:
time: 353 us; the launch traced here: 352 us
  waiting for transfers between devices  217 us (61%)
  starting transfers between devices  48.4 us (14%)
  Pallas kernels  43.4 us (12%)
  matrix products  21.9 us (6%)
  local copies, waits for them, and re-layouts  11.3 us (3%)
  other arithmetic  9.15 us (3%)
    all_to_all x1, waiting for transfers between devices, local(): tiles = lax.all_to_all(sent, 'seq', split_axis=0, concat_axis=0, tiled=True)  159 us
    all_to_all x1, waiting for transfers between devices, local(): back = lax.all_to_all(done, 'seq', split_axis=0, concat_axis=0, tiled=True)  51.2 us
    dot_general x7, matrix products, dot(): return jnp.dot(a, b, preferred_element_type=F32)  21.9 us
    pallas_call x1, Pallas kernels, rand_attend(): pl.pallas_call(kernel, out_shape=jax.ShapeDtypeStruct((peers, blk, hd), B...  18.9 us
    ppermute x1, starting transfers between devices, local(): after = lax.ppermute(pair[:blk], 'seq', down)  14 us
    pallas_call x1, Pallas kernels, near_attend(): pl.pallas_call(kernel, out_shape=(out, out), grid_spec=pltpu.PrefetchScal...  13.4 us
    all_to_all x1, starting transfers between devices, local(): tiles = lax.all_to_all(sent, 'seq', split_axis=0, concat_axis=0, tiled=True)  9.94 us
    pallas_call x1, Pallas kernels, finish_pack(): pl.pallas_call(kernel, out_shape=(jax.ShapeDtypeStruct((slots, blk, wide)...  9.36 us
  transfers between devices with their start and end apart: 20, of which 5 were waited for; matrix products, arithmetic and copies ran while one was open for 10% of the time, Pallas kernels for 6%

profile of v3, /device:TPU:1, one launch (start us, length us, event | category | flops | bytes accessed | tf_op | source)
XLA Modules:
  0.0 351.7 jit_solution(17189344256456673296)
XLA Ops:
  0.0 0.9 slice_select_fusion
  0.9 0.7 collective-permute-start.7
  1.6 0.7 collective-permute-start.8
  2.3 1.3 collective-permute-start.6
  3.6 2.1 collective-permute-start
  5.7 1.4 collective-permute-start.1
  7.2 1.5 constant_dynamic-slice_fusion.w_ref
  8.7 6.2 %fusion.3 = f32[1536,1024]{0,1:T(8,128)} fusion(bf16[1024,512]{1,0:T(8,128)(2,1)} %param.5, bf16[2048,1536]{1,0:T(8,128)(2,1)} %param.6, s32[]{:T(128)S(6)} %select_n.199), kind=kOutput, calls=%fused_computation.5 | convolution fusion | flops 1610612736 | bytes 8912900 | tf_op jit(solution)/shard_map/dot_general | solution.py:17
  14.9 1.1 reshape.216
  16.0 0.7 select_reduce_fusion.1
  16.7 0.0 collective-permute-done.7
  16.7 0.0 collective-permute-done.8
  16.7 1.0 add_add_fusion.2
  17.7 0.7 collective-permute-start.11
  18.4 0.7 collective-permute-start.10
  19.1 1.3 collective-permute-start.9
  20.4 0.5 and_select_fusion
  20.9 0.7 pad_add_fusion
  21.6 0.7 copy.26
  22.3 0.9 reshape.219.index_ref
  23.2 0.0 collective-permute-done.11
  23.2 1.1 add_add_fusion.1
  24.3 0.8 collective-permute-start.14
  25.1 0.7 collective-permute-start.13
  25.8 1.3 collective-permute-start.12
  27.1 1.1 slice.36
  28.2 0.1 collective-permute-start.2
  28.4 2.7 collective-permute-start.3
  31.1 3.5 fusion.1
  34.6 6.1 %add_bitcast_fusion.total_ref = f32[1024,1536]{1,0:T(8,128)} fusion(f32[1536,1024]{0,1:T(8,128)S(1)} %bitcast.36, f32[1536,1024]{0,1:T(8,128)S(1)} %fusion.1, bf16[1024,512]{1,0:T(8,128)(2,1)S(1)} %collective-permute-done.1, bf16[2048,1536]{1,0:T(8,128)(2,1)} %param.6, s32[]{:T(128)S(6)} %select_n.203), kind=kOutput, calls=%fused_computation | convolution fusion | flops 1613758464 | bytes 21495812 | tf_op jit(solution)/shard_map/dot_general | solution.py:17
  40.7 9.4 %finish_pack.1 = (bf16[128,128,256]{2,1,0:T(8,128)(2,1)}, bf16[1024,1024]{1,0:T(8,128)(2,1)S(1)}, bf16[1024,512]{1,0:T(8,128)(2,1)S(1)}) custom-call(s32[128]{0:T(128)S(1)} %reshape.219.index_ref, f32[1024,1536]{1,0:T(8,128)} %add_bitcast_fusion.total_ref, bf16[512,512]{1,0:T(8,128)(2,1)S(1)} %collective-permute-done.2.top_ref, ...), custom_call_target="tpu_custom_call" | custom-call | tf_op jit(solution)/shard_map/finish_pack/pallas_call | solution.py:60
  50.1 1.3 copy-done.1
  51.5 14.0 %collective-permute-start.5 = (bf16[128,1024]{1,0:T(8,128)(2,1)S(1)}, bf16[128,1024]{1,0:T(8,128)(2,1)S(1)}, u32[]{:S(2)}, u32[]{:S(2)}) collective-permute-start(bf16[128,1024]{1,0:T(8,128)(2,1)S(1)} %get-tuple-element.31), channel_id=1, source_target_pairs={{4,0},{8,4},{12,8},{16,12},{20,16},{24,20},{28,24},{32,28},{36,32}... | collective-permute-start | bytes 786440 | tf_op jit(solution)/shard_map/ppermute | solution.py:300
  65.4 1.9 collective-permute-start.4
  67.4 0.8 collective-permute-start.17
  68.2 0.9 collective-permute-start.16
  69.1 0.6 collective-permute-start.15
  69.7 3.4 collective-permute-done.17
  73.1 0.8 collective-permute-done.16
  73.9 2.5 collective-permute-done.15
  76.4 9.9 %all-to-all-start = ((bf16[128,128,256]{2,1,0:T(8,128)(2,1)}), bf16[128,128,256]{2,1,0:T(8,128)(2,1)}, u32[]{:S(2)}, u32[]{:S(2)}) async-start(bf16[128,128,256]{2,1,0:T(8,128)(2,1)} %get-tuple-element.26), calls=%async_computation | async-start | bytes 16777216 | tf_op jit(solution)/shard_map/all_to_all | solution.py:304
  86.4 0.1 dynamic-slice_bitcast_fusion
  86.5 0.1 copy.25
  86.5 0.1 reshape.218.count_ref
  86.6 0.2 copy.24
  86.8 0.2 dynamic-slice_reduce_fusion
  87.0 0.1 add_convert_fusion.edge_ref
  87.1 0.2 convert_reduce_fusion
  87.3 0.2 select_reduce_fusion.2.target_ref
  87.5 1.5 fusion.10
  89.1 1.5 fusion.7
  90.6 1.5 convolution_add_fusion
  92.2 1.5 fusion.6.first_ref
  93.7 3.4 pad_maximum_fusion.kv_ref
  97.1 13.4 %near_attend.1 = (f32[32,128,128]{2,1,0:T(8,128)S(1)}, f32[32,128,128]{2,1,0:T(8,128)S(1)}) custom-call(s32[2]{0:T(128)S(1)} %add_convert_fusion.edge_ref, bf16[1024,512]{1,0:T(8,128)(2,1)S(1)} %get-tuple-element.16.q_ref, bf16[1280,1024]{1,0:T(8,128)(2,1)} %pad_maximum_fusion.kv_ref, bf16[128,1024]{1,0:T(8,128)(2,1)S(1)} %fusion.6.first_ref), custom_call_target="tpu_custom_call" | custom-call | tf_op jit(solution)/shard_map/near_attend/pallas_call | solution.py:133
  110.5 1.3 copy-done.2
  111.8 1.3 copy-done.4
  113.1 159.0 %all-to-all-done.tiles_ref = bf16[128,128,256]{2,1,0:T(8,128)(2,1)} async-done(((bf16[128,128,256]{2,1,0:T(8,128)(2,1)}), bf16[128,128,256]{2,1,0:T(8,128)(2,1)}, u32[]{:S(2)}, u32[]{:S(2)}) %all-to-all-start) | async-done | bytes 8388640 | tf_op jit(solution)/shard_map/all_to_all | solution.py:304
  272.1 1.6 copy-done.3
  273.7 18.9 %rand_attend.1 = bf16[64,128,128]{2,1,0:T(8,128)(2,1)} custom-call(s32[128]{0:T(128)S(1)} %multiply_add_fusion.1.slot_ref, s32[32]{0:T(128)S(1)} %reshape.218.count_ref, s32[32]{0:T(128)S(1)} %select_reduce_fusion.2.target_ref, bf16[1024,512]{1,0:T(8,128)(2,1)S(1)} %get-tuple-element.16.q_ref, f32[32,128,128]{2,1,0:T(8,128)S(1)} %copy-done.3, ...), custom_call_target="tpu_custom_call" | custom-call | tf_op jit(solution)/shard_map/rand_attend/pallas_call | solution.py:204
  292.6 5.9 %all-to-all-start.1 = ((bf16[64,128,128]{2,1,0:T(8,128)(2,1)}), bf16[64,128,128]{2,1,0:T(8,128)(2,1)S(1)}, u32[]{:S(2)}, u32[]{:S(2)}) async-start(bf16[64,128,128]{2,1,0:T(8,128)(2,1)} %rand_attend.1), calls=%async_computation.1 | async-start | bytes 4194304 | tf_op jit(solution)/shard_map/all_to_all | solution.py:314
  298.6 0.1 and_select_fusion.5.index_ref
  298.6 51.2 %all-to-all-done.1.in_ref = bf16[64,128,128]{2,1,0:T(8,128)(2,1)S(1)} async-done(((bf16[64,128,128]{2,1,0:T(8,128)(2,1)}), bf16[64,128,128]{2,1,0:T(8,128)(2,1)S(1)}, u32[]{:S(2)}, u32[]{:S(2)}) %all-to-all-start.1) | async-done | bytes 2097184 | tf_op jit(solution)/shard_map/all_to_all | solution.py:314
  349.8 1.8 take_tiles.1
  (33 shorter events, 0.2 us)
Async XLA Ops:
  0.0 86.4 %copy-start = (s32[4,512]{1,0:T(4,128)S(1)}, s32[4,512]{1,0:T(4,128)}, u32[]{:S(2)}) copy-start(s32[4,512]{1,0:T(4,128)} %param.9) | copy-start | bytes 24580
  0.9 15.8 %collective-permute-start.7 = (bf16[128,512]{1,0:T(8,128)(2,1)S(1)}, bf16[128,512]{1,0:T(8,128)(2,1)S(1)}, u32[]{:S(2)}, u32[]{:S(2)}) collective-permute-start(bf16[128,512]{1,0:T(8,128)(2,1)S(1)} %slice_select_fusion), channel_id=1, source_target_pairs={{0,128},{1,129},{2,130},{3,131}} | collective-permute-start | bytes 393224 | tf_op jit(solution)/shard_map/ppermute | solution.py:246
  1.6 15.1 %collective-permute-start.8 = (bf16[128,512]{1,0:T(8,128)(2,1)S(1)}, bf16[128,512]{1,0:T(8,128)(2,1)S(1)}, u32[]{:S(2)}, u32[]{:S(2)}) collective-permute-start(bf16[128,512]{1,0:T(8,128)(2,1)S(1)} %slice_select_fusion), channel_id=1, source_target_pairs={{0,192},{1,193},{2,194},{3,195}} | collective-permute-start | bytes 393224 | tf_op jit(solution)/shard_map/ppermute | solution.py:246
  2.3 14.4 %collective-permute-start.6 = (bf16[128,512]{1,0:T(8,128)(2,1)S(1)}, bf16[128,512]{1,0:T(8,128)(2,1)}, u32[]{:S(2)}, u32[]{:S(2)}) collective-permute-start(bf16[128,512]{1,0:T(8,128)(2,1)S(1)} %slice_select_fusion), channel_id=1, source_target_pairs={{0,64},{1,65},{2,66},{3,67}} | collective-permute-start | bytes 393224 | tf_op jit(solution)/shard_map/ppermute | solution.py:246
  3.6 23.5 %collective-permute-start = (bf16[1024,512]{1,0:T(8,128)(2,1)}, bf16[1024,512]{1,0:T(8,128)(2,1)}, u32[]{:S(2)}, u32[]{:S(2)}) collective-permute-start(bf16[1024,512]{1,0:T(8,128)(2,1)} %param.5), channel_id=1, source_target_pairs={{0,1},{1,2},{2,3},{3,0},{4,5},{5,6},{6,7},{7,4},{8,9},{9,10},{10,1... | collective-permute-start | bytes 3145736 | tf_op jit(solution)/shard_map/ppermute | solution.py:285
  5.7 22.6 %collective-permute-start.1 = (bf16[1024,512]{1,0:T(8,128)(2,1)}, bf16[1024,512]{1,0:T(8,128)(2,1)S(1)}, u32[]{:S(2)}, u32[]{:S(2)}) collective-permute-start(bf16[1024,512]{1,0:T(8,128)(2,1)} %param.5), channel_id=1, source_target_pairs={{1,0},{2,1},{3,2},{0,3},{5,4},{6,5},{7,6},{4,7},{9,8},{10,9},{11,1... | collective-permute-start | bytes 3145736 | tf_op jit(solution)/shard_map/ppermute | solution.py:286
  17.7 5.5 %collective-permute-start.11 = (bf16[128,512]{1,0:T(8,128)(2,1)S(1)}, bf16[128,512]{1,0:T(8,128)(2,1)S(1)}, u32[]{:S(2)}, u32[]{:S(2)}) collective-permute-start(bf16[128,512]{1,0:T(8,128)(2,1)S(1)} %add_add_fusion.2), channel_id=1, source_target_pairs={{0,48},{64,112},{128,176},{192,240},{1,49},{65,113},{129,177},{193... | collective-permute-start | bytes 393224 | tf_op jit(solution)/shard_map/ppermute | solution.py:246
  18.4 4.8 %collective-permute-start.10 = (bf16[128,512]{1,0:T(8,128)(2,1)S(1)}, bf16[128,512]{1,0:T(8,128)(2,1)S(1)}, u32[]{:S(2)}, u32[]{:S(2)}) collective-permute-start(bf16[128,512]{1,0:T(8,128)(2,1)S(1)} %add_add_fusion.2), channel_id=1, source_target_pairs={{0,32},{64,96},{128,160},{192,224},{1,33},{65,97},{129,161},{193,2... | collective-permute-start | bytes 393224 | tf_op jit(solution)/shard_map/ppermute | solution.py:246
  19.1 4.1 %collective-permute-start.9 = (bf16[128,512]{1,0:T(8,128)(2,1)S(1)}, bf16[128,512]{1,0:T(8,128)(2,1)}, u32[]{:S(2)}, u32[]{:S(2)}) collective-permute-start(bf16[128,512]{1,0:T(8,128)(2,1)S(1)} %add_add_fusion.2), channel_id=1, source_target_pairs={{0,16},{64,80},{128,144},{192,208},{1,17},{65,81},{129,145},{193,2... | collective-permute-start | bytes 393224 | tf_op jit(solution)/shard_map/ppermute | solution.py:246
  23.2 11.4 %slice-start = ((s8[6291456]{0:T(1024)(128)(4,1)}), s8[4194304]{0:T(1024)(128)(4,1)S(1)}, s32[]{:S(2)}) async-start(s8[6291456]{0:T(1024)(128)(4,1)} %bitcast.35), calls=%async_computation.2 | async-start | bytes 8388608
  24.3 43.0 %collective-permute-start.14 = (bf16[128,512]{1,0:T(8,128)(2,1)S(1)}, bf16[128,512]{1,0:T(8,128)(2,1)S(1)}, u32[]{:S(2)}, u32[]{:S(2)}) collective-permute-start(bf16[128,512]{1,0:T(8,128)(2,1)S(1)} %add_add_fusion.1), channel_id=1, source_target_pairs={{0,12},{16,28},{32,44},{48,60},{64,76},{80,92},{96,108},{112,124},... | collective-permute-start | bytes 393224 | tf_op jit(solution)/shard_map/ppermute | solution.py:246
  25.1 42.2 %collective-permute-start.13 = (bf16[128,512]{1,0:T(8,128)(2,1)S(1)}, bf16[128,512]{1,0:T(8,128)(2,1)S(1)}, u32[]{:S(2)}, u32[]{:S(2)}) collective-permute-start(bf16[128,512]{1,0:T(8,128)(2,1)S(1)} %add_add_fusion.1), channel_id=1, source_target_pairs={{0,8},{16,24},{32,40},{48,56},{64,72},{80,88},{96,104},{112,120},{... | collective-permute-start | bytes 393224 | tf_op jit(solution)/shard_map/ppermute | solution.py:246
  25.8 41.6 %collective-permute-start.12 = (bf16[128,512]{1,0:T(8,128)(2,1)S(1)}, bf16[128,512]{1,0:T(8,128)(2,1)S(1)}, u32[]{:S(2)}, u32[]{:S(2)}) collective-permute-start(bf16[128,512]{1,0:T(8,128)(2,1)S(1)} %add_add_fusion.1), channel_id=1, source_target_pairs={{0,4},{16,20},{32,36},{48,52},{64,68},{80,84},{96,100},{112,116},{... | collective-permute-start | bytes 393224 | tf_op jit(solution)/shard_map/ppermute | solution.py:246
  28.2 12.5 %collective-permute-start.2 = (bf16[512,512]{1,0:T(8,128)(2,1)S(1)}, bf16[512,512]{1,0:T(8,128)(2,1)S(1)}, u32[]{:S(2)}, u32[]{:S(2)}) collective-permute-start(bf16[512,512]{1,0:T(8,128)(2,1)S(1)} %slice.36), channel_id=1, source_target_pairs={{0,1},{1,2},{2,3},{3,0},{4,5},{5,6},{6,7},{7,4},{8,9},{9,10},{10,1... | collective-permute-start | bytes 1572872 | tf_op jit(solution)/shard_map/ppermute | solution.py:287
  28.4 6.3 %slice-start.1 = ((s8[6291456]{0:T(1024)(128)(4,1)}), s8[2097152]{0:T(1024)(128)(4,1)S(1)}, s32[]{:S(2)}) async-start(s8[6291456]{0:T(1024)(128)(4,1)} %bitcast.35), calls=%async_computation.3 | async-start | bytes 4194304
  28.4 12.4 %collective-permute-start.3 = (bf16[512,512]{1,0:T(8,128)(2,1)S(1)}, bf16[512,512]{1,0:T(8,128)(2,1)S(1)}, u32[]{:S(2)}, u32[]{:S(2)}) collective-permute-start(bf16[512,512]{1,0:T(8,128)(2,1)S(1)} %slice.37), channel_id=1, source_target_pairs={{1,0},{2,1},{3,2},{0,3},{5,4},{6,5},{7,6},{4,7},{9,8},{10,9},{11,1... | collective-permute-start | bytes 1572872 | tf_op jit(solution)/shard_map/ppermute | solution.py:288
  50.1 1.3 copy-start.1
  51.5 24.9 %collective-permute-start.5 = (bf16[128,1024]{1,0:T(8,128)(2,1)S(1)}, bf16[128,1024]{1,0:T(8,128)(2,1)S(1)}, u32[]{:S(2)}, u32[]{:S(2)}) collective-permute-start(bf16[128,1024]{1,0:T(8,128)(2,1)S(1)} %get-tuple-element.31), channel_id=1, source_target_pairs={{4,0},{8,4},{12,8},{16,12},{20,16},{24,20},{28,24},{32,28},{36,32}... | collective-permute-start | bytes 786440 | tf_op jit(solution)/shard_map/ppermute | solution.py:300
  65.4 11.0 %collective-permute-start.4 = (bf16[128,1024]{1,0:T(8,128)(2,1)S(1)}, bf16[128,1024]{1,0:T(8,128)(2,1)}, u32[]{:S(2)}, u32[]{:S(2)}) collective-permute-start(bf16[128,1024]{1,0:T(8,128)(2,1)S(1)} %get-tuple-element.32), channel_id=1, source_target_pairs={{0,4},{4,8},{8,12},{12,16},{16,20},{20,24},{24,28},{28,32},{32,36}... | collective-permute-start | bytes 786440 | tf_op jit(solution)/shard_map/ppermute | solution.py:299
  67.4 5.6 %collective-permute-start.17 = (bf16[128,512]{1,0:T(8,128)(2,1)S(1)}, bf16[128,512]{1,0:T(8,128)(2,1)S(1)}, u32[]{:S(2)}, u32[]{:S(2)}) collective-permute-start(bf16[128,512]{1,0:T(8,128)(2,1)S(1)} %add_add_fusion), channel_id=1, source_target_pairs={{0,2},{1,3},{2,0},{3,1},{4,6},{5,7},{6,4},{7,5},{8,10},{9,11},{10,... | collective-permute-start | bytes 393224 | tf_op jit(solution)/shard_map/ppermute | solution.py:291
  68.2 5.7 %collective-permute-start.16 = (bf16[128,512]{1,0:T(8,128)(2,1)S(1)}, bf16[128,512]{1,0:T(8,128)(2,1)S(1)}, u32[]{:S(2)}, u32[]{:S(2)}) collective-permute-start(bf16[128,512]{1,0:T(8,128)(2,1)S(1)} %add_add_fusion), channel_id=1, source_target_pairs={{1,0},{2,1},{3,2},{0,3},{5,4},{6,5},{7,6},{4,7},{9,8},{10,9},{11,1... | collective-permute-start | bytes 393224 | tf_op jit(solution)/shard_map/ppermute | solution.py:290
  69.1 7.3 %collective-permute-start.15 = (bf16[128,512]{1,0:T(8,128)(2,1)S(1)}, bf16[128,512]{1,0:T(8,128)(2,1)S(1)}, u32[]{:S(2)}, u32[]{:S(2)}) collective-permute-start(bf16[128,512]{1,0:T(8,128)(2,1)S(1)} %add_add_fusion), channel_id=1, source_target_pairs={{0,1},{1,2},{2,3},{3,0},{4,5},{5,6},{6,7},{7,4},{8,9},{9,10},{10,1... | collective-permute-start | bytes 393224 | tf_op jit(solution)/shard_map/ppermute | solution.py:289
  76.4 10.9 %copy-start.5 = (s32[1,2048]{1,0:T(1,128)S(1)}, s32[1,2048]{1,0:T(1,128)}, u32[]{:S(2)}) copy-start(s32[1,2048]{1,0:T(1,128)} %param.7) | copy-start | bytes 24580
  76.4 195.7 %all-to-all-start = ((bf16[128,128,256]{2,1,0:T(8,128)(2,1)}), bf16[128,128,256]{2,1,0:T(8,128)(2,1)}, u32[]{:S(2)}, u32[]{:S(2)}) async-start(bf16[128,128,256]{2,1,0:T(8,128)(2,1)} %get-tuple-element.26), calls=%async_computation | async-start | bytes 16777216 | tf_op jit(solution)/shard_map/all_to_all | solution.py:304
  110.5 1.3 copy-start.2
  111.8 1.3 copy-start.4
  272.1 1.6 copy-start.3
  292.6 57.2 %all-to-all-start.1 = ((bf16[64,128,128]{2,1,0:T(8,128)(2,1)}), bf16[64,128,128]{2,1,0:T(8,128)(2,1)S(1)}, u32[]{:S(2)}, u32[]{:S(2)}) async-start(bf16[64,128,128]{2,1,0:T(8,128)(2,1)} %rand_attend.1), calls=%async_computation.1 | async-start | bytes 4194304 | tf_op jit(solution)/shard_map/all_to_all | solution.py:314

commit v4 on v3

v4 whole, which is shorter than its diff:
```python
import math

import jax
import jax.numpy as jnp
from jax import lax
from jax.experimental import pallas as pl
from jax.experimental.pallas import tpu as pltpu
from jax.sharding import PartitionSpec as P

NEG = -1e30
BF = jnp.bfloat16
F32 = jnp.float32
VMEM_BYTES = 48 << 20


def dot(a, b):
    return jnp.dot(a, b, preferred_element_type=F32)


def dot_t(a, b):
    return lax.dot_general(a, b, (((1,), (1,)), ((), ())), preferred_element_type=F32)


def params():
    return pltpu.CompilerParams(vmem_limit_bytes=VMEM_BYTES)


def pack_tiles(index, pair, slots, rows, heads, blk, hd):
    width = heads * hd

    def kernel(index_ref, pair_ref, out_ref, tiles, sems):
        def copy(s):
            return pltpu.make_async_copy(tiles.at[index_ref[s]], out_ref.at[s], sems.at[s])

        for e in range(heads):
            for r in range(rows):
                at = slice(r * blk, (r + 1) * blk)
                tiles[e * rows + r, :, :hd] = pair_ref[at, e * hd : (e + 1) * hd]
                tiles[e * rows + r, :, hd:] = pair_ref[at, width + e * hd : width + (e + 1) * hd].T
        for s in range(slots):
            copy(s).start()
        for s in range(slots):
            copy(s).wait()

    return pl.pallas_call(
        kernel,
        out_shape=jax.ShapeDtypeStruct((slots, blk, 2 * hd), BF),
        grid_spec=pltpu.PrefetchScalarGridSpec(
            num_scalar_prefetch=1,
            grid=(1,),
            in_specs=[pl.BlockSpec(memory_space=pltpu.VMEM)],
            out_specs=pl.BlockSpec(memory_space=pl.ANY),
            scratch_shapes=[
                pltpu.VMEM((rows * heads, blk, 2 * hd), BF),
                pltpu.SemaphoreType.DMA((slots,)),
            ],
        ),
        compiler_params=params(),
        name="pack_tiles",
    )(index, pair)


def take_tiles(index, tiles):
    count = index.shape[0]

    def kernel(index_ref, in_ref, out_ref, sems):
        def copy(i):
            return pltpu.make_async_copy(in_ref.at[index_ref[i]], out_ref.at[i], sems.at[i])

        for i in range(count):
            copy(i).start()
        for i in range(count):
            copy(i).wait()

    return pl.pallas_call(
        kernel,
        out_shape=jax.ShapeDtypeStruct((count, *tiles.shape[1:]), tiles.dtype),
        grid_spec=pltpu.PrefetchScalarGridSpec(
            num_scalar_prefetch=1,
            grid=(1,),
            in_specs=[pl.BlockSpec(memory_space=pltpu.VMEM)],
            out_specs=pl.BlockSpec(memory_space=pl.ANY),
            scratch_shapes=[pltpu.SemaphoreType.DMA((count,))],
        ),
        compiler_params=params(),
        name="take_tiles",
    )(index, tiles)


def near_attend(edges, query, around, first, rows, heads, blk, hd, factor):
    width = heads * hd

    def kernel(edge_ref, q_ref, kv_ref, first_ref, acc_ref, stat_ref):
        r = pl.program_id(0)
        window = pl.ds(pl.multiple_of(r * blk, blk), 3 * blk)
        key = lax.broadcasted_iota(jnp.int32, (3 * blk, blk), 0)
        low = jnp.where((r == 0) & (edge_ref[0] == 1), blk, 0)
        high = jnp.where((r == rows - 1) & (edge_ref[1] == 1), 2 * blk, 3 * blk)
        usable = (key >= low) & (key < high)
        row = lax.broadcasted_iota(jnp.int32, (8, blk), 0)
        for e in range(heads):
            keys = slice(e * hd, (e + 1) * hd)
            values = slice(width + e * hd, width + (e + 1) * hd)
            q = q_ref[:, keys]
            near = jnp.where(usable, dot_t(kv_ref[window, keys], q) * factor, NEG)
            glob = dot_t(first_ref[:, keys], q) * factor
            top = jnp.maximum(
                jnp.max(near, axis=0, keepdims=True), jnp.max(glob, axis=0, keepdims=True)
            )
            near = jnp.exp2(near - top)
            glob = jnp.exp2(glob - top)
            total = jnp.sum(near, axis=0, keepdims=True) + jnp.sum(glob, axis=0, keepdims=True)
            acc_ref[e] = dot(kv_ref[window, values].T, near.astype(BF)) + dot(
                first_ref[:, values].T, glob.astype(BF)
            )
            stat_ref[e] = jnp.where(row == 0, top, total)

    return pl.pallas_call(
        kernel,
        out_shape=(
            jax.ShapeDtypeStruct((rows * heads, hd, blk), F32),
            jax.ShapeDtypeStruct((rows * heads, 8, blk), F32),
        ),
        grid_spec=pltpu.PrefetchScalarGridSpec(
            num_scalar_prefetch=1,
            grid=(rows,),
            in_specs=[
                pl.BlockSpec((blk, width), lambda r, s: (r, 0)),
                pl.BlockSpec(around.shape, lambda r, s: (0, 0)),
                pl.BlockSpec(first.shape, lambda r, s: (0, 0)),
            ],
            out_specs=(
                pl.BlockSpec((heads, hd, blk), lambda r, s: (r, 0, 0)),
                pl.BlockSpec((heads, 8, blk), lambda r, s: (r, 0, 0)),
            ),
        ),
        compiler_params=params(),
        name="near_attend",
    )(edges, query, around, first)


def rand_attend(slot, count, target, query, tiles, acc, stat, rows, heads, blk, hd, rand, peers, factor):
    items = rows * heads
    slots = items * rand

    def kernel(
        slot_ref, count_ref, target_ref, q_ref, acc_ref, stat_ref, tiles_ref, out_ref,
        buffer, done, in_sems, out_sems,
    ):
        def fetch(n):
            return pltpu.make_async_copy(tiles_ref.at[slot_ref[n]], buffer.at[n], in_sems.at[n])

        def deliver(i):
            return pltpu.make_async_copy(done.at[i], out_ref.at[target_ref[i]], out_sems.at[i])

        for n in range(slots):
            fetch(n).start()
        key = lax.broadcasted_iota(jnp.int32, (rand * blk, blk), 0)

        def step(r, carry):
            first = r * heads
            for n in range(heads * rand):
                fetch(first * rand + n).wait()
            at = pl.ds(pl.multiple_of(r * blk, blk), blk)
            each = range(heads)
            keys = [
                buffer[pl.ds((first + e) * rand, rand), :, :hd].reshape(rand * blk, hd) for e in each
            ]
            scores = [dot_t(keys[e], q_ref[at, e * hd : (e + 1) * hd]) for e in each]
            scores = [
                jnp.where(key < count_ref[first + e] * blk, scores[e] * factor, NEG) for e in each
            ]
            top0 = [stat_ref[first + e, 0:1] for e in each]
            total0 = [stat_ref[first + e, 1:2] for e in each]
            top = [jnp.maximum(jnp.max(scores[e], axis=0, keepdims=True), top0[e]) for e in each]
            keep = [jnp.exp2(top0[e] - top[e]) for e in each]
            expo = [jnp.exp2(scores[e] - top[e]) for e in each]
            total = [total0[e] * keep[e] + jnp.sum(expo[e], axis=0, keepdims=True) for e in each]
            values = [
                jnp.concatenate([buffer[(first + e) * rand + j, :, hd:] for j in range(rand)], axis=1)
                for e in each
            ]
            summed = [acc_ref[first + e] * keep[e] + dot(values[e], expo[e].astype(BF)) for e in each]
            for e in each:
                done[first + e] = (summed[e] / total[e]).T.astype(BF)
            for e in each:
                deliver(first + e).start()
            return carry

        lax.fori_loop(0, rows, step, 0)
        for i in range(items):
            deliver(i).wait()

    vmem = pl.BlockSpec(memory_space=pltpu.VMEM)
    anywhere = pl.BlockSpec(memory_space=pl.ANY)
    return pl.pallas_call(
        kernel,
        out_shape=jax.ShapeDtypeStruct((peers, blk, hd), BF),
        grid_spec=pltpu.PrefetchScalarGridSpec(
            num_scalar_prefetch=3,
            grid=(1,),
            in_specs=[vmem, vmem, vmem, anywhere],
            out_specs=anywhere,
            scratch_shapes=[
                pltpu.VMEM((slots, blk, 2 * hd), BF),
                pltpu.VMEM((items, blk, hd), BF),
                pltpu.SemaphoreType.DMA((slots,)),
                pltpu.SemaphoreType.DMA((items,)),
            ],
        ),
        compiler_params=params(),
        name="rand_attend",
    )(slot, count, target, query, acc, stat, tiles)


def local(tokens, w_qkv, item_at, rand_cols, rand_used):
    peers = lax.axis_size("seq")
    me = lax.axis_index("seq")
    groups = lax.axis_size("head")
    mine_y = lax.axis_index("head")
    heads, nblocks, rand = rand_cols.shape
    rows = nblocks // peers
    count, depth = tokens.shape
    blk = count // rows
    hd = w_qkv.shape[1] // (3 * heads)
    width = heads * hd
    items = heads * rows
    factor = math.log2(math.e) / math.sqrt(hd)

    asked = rand_cols.reshape(heads, peers, rows, rand).transpose(1, 2, 0, 3)
    asked = asked.reshape(peers, items * rand)
    order = jnp.arange(items * rand, dtype=jnp.int32)
    head_of = (order // rand) % heads
    code = order * items + head_of * rows + asked % rows
    mine = asked // rows == me
    low = jnp.min(jnp.where(mine, code, jnp.int32(1 << 30)), axis=1) % items
    high = jnp.max(jnp.where(mine, code, 0), axis=1) % items
    send_tile = jnp.stack([low, high], axis=1).reshape(-1)
    wanted = lax.dynamic_index_in_dim(asked, me, 0, keepdims=False)
    source = wanted // rows
    again = jnp.sum(
        ((source[:, None] == source[None, :]) & (order[None, :] < order[:, None])).astype(jnp.int32),
        axis=1,
    )
    slot = source * 2 + again
    my_used = lax.dynamic_slice_in_dim(rand_used, me * rows, rows, axis=1).T.reshape(-1)
    number = jnp.arange(items, dtype=jnp.int32)
    my_item = (number % heads) * nblocks + me * rows + number // heads
    place = jnp.arange(peers * items, dtype=jnp.int32)
    target = jnp.sum(
        jnp.where(item_at[0][None, :] == my_item[:, None], place[None, :] // items, 0), axis=1
    )
    home = (lax.dynamic_slice_in_dim(item_at[0], me * items, items) % nblocks) // rows
    edges = jnp.stack([me == 0, me == peers - 1]).astype(jnp.int32)

    def weight(shift, first, size):
        row = (mine_y + shift) % groups * depth
        return lax.dynamic_slice(w_qkv, (row, jnp.int32(first)), (depth, size))

    def w_pair(shift):
        return weight(shift, width, 2 * width)

    def w_query(shift):
        return weight(shift, 0, width)

    def spread(block, stride):
        holders = range(0, peers, 4 * stride)
        got = [
            lax.ppermute(block, "seq", [(h, h + k * stride) for h in holders]) for k in (1, 2, 3)
        ]
        return block + got[0] + got[1] + got[2]

    onward = [(i, (i + 1) % groups) for i in range(groups)]
    backward = [(b, a) for a, b in onward]
    across = [(i, (i + 2) % groups) for i in range(groups)]
    middle = count // 2
    from_low = lax.ppermute(tokens, "head", onward)
    from_high = lax.ppermute(tokens, "head", backward)
    zero = tokens[:blk]
    zero = jnp.where(me == 0, zero, jnp.zeros_like(zero))
    zero = spread(spread(spread(zero, peers // 4), peers // 16), peers // 64)
    far_top = lax.ppermute(from_low[:middle], "head", onward)
    far_bottom = lax.ppermute(from_high[middle:], "head", backward)
    total = dot(tokens, w_pair(0)) + dot(from_low, w_pair(3))
    total, zero = lax.optimization_barrier((total, zero))
    zero_low = lax.ppermute(zero, "head", onward)
    zero_high = lax.ppermute(zero, "head", backward)
    zero_far = lax.ppermute(zero, "head", across)
    total += dot(from_high, w_pair(1))
    far_top, far_bottom, zero_low, zero_high, zero_far = lax.optimization_barrier(
        (far_top, far_bottom, zero_low, zero_high, zero_far)
    )
    pair = jnp.concatenate(
        [
            (total[:middle] + dot(far_top, w_pair(2))).astype(BF),
            (total[middle:] + dot(far_bottom, w_pair(2))).astype(BF),
        ],
        axis=0,
    )
    up = [(i, i + 1) for i in range(peers - 1)]
    down = [(b, a) for a, b in up]
    before = lax.ppermute(pair[-blk:], "seq", up)
    after = lax.ppermute(pair[:blk], "seq", down)
    sent = pack_tiles(send_tile, pair, 2 * peers, rows, heads, blk, hd)
    sent, before, after, far_top, far_bottom = lax.optimization_barrier(
        (sent, before, after, far_top, far_bottom)
    )
    tiles = lax.all_to_all(sent, "seq", split_axis=0, concat_axis=0, tiled=True)

    around = jnp.concatenate([before, pair, after], axis=0)
    far = jnp.concatenate([far_top, far_bottom], axis=0)
    query = dot(far, w_query(2)) + dot(tokens, w_query(0))
    query = (query + dot(from_low, w_query(3)) + dot(from_high, w_query(1))).astype(BF)
    first = dot(zero, w_pair(0)) + dot(zero_low, w_pair(3))
    first = (first + dot(zero_high, w_pair(1)) + dot(zero_far, w_pair(2))).astype(BF)
    acc, stat = near_attend(edges, query, around, first, rows, heads, blk, hd, factor)
    done = rand_attend(
        slot, my_used, target, query, tiles, acc, stat, rows, heads, blk, hd, rand, peers, factor
    )
    back = lax.all_to_all(done, "seq", split_axis=0, concat_axis=0, tiled=True)
    return take_tiles(home, back)[None]


def solution(mesh):
    return jax.shard_map(
        local,
        mesh=mesh,
        in_specs=(
            P("seq", "head"),
            P(None, "head"),
            P("head", None),
            P("head", None, None),
            P("head", None),
        ),
        out_specs=P("head", "seq", None, None),
        check_vma=False,
    )
```

time: 353 us -> 341 us (0.966)
  waiting for transfers between devices: 217 us -> 241 us
  Pallas kernels: 43.4 us -> 27.9 us
  starting transfers between devices: 48.4 us -> 39.5 us
  local copies, waits for them, and re-layouts: 11.3 us -> 5 us
    ppermute x1, starting transfers between devices: 14 us -> 2.09 us  [local(): after = lax.ppermute(pair[:blk], 'seq', down)]
    ppermute x1, waiting for transfers between devices: 0.01 us -> 11.7 us  [local(): far_top = lax.ppermute(from_low[:middle], 'head', onward)]
    pallas_call x2, Pallas kernels: 22.7 us -> 14.8 us  [the longest x1 9.39 us: near_attend(): pl.pallas_call(kernel, out_shape=(jax.ShapeDtypeStruct((rows * heads, hd,...]
    pallas_call x1, Pallas kernels: 18.9 us -> 11.3 us  [rand_attend(): pl.pallas_call(kernel, out_shape=jax.ShapeDtypeStruct((peers, blk, hd), B...]
    ppermute x12, waiting for transfers between devices: 6.76 us -> 14.1 us  [the longest x9 14.1 us: spread(): lax.ppermute(block, 'seq', [(h, h + k * stride) for h in holders])]
    all_to_all x1, waiting for transfers between devices: 159 us -> 164 us  [local(): tiles = lax.all_to_all(sent, 'seq', split_axis=0, concat_axis=0, tiled=True)]
    unnamed x16 -> x38, local copies, waits for them, and re-layouts: 5.58 us -> 1.43 us
    dot_general x7 -> x13, matrix products: 21.9 us -> 19.7 us  [dot(): return jnp.dot(a, b, preferred_element_type=F32)]
  transfers between devices with their start and end apart: 20 -> 20, of which waited for: 5 -> 4; matrix products, arithmetic and copies ran while one was open for 10% -> 8% of each run, Pallas kernels for 6% -> 4%
where the time goes in v4:
time: 341 us
  waiting for transfers between devices  241 us (71%)
  starting transfers between devices  39.5 us (12%)
  Pallas kernels  27.9 us (8%)
  matrix products  19.7 us (6%)
  other arithmetic  6.45 us (2%)
  local copies, waits for them, and re-layouts  5 us (1%)
    all_to_all x1, waiting for transfers between devices, local(): tiles = lax.all_to_all(sent, 'seq', split_axis=0, concat_axis=0, tiled=True)  164 us
    all_to_all x1, waiting for transfers between devices, local(): back = lax.all_to_all(done, 'seq', split_axis=0, concat_axis=0, tiled=True)  51.2 us
    dot_general x13, matrix products, dot(): return jnp.dot(a, b, preferred_element_type=F32)  19.7 us
    ppermute x9, waiting for transfers between devices, spread(): lax.ppermute(block, 'seq', [(h, h + k * stride) for h in holders])  14.1 us
    ppermute x1, waiting for transfers between devices, local(): far_top = lax.ppermute(from_low[:middle], 'head', onward)  11.7 us
    pallas_call x1, Pallas kernels, rand_attend(): pl.pallas_call(kernel, out_shape=jax.ShapeDtypeStruct((peers, blk, hd), B...  11.3 us
    all_to_all x1, starting transfers between devices, local(): tiles = lax.all_to_all(sent, 'seq', split_axis=0, concat_axis=0, tiled=True)  11 us
    pallas_call x1, Pallas kernels, near_attend(): pl.pallas_call(kernel, out_shape=(jax.ShapeDtypeStruct((rows * heads, hd,...  9.39 us
  transfers between devices with their start and end apart: 20, of which 4 were waited for; matrix products, arithmetic and copies ran while one was open for 8% of the time, Pallas kernels for 4%

profile of v4, /device:TPU:1, one launch (start us, length us, event | category | flops | bytes accessed | tf_op | source)
XLA Modules:
  0.0 340.7 jit_solution(6155461439773235809)
XLA Ops:
  0.0 2.1 collective-permute-start
  2.1 0.9 slice_select_fusion
  3.1 0.7 collective-permute-start.3
  3.8 0.7 collective-permute-start.2
  4.4 0.7 collective-permute-start.1
  5.1 1.5 collective-permute-start.10
  6.6 4.8 %fusion.16 = f32[1024,1024]{0,1:T(8,128)} fusion(bf16[1024,512]{1,0:T(8,128)(2,1)} %param.5, bf16[2048,1536]{1,0:T(8,128)(2,1)} %param.6, s32[]{:T(128)S(6)} %select_n.214), kind=kOutput, calls=%fused_computation.27 | convolution fusion | flops 1073741824 | bytes 6291460 | tf_op jit(solution)/shard_map/dot_general | solution.py:17
  11.4 0.3 reshape.216
  11.8 1.1 add_add_fusion.2
  12.9 0.7 collective-permute-start.6
  13.5 0.7 collective-permute-start.5
  14.2 0.7 collective-permute-start.4
  14.9 0.7 select_reduce_fusion.1
  15.7 0.7 collective-permute-start.9
  16.4 0.7 collective-permute-start.8
  17.0 1.3 collective-permute-start.7
  18.4 14.1 %collective-permute-done.7 = bf16[128,512]{1,0:T(8,128)(2,1)S(1)} collective-permute-done((bf16[128,512]{1,0:T(8,128)(2,1)S(1)}, bf16[128,512]{1,0:T(8,128)(2,1)S(1)}, u32[]{:S(2)}, u32[]{:S(2)}) %collective-permute-start.7) | collective-permute-done | bytes 131104 | tf_op jit(solution)/shard_map/ppermute | solution.py:269
  32.5 4.0 %add_bitcast_fusion = f32[1024,1024]{1,0:T(8,128)S(1)} fusion(f32[1024,1024]{0,1:T(8,128)} %fusion.16, bf16[1024,512]{1,0:T(8,128)(2,1)S(1)} %collective-permute-done, bf16[2048,1536]{1,0:T(8,128)(2,1)} %param.6, s32[]{:T(128)S(6)} %select_n.216), kind=kOutput, calls=%fused_computation.1 | convolution fusion | flops 1074790400 | bytes 10485764 | tf_op jit(solution)/shard_map/dot_general | solution.py:17
  36.5 0.2 collective-permute-start.13
  36.7 2.6 collective-permute-start.14
  39.3 0.5 collective-permute-start.15
  39.8 0.5 collective-permute-start.11
  40.3 2.4 collective-permute-start.12
  42.7 1.2 fusion.10
  43.9 1.4 bitcast_add_fusion
  45.4 11.7 %collective-permute-done.11 = bf16[512,512]{1,0:T(8,128)(2,1)S(1)} collective-permute-done((bf16[512,512]{1,0:T(8,128)(2,1)S(1)}, bf16[512,512]{1,0:T(8,128)(2,1)S(1)}, u32[]{:S(2)}, u32[]{:S(2)}) %collective-permute-start.11) | collective-permute-done | bytes 524320 | tf_op jit(solution)/shard_map/ppermute | solution.py:282
  57.1 0.7 fusion
  57.8 0.7 fusion.1
  58.6 0.7 slice.32
  59.3 4.2 %collective-permute-start.16 = (bf16[128,1024]{1,0:T(8,128)(2,1)}, bf16[128,1024]{1,0:T(8,128)(2,1)}, u32[]{:S(2)}, u32[]{:S(2)}) collective-permute-start(bf16[128,1024]{1,0:T(8,128)(2,1)} %slice.32), channel_id=1, source_target_pairs={{0,4},{4,8},{8,12},{12,16},{16,20},{20,24},{24,28},{28,32},{32,36}... | collective-permute-start | bytes 786440 | tf_op jit(solution)/shard_map/ppermute | solution.py:302
  63.5 0.7 slice.33
  64.2 2.1 collective-permute-start.17
  66.3 0.1 copy.32
  66.4 0.1 reshape.219.index_ref
  66.6 0.2 pad_maximum_fusion.1.pair_ref
  66.8 5.4 %pack_tiles.1 = bf16[128,128,256]{2,1,0:T(8,128)(2,1)} custom-call(s32[128]{0:T(128)S(1)} %reshape.219.index_ref, bf16[1024,1024]{1,0:T(8,128)(2,1)S(1)} %pad_maximum_fusion.1.pair_ref), custom_call_target="tpu_custom_call" | custom-call | tf_op jit(solution)/shard_map/pack_tiles/pallas_call | solution.py:45
  72.2 0.0 collective-permute-done.17
  72.2 11.0 %all-to-all-start = ((bf16[128,128,256]{2,1,0:T(8,128)(2,1)}), bf16[128,128,256]{2,1,0:T(8,128)(2,1)}, u32[]{:S(2)}, u32[]{:S(2)}) async-start(bf16[128,128,256]{2,1,0:T(8,128)(2,1)} %pack_tiles.1), calls=%async_computation | async-start | bytes 16777216 | tf_op jit(solution)/shard_map/all_to_all | solution.py:308
  83.2 1.2 copy.30
  84.5 0.1 dynamic-slice_bitcast_fusion
  84.6 0.1 copy.31
  84.6 0.1 reshape.218.count_ref
  84.7 0.2 dynamic-slice_reduce_fusion
  84.9 0.1 add_convert_fusion.edge_ref
  85.0 0.2 convert_reduce_fusion
  85.2 0.2 select_reduce_fusion.2.target_ref
  85.4 2.2 fusion.33
  87.7 0.0 slice-start.3
  87.7 1.9 fusion.31
  89.6 1.6 fusion.18
  91.3 0.3 fusion.12
  91.6 0.3 convolution_add_fusion.1
  92.0 0.3 fusion.4.first_ref
  92.3 0.7 fusion.5
  93.0 1.3 pad_maximum_fusion.kv_ref
  94.4 0.8 fusion.2.q_ref
  95.2 9.4 %near_attend.1 = (f32[32,128,128]{2,1,0:T(8,128)S(1)}, f32[32,8,128]{2,1,0:T(8,128)S(1)}) custom-call(s32[2]{0:T(128)S(1)} %add_convert_fusion.edge_ref, bf16[1024,512]{1,0:T(8,128)(2,1)S(1)} %fusion.2.q_ref, bf16[1280,1024]{1,0:T(8,128)(2,1)S(1)} %pad_maximum_fusion.kv_ref, bf16[128,1024]{1,0:T(8,128)(2,1)S(1)} %fusion.4.first_ref), custom_call_target="tpu_custom_call" | custom-call | tf_op jit(solution)/shard_map/near_attend/pallas_call | solution.py:118
  104.6 164.4 %all-to-all-done.tiles_ref = bf16[128,128,256]{2,1,0:T(8,128)(2,1)} async-done(((bf16[128,128,256]{2,1,0:T(8,128)(2,1)}), bf16[128,128,256]{2,1,0:T(8,128)(2,1)}, u32[]{:S(2)}, u32[]{:S(2)}) %all-to-all-start) | async-done | bytes 8388640 | tf_op jit(solution)/shard_map/all_to_all | solution.py:308
  269.0 11.3 %rand_attend.1 = bf16[64,128,128]{2,1,0:T(8,128)(2,1)S(1)} custom-call(s32[128]{0:T(128)S(1)} %multiply_add_fusion.1.slot_ref, s32[32]{0:T(128)S(1)} %reshape.218.count_ref, s32[32]{0:T(128)S(1)} %select_reduce_fusion.2.target_ref, bf16[1024,512]{1,0:T(8,128)(2,1)S(1)} %fusion.2.q_ref, f32[32,128,128]{2,1,0:T(8,128)S(1)} %get-tuple-element.30.acc_ref, ...), custom_call_target="tpu_custom_call" | custom-call | tf_op jit(solution)/shard_map/rand_attend/pallas_call | solution.py:196
  280.3 1.3 copy-done.1
  281.6 5.9 %all-to-all-start.1 = ((bf16[64,128,128]{2,1,0:T(8,128)(2,1)}), bf16[64,128,128]{2,1,0:T(8,128)(2,1)S(1)}, u32[]{:S(2)}, u32[]{:S(2)}) async-start(bf16[64,128,128]{2,1,0:T(8,128)(2,1)} %copy-done.1), calls=%async_computation.1 | async-start | bytes 4194304 | tf_op jit(solution)/shard_map/all_to_all | solution.py:320
  287.5 0.1 and_select_fusion.5.index_ref
  287.6 51.2 %all-to-all-done.1.in_ref = bf16[64,128,128]{2,1,0:T(8,128)(2,1)S(1)} async-done(((bf16[64,128,128]{2,1,0:T(8,128)(2,1)}), bf16[64,128,128]{2,1,0:T(8,128)(2,1)S(1)}, u32[]{:S(2)}, u32[]{:S(2)}) %all-to-all-start.1) | async-done | bytes 2097184 | tf_op jit(solution)/shard_map/all_to_all | solution.py:320
  338.8 1.8 take_tiles.1
  (64 shorter events, 0.3 us)
Async XLA Ops:
  0.0 84.5 %copy-start = (s32[4,512]{1,0:T(4,128)S(1)}, s32[4,512]{1,0:T(4,128)}, u32[]{:S(2)}) copy-start(s32[4,512]{1,0:T(4,128)} %param.9) | copy-start | bytes 24580
  0.0 11.4 %copy-start.13 = (s32[4,512,4]{1,2,0:T(4,128)S(1)}, s32[4,512,4]{1,2,0:T(4,128)}, u32[]{:S(2)}) copy-start(s32[4,512,4]{1,2,0:T(4,128)} %param.8) | copy-start | bytes 98308
  0.0 32.5 %collective-permute-start = (bf16[1024,512]{1,0:T(8,128)(2,1)}, bf16[1024,512]{1,0:T(8,128)(2,1)S(1)}, u32[]{:S(2)}, u32[]{:S(2)}) collective-permute-start(bf16[1024,512]{1,0:T(8,128)(2,1)} %param.5), channel_id=1, source_target_pairs={{0,1},{1,2},{2,3},{3,0},{4,5},{5,6},{6,7},{7,4},{8,9},{9,10},{10,1... | collective-permute-start | bytes 3145736 | tf_op jit(solution)/shard_map/ppermute | solution.py:277
  3.1 8.7 %collective-permute-start.3 = (bf16[128,512]{1,0:T(8,128)(2,1)S(1)}, bf16[128,512]{1,0:T(8,128)(2,1)S(1)}, u32[]{:S(2)}, u32[]{:S(2)}) collective-permute-start(bf16[128,512]{1,0:T(8,128)(2,1)S(1)} %slice_select_fusion), channel_id=1, source_target_pairs={{0,192},{1,193},{2,194},{3,195}} | collective-permute-start | bytes 393224 | tf_op jit(solution)/shard_map/ppermute | solution.py:269
  3.8 8.0 %collective-permute-start.2 = (bf16[128,512]{1,0:T(8,128)(2,1)S(1)}, bf16[128,512]{1,0:T(8,128)(2,1)S(1)}, u32[]{:S(2)}, u32[]{:S(2)}) collective-permute-start(bf16[128,512]{1,0:T(8,128)(2,1)S(1)} %slice_select_fusion), channel_id=1, source_target_pairs={{0,128},{1,129},{2,130},{3,131}} | collective-permute-start | bytes 393224 | tf_op jit(solution)/shard_map/ppermute | solution.py:269
  4.4 7.4 %collective-permute-start.1 = (bf16[128,512]{1,0:T(8,128)(2,1)S(1)}, bf16[128,512]{1,0:T(8,128)(2,1)S(1)}, u32[]{:S(2)}, u32[]{:S(2)}) collective-permute-start(bf16[128,512]{1,0:T(8,128)(2,1)S(1)} %slice_select_fusion), channel_id=1, source_target_pairs={{0,64},{1,65},{2,66},{3,67}} | collective-permute-start | bytes 393224 | tf_op jit(solution)/shard_map/ppermute | solution.py:269
  5.1 35.2 %collective-permute-start.10 = (bf16[1024,512]{1,0:T(8,128)(2,1)}, bf16[1024,512]{1,0:T(8,128)(2,1)S(1)}, u32[]{:S(2)}, u32[]{:S(2)}) collective-permute-start(bf16[1024,512]{1,0:T(8,128)(2,1)} %param.5), channel_id=1, source_target_pairs={{1,0},{2,1},{3,2},{0,3},{5,4},{6,5},{7,6},{4,7},{9,8},{10,9},{11,1... | collective-permute-start | bytes 3145736 | tf_op jit(solution)/shard_map/ppermute | solution.py:278
  11.7 24.8 %copy-start.4 = (s32[4,64,8,4]{2,1,3,0:T(8,128)}, s32[4,64,8,4]{2,1,3,0:T(8,128)S(1)}, u32[]{:S(2)}) copy-start(s32[4,64,8,4]{2,1,3,0:T(8,128)S(1)} %reshape.216) | copy-start | bytes 98308
  12.9 2.8 collective-permute-start.6
  13.5 2.1 collective-permute-start.5
  14.2 1.4 collective-permute-start.4
  15.7 2.7 collective-permute-start.9
  16.4 2.0 collective-permute-start.8
  17.0 15.4 %collective-permute-start.7 = (bf16[128,512]{1,0:T(8,128)(2,1)S(1)}, bf16[128,512]{1,0:T(8,128)(2,1)S(1)}, u32[]{:S(2)}, u32[]{:S(2)}) collective-permute-start(bf16[128,512]{1,0:T(8,128)(2,1)S(1)} %add_add_fusion.1), channel_id=1, source_target_pairs={{0,4},{16,20},{32,36},{48,52},{64,68},{80,84},{96,100},{112,116},{... | collective-permute-start | bytes 393224 | tf_op jit(solution)/shard_map/ppermute | solution.py:269
  32.4 10.2 %slice-start = ((s8[6291456]{0:T(1024)(128)(4,1)}), s8[4194304]{0:T(1024)(128)(4,1)S(1)}, s32[]{:S(2)}) async-start(s8[6291456]{0:T(1024)(128)(4,1)} %bitcast.54), calls=%async_computation.2 | async-start | bytes 8388608
  32.5 10.2 %slice-start.1 = ((s8[6291456]{0:T(1024)(128)(4,1)}), s8[2097152]{0:T(1024)(128)(4,1)S(1)}, s32[]{:S(2)}) async-start(s8[6291456]{0:T(1024)(128)(4,1)} %bitcast.54), calls=%async_computation.3 | async-start | bytes 4194304
  36.5 8.8 %collective-permute-start.13 = (bf16[128,512]{1,0:T(8,128)(2,1)S(1)}, bf16[128,512]{1,0:T(8,128)(2,1)S(1)}, u32[]{:S(2)}, u32[]{:S(2)}) collective-permute-start(bf16[128,512]{1,0:T(8,128)(2,1)S(1)} %add_add_fusion), channel_id=1, source_target_pairs={{0,1},{1,2},{2,3},{3,0},{4,5},{5,6},{6,7},{7,4},{8,9},{9,10},{10,1... | collective-permute-start | bytes 393224 | tf_op jit(solution)/shard_map/ppermute | solution.py:286
  36.7 8.6 %collective-permute-start.14 = (bf16[128,512]{1,0:T(8,128)(2,1)S(1)}, bf16[128,512]{1,0:T(8,128)(2,1)S(1)}, u32[]{:S(2)}, u32[]{:S(2)}) collective-permute-start(bf16[128,512]{1,0:T(8,128)(2,1)S(1)} %add_add_fusion), channel_id=1, source_target_pairs={{1,0},{2,1},{3,2},{0,3},{5,4},{6,5},{7,6},{4,7},{9,8},{10,9},{11,1... | collective-permute-start | bytes 393224 | tf_op jit(solution)/shard_map/ppermute | solution.py:287
  39.3 6.1 %collective-permute-start.15 = (bf16[128,512]{1,0:T(8,128)(2,1)S(1)}, bf16[128,512]{1,0:T(8,128)(2,1)S(1)}, u32[]{:S(2)}, u32[]{:S(2)}) collective-permute-start(bf16[128,512]{1,0:T(8,128)(2,1)S(1)} %add_add_fusion), channel_id=1, source_target_pairs={{0,2},{1,3},{2,0},{3,1},{4,6},{5,7},{6,4},{7,5},{8,10},{9,11},{10,... | collective-permute-start | bytes 393224 | tf_op jit(solution)/shard_map/ppermute | solution.py:288
  39.8 17.3 %collective-permute-start.11 = (bf16[512,512]{1,0:T(8,128)(2,1)S(1)}, bf16[512,512]{1,0:T(8,128)(2,1)S(1)}, u32[]{:S(2)}, u32[]{:S(2)}) collective-permute-start(bf16[512,512]{1,0:T(8,128)(2,1)S(1)} %slice.29), channel_id=1, source_target_pairs={{0,1},{1,2},{2,3},{3,0},{4,5},{5,6},{6,7},{7,4},{8,9},{9,10},{10,1... | collective-permute-start | bytes 1572872 | tf_op jit(solution)/shard_map/ppermute | solution.py:282
  40.3 5.0 %copy-start.2 = (bf16[1024,512]{1,0:T(8,128)(2,1)}, bf16[1024,512]{1,0:T(8,128)(2,1)S(1)}, u32[]{:S(2)}) copy-start(bf16[1024,512]{1,0:T(8,128)(2,1)S(1)} %collective-permute-done.10) | copy-start | bytes 3145732
  40.3 16.8 %collective-permute-start.12 = (bf16[512,512]{1,0:T(8,128)(2,1)S(1)}, bf16[512,512]{1,0:T(8,128)(2,1)S(1)}, u32[]{:S(2)}, u32[]{:S(2)}) collective-permute-start(bf16[512,512]{1,0:T(8,128)(2,1)S(1)} %slice.30), channel_id=1, source_target_pairs={{1,0},{2,1},{3,2},{0,3},{5,4},{6,5},{7,6},{4,7},{9,8},{10,9},{11,1... | collective-permute-start | bytes 1572872 | tf_op jit(solution)/shard_map/ppermute | solution.py:283
  45.3 13.2 %copy-start.11 = (bf16[128,512]{1,0:T(8,128)(2,1)}, bf16[128,512]{1,0:T(8,128)(2,1)S(1)}, u32[]{:S(2)}) copy-start(bf16[128,512]{1,0:T(8,128)(2,1)S(1)} %collective-permute-done.14) | copy-start | bytes 393220
  45.4 13.2 %copy-start.9 = (bf16[128,512]{1,0:T(8,128)(2,1)}, bf16[128,512]{1,0:T(8,128)(2,1)S(1)}, u32[]{:S(2)}) copy-start(bf16[128,512]{1,0:T(8,128)(2,1)S(1)} %collective-permute-done.15) | copy-start | bytes 393220
  57.1 1.5 copy-start.5
  57.1 1.5 copy-start.7
  59.3 12.9 %collective-permute-start.16 = (bf16[128,1024]{1,0:T(8,128)(2,1)}, bf16[128,1024]{1,0:T(8,128)(2,1)}, u32[]{:S(2)}, u32[]{:S(2)}) collective-permute-start(bf16[128,1024]{1,0:T(8,128)(2,1)} %slice.32), channel_id=1, source_target_pairs={{0,4},{4,8},{8,12},{12,16},{16,20},{20,24},{24,28},{28,32},{32,36}... | collective-permute-start | bytes 786440 | tf_op jit(solution)/shard_map/ppermute | solution.py:302
  64.2 8.0 %collective-permute-start.17 = (bf16[128,1024]{1,0:T(8,128)(2,1)}, bf16[128,1024]{1,0:T(8,128)(2,1)}, u32[]{:S(2)}, u32[]{:S(2)}) collective-permute-start(bf16[128,1024]{1,0:T(8,128)(2,1)} %slice.33), channel_id=1, source_target_pairs={{4,0},{8,4},{12,8},{16,12},{20,16},{24,20},{28,24},{32,28},{36,32}... | collective-permute-start | bytes 786440 | tf_op jit(solution)/shard_map/ppermute | solution.py:303
  72.2 13.0 %copy-start.14 = (s32[1,2048]{1,0:T(1,128)S(1)}, s32[1,2048]{1,0:T(1,128)}, u32[]{:S(2)}) copy-start(s32[1,2048]{1,0:T(1,128)} %param.7) | copy-start | bytes 24580
  72.2 196.8 %all-to-all-start = ((bf16[128,128,256]{2,1,0:T(8,128)(2,1)}), bf16[128,128,256]{2,1,0:T(8,128)(2,1)}, u32[]{:S(2)}, u32[]{:S(2)}) async-start(bf16[128,128,256]{2,1,0:T(8,128)(2,1)} %pack_tiles.1), calls=%async_computation | async-start | bytes 16777216 | tf_op jit(solution)/shard_map/all_to_all | solution.py:308
  85.4 5.8 %slice-start.2 = ((s8[6291456]{0:T(1024)(128)(4,1)}), s8[4194304]{0:T(1024)(128)(4,1)S(1)}, s32[]{:S(2)}) async-start(s8[6291456]{0:T(1024)(128)(4,1)} %bitcast.56), calls=%async_computation.4 | async-start | bytes 8388608
  87.7 1.9 copy-start.10
  87.7 3.6 %slice-start.3 = ((s8[6291456]{0:T(1024)(128)(4,1)}), s8[2097152]{0:T(1024)(128)(4,1)S(1)}, s32[]{:S(2)}) async-start(s8[6291456]{0:T(1024)(128)(4,1)} %bitcast.56), calls=%async_computation.5 | async-start | bytes 4194304
  89.6 2.3 copy-start.12
  89.6 2.7 copy-start.6
  89.6 2.7 copy-start.8
  92.3 2.0 copy-start.3
  280.3 1.3 copy-start.1
  281.6 57.2 %all-to-all-start.1 = ((bf16[64,128,128]{2,1,0:T(8,128)(2,1)}), bf16[64,128,128]{2,1,0:T(8,128)(2,1)S(1)}, u32[]{:S(2)}, u32[]{:S(2)}) async-start(bf16[64,128,128]{2,1,0:T(8,128)(2,1)} %copy-done.1), calls=%async_computation.1 | async-start | bytes 4194304 | tf_op jit(solution)/shard_map/all_to_all | solution.py:320

commit v5 on v4

--- a/solution.py
+++ b/solution.py
@@ -281,15 +281,9 @@
     zero = spread(spread(spread(zero, peers // 4), peers // 16), peers // 64)
     far_top = lax.ppermute(from_low[:middle], "head", onward)
     far_bottom = lax.ppermute(from_high[middle:], "head", backward)
-    total = dot(tokens, w_pair(0)) + dot(from_low, w_pair(3))
-    total, zero = lax.optimization_barrier((total, zero))
-    zero_low = lax.ppermute(zero, "head", onward)
-    zero_high = lax.ppermute(zero, "head", backward)
-    zero_far = lax.ppermute(zero, "head", across)
-    total += dot(from_high, w_pair(1))
-    far_top, far_bottom, zero_low, zero_high, zero_far = lax.optimization_barrier(
-        (far_top, far_bottom, zero_low, zero_high, zero_far)
-    )
+    own, zero = lax.optimization_barrier((tokens, zero))
+    total = dot(own, w_pair(0)) + dot(from_low, w_pair(3)) + dot(from_high, w_pair(1))
+    far_top, far_bottom, zero = lax.optimization_barrier((far_top, far_bottom, zero))
     pair = jnp.concatenate(
         [
             (total[:middle] + dot(far_top, w_pair(2))).astype(BF),
@@ -302,11 +296,14 @@
     before = lax.ppermute(pair[-blk:], "seq", up)
     after = lax.ppermute(pair[:blk], "seq", down)
     sent = pack_tiles(send_tile, pair, 2 * peers, rows, heads, blk, hd)
-    sent, before, after, far_top, far_bottom = lax.optimization_barrier(
-        (sent, before, after, far_top, far_bottom)
+    sent, before, after, far_top, far_bottom, zero = lax.optimization_barrier(
+        (sent, before, after, far_top, far_bottom, zero)
     )
     tiles = lax.all_to_all(sent, "seq", split_axis=0, concat_axis=0, tiled=True)
 
+    zero_low = lax.ppermute(zero, "head", onward)
+    zero_high = lax.ppermute(zero, "head", backward)
+    zero_far = lax.ppermute(zero, "head", across)
     around = jnp.concatenate([before, pair, after], axis=0)
     far = jnp.concatenate([far_top, far_bottom], axis=0)
     query = dot(far, w_query(2)) + dot(tokens, w_query(0))

time: 341 us -> 334 us (0.979)
  waiting for transfers between devices: 241 us -> 233 us
    ppermute x1, waiting for transfers between devices: 11.7 us -> 6.68 us  [local(): far_top = lax.ppermute(from_low[:middle], 'head', onward)]
    all_to_all x1, waiting for transfers between devices: 164 us -> 160 us  [local(): tiles = lax.all_to_all(sent, 'seq', split_axis=0, concat_axis=0, tiled=True)]
  transfers between devices with their start and end apart: 20 -> 20, of which waited for: 4 -> 6; matrix products, arithmetic and copies ran while one was open for 8% -> 8% of each run, Pallas kernels for 4% -> 4%
where the time goes in v5:
time: 334 us
  waiting for transfers between devices  233 us (70%)
  starting transfers between devices  41.6 us (12%)
  Pallas kernels  27.9 us (8%)
  matrix products  17.1 us (5%)
  local copies, waits for them, and re-layouts  7.02 us (2%)
  other arithmetic  6.64 us (2%)
    all_to_all x1, waiting for transfers between devices, local(): tiles = lax.all_to_all(sent, 'seq', split_axis=0, concat_axis=0, tiled=True)  160 us
    all_to_all x1, waiting for transfers between devices, local(): back = lax.all_to_all(done, 'seq', split_axis=0, concat_axis=0, tiled=True)  51.2 us
    dot_general x13, matrix products, dot(): return jnp.dot(a, b, preferred_element_type=F32)  17.1 us
    ppermute x9, waiting for transfers between devices, spread(): lax.ppermute(block, 'seq', [(h, h + k * stride) for h in holders])  13.1 us
    all_to_all x1, starting transfers between devices, local(): tiles = lax.all_to_all(sent, 'seq', split_axis=0, concat_axis=0, tiled=True)  11.7 us
    pallas_call x1, Pallas kernels, rand_attend(): pl.pallas_call(kernel, out_shape=jax.ShapeDtypeStruct((peers, blk, hd), B...  11.3 us
    pallas_call x1, Pallas kernels, near_attend(): pl.pallas_call(kernel, out_shape=(jax.ShapeDtypeStruct((rows * heads, hd,...  9.39 us
    ppermute x9, starting transfers between devices, spread(): lax.ppermute(block, 'seq', [(h, h + k * stride) for h in holders])  7.28 us
  transfers between devices with their start and end apart: 20, of which 6 were waited for; matrix products, arithmetic and copies ran while one was open for 8% of the time, Pallas kernels for 4%

profile of v5, /device:TPU:1, one launch (start us, length us, event | category | flops | bytes accessed | tf_op | source)
XLA Modules:
  0.0 333.6 jit_solution(13371336480968932764)
XLA Ops:
  0.0 0.9 slice_select_fusion
  0.9 0.7 collective-permute-start.2
  1.6 0.7 collective-permute-start.1
  2.3 1.3 collective-permute-start
  3.6 2.1 collective-permute-start.9
  5.7 1.4 collective-permute-start.10
  7.2 2.0 reshape.216
  9.3 1.0 add_add_fusion.2
  10.3 0.7 collective-permute-start.5
  11.0 0.7 collective-permute-start.4
  11.6 0.7 collective-permute-start.3
  12.3 1.8 select_reduce_fusion.1
  14.1 0.7 collective-permute-start.8
  14.8 0.7 collective-permute-start.7
  15.5 1.3 collective-permute-start.6
  16.8 13.0 %collective-permute-done.6 = bf16[128,512]{1,0:T(8,128)(2,1)S(1)} collective-permute-done((bf16[128,512]{1,0:T(8,128)(2,1)S(1)}, bf16[128,512]{1,0:T(8,128)(2,1)S(1)}, u32[]{:S(2)}, u32[]{:S(2)}) %collective-permute-start.6) | collective-permute-done | bytes 131104 | tf_op jit(solution)/shard_map/ppermute | solution.py:269
  29.9 2.9 fusion.18
  32.9 0.2 collective-permute-start.11
  33.1 1.1 slice.30
  34.2 2.7 collective-permute-start.12
  36.8 1.2 fusion.15
  38.1 2.5 bitcast_add_fusion
  40.6 6.7 %collective-permute-done.11 = bf16[512,512]{1,0:T(8,128)(2,1)S(1)} collective-permute-done((bf16[512,512]{1,0:T(8,128)(2,1)S(1)}, bf16[512,512]{1,0:T(8,128)(2,1)S(1)}, u32[]{:S(2)}, u32[]{:S(2)}) %collective-permute-start.11) | collective-permute-done | bytes 524320 | tf_op jit(solution)/shard_map/ppermute | solution.py:282
  47.3 0.1 collective-permute-done.12
  47.4 0.7 fusion
  48.1 0.7 fusion.1
  48.8 0.2 copy-done.3
  49.1 0.8 slice.32
  49.9 4.3 %collective-permute-start.13 = (bf16[128,1024]{1,0:T(8,128)(2,1)}, bf16[128,1024]{1,0:T(8,128)(2,1)S(1)}, u32[]{:S(2)}, u32[]{:S(2)}) collective-permute-start(bf16[128,1024]{1,0:T(8,128)(2,1)} %slice.32), channel_id=1, source_target_pairs={{0,4},{4,8},{8,12},{12,16},{16,20},{20,24},{24,28},{28,32},{32,36}... | collective-permute-start | bytes 786440 | tf_op jit(solution)/shard_map/ppermute | solution.py:296
  54.2 0.7 slice.33
  55.0 1.9 collective-permute-start.14
  56.9 0.1 copy.26
  57.0 0.1 reshape.219.index_ref
  57.2 1.7 pad_maximum_fusion.1.pair_ref
  58.9 5.4 %pack_tiles.1 = bf16[128,128,256]{2,1,0:T(8,128)(2,1)} custom-call(s32[128]{0:T(128)S(1)} %reshape.219.index_ref, bf16[1024,1024]{1,0:T(8,128)(2,1)S(1)} %pad_maximum_fusion.1.pair_ref), custom_call_target="tpu_custom_call" | custom-call | tf_op jit(solution)/shard_map/pack_tiles/pallas_call | solution.py:45
  64.4 11.7 %all-to-all-start = ((bf16[128,128,256]{2,1,0:T(8,128)(2,1)}), bf16[128,128,256]{2,1,0:T(8,128)(2,1)}, u32[]{:S(2)}, u32[]{:S(2)}) async-start(bf16[128,128,256]{2,1,0:T(8,128)(2,1)} %pack_tiles.1), calls=%async_computation | async-start | bytes 16777216 | tf_op jit(solution)/shard_map/all_to_all | solution.py:302
  76.1 0.2 copy.24
  76.3 0.1 dynamic-slice_bitcast_fusion
  76.4 0.1 copy.25
  76.5 0.1 reshape.218.count_ref
  76.5 0.2 dynamic-slice_reduce_fusion
  76.9 0.2 convert_reduce_fusion
  77.0 0.2 select_reduce_fusion.2.target_ref
  77.3 1.9 fusion.29
  79.2 1.9 fusion.27
  81.1 2.3 collective-permute-start.17
  83.4 1.3 collective-permute-start.16
  84.7 0.5 collective-permute-start.15
  85.2 1.7 fusion.6
  87.0 2.2 fusion.2.q_ref
  89.2 0.3 pad_maximum_fusion.kv_ref
  89.6 0.3 fusion.20
  89.9 1.2 collective-permute-done.16
  91.1 0.3 fusion.10
  91.4 0.3 fusion.13
  91.7 0.3 fusion.5.first_ref
  92.0 9.4 %near_attend.1 = (f32[32,128,128]{2,1,0:T(8,128)S(1)}, f32[32,8,128]{2,1,0:T(8,128)S(1)}) custom-call(s32[2]{0:T(128)S(1)} %add_convert_fusion.edge_ref, bf16[1024,512]{1,0:T(8,128)(2,1)S(1)} %fusion.2.q_ref, bf16[1280,1024]{1,0:T(8,128)(2,1)S(1)} %pad_maximum_fusion.kv_ref, bf16[128,1024]{1,0:T(8,128)(2,1)S(1)} %fusion.5.first_ref), custom_call_target="tpu_custom_call" | custom-call | tf_op jit(solution)/shard_map/near_attend/pallas_call | solution.py:118
  101.4 160.4 %all-to-all-done.tiles_ref = bf16[128,128,256]{2,1,0:T(8,128)(2,1)} async-done(((bf16[128,128,256]{2,1,0:T(8,128)(2,1)}), bf16[128,128,256]{2,1,0:T(8,128)(2,1)}, u32[]{:S(2)}, u32[]{:S(2)}) %all-to-all-start) | async-done | bytes 8388640 | tf_op jit(solution)/shard_map/all_to_all | solution.py:302
  261.9 11.3 %rand_attend.1 = bf16[64,128,128]{2,1,0:T(8,128)(2,1)S(1)} custom-call(s32[128]{0:T(128)S(1)} %multiply_add_fusion.1.slot_ref, s32[32]{0:T(128)S(1)} %reshape.218.count_ref, s32[32]{0:T(128)S(1)} %select_reduce_fusion.2.target_ref, bf16[1024,512]{1,0:T(8,128)(2,1)S(1)} %fusion.2.q_ref, f32[32,128,128]{2,1,0:T(8,128)S(1)} %get-tuple-element.28.acc_ref, ...), custom_call_target="tpu_custom_call" | custom-call | tf_op jit(solution)/shard_map/rand_attend/pallas_call | solution.py:196
  273.2 1.3 copy-done.2
  274.5 5.9 %all-to-all-start.1 = ((bf16[64,128,128]{2,1,0:T(8,128)(2,1)}), bf16[64,128,128]{2,1,0:T(8,128)(2,1)S(1)}, u32[]{:S(2)}, u32[]{:S(2)}) async-start(bf16[64,128,128]{2,1,0:T(8,128)(2,1)} %copy-done.2), calls=%async_computation.1 | async-start | bytes 4194304 | tf_op jit(solution)/shard_map/all_to_all | solution.py:317
  280.4 0.1 and_select_fusion.5.index_ref
  280.5 51.2 %all-to-all-done.1.in_ref = bf16[64,128,128]{2,1,0:T(8,128)(2,1)S(1)} async-done(((bf16[64,128,128]{2,1,0:T(8,128)(2,1)}), bf16[64,128,128]{2,1,0:T(8,128)(2,1)S(1)}, u32[]{:S(2)}, u32[]{:S(2)}) %all-to-all-start.1) | async-done | bytes 2097184 | tf_op jit(solution)/shard_map/all_to_all | solution.py:317
  331.6 1.8 take_tiles.1
  (61 shorter events, 0.4 us)
Async XLA Ops:
  0.0 76.3 %copy-start = (s32[4,512]{1,0:T(4,128)S(1)}, s32[4,512]{1,0:T(4,128)}, u32[]{:S(2)}) copy-start(s32[4,512]{1,0:T(4,128)} %param.9) | copy-start | bytes 24580
  0.9 8.3 %collective-permute-start.2 = (bf16[128,512]{1,0:T(8,128)(2,1)S(1)}, bf16[128,512]{1,0:T(8,128)(2,1)S(1)}, u32[]{:S(2)}, u32[]{:S(2)}) collective-permute-start(bf16[128,512]{1,0:T(8,128)(2,1)S(1)} %slice_select_fusion), channel_id=1, source_target_pairs={{0,192},{1,193},{2,194},{3,195}} | collective-permute-start | bytes 393224 | tf_op jit(solution)/shard_map/ppermute | solution.py:269
  1.6 7.6 %collective-permute-start.1 = (bf16[128,512]{1,0:T(8,128)(2,1)S(1)}, bf16[128,512]{1,0:T(8,128)(2,1)S(1)}, u32[]{:S(2)}, u32[]{:S(2)}) collective-permute-start(bf16[128,512]{1,0:T(8,128)(2,1)S(1)} %slice_select_fusion), channel_id=1, source_target_pairs={{0,128},{1,129},{2,130},{3,131}} | collective-permute-start | bytes 393224 | tf_op jit(solution)/shard_map/ppermute | solution.py:269
  2.3 7.0 %collective-permute-start = (bf16[128,512]{1,0:T(8,128)(2,1)S(1)}, bf16[128,512]{1,0:T(8,128)(2,1)}, u32[]{:S(2)}, u32[]{:S(2)}) collective-permute-start(bf16[128,512]{1,0:T(8,128)(2,1)S(1)} %slice_select_fusion), channel_id=1, source_target_pairs={{0,64},{1,65},{2,66},{3,67}} | collective-permute-start | bytes 393224 | tf_op jit(solution)/shard_map/ppermute | solution.py:269
  3.6 29.3 %collective-permute-start.9 = (bf16[1024,512]{1,0:T(8,128)(2,1)}, bf16[1024,512]{1,0:T(8,128)(2,1)S(1)}, u32[]{:S(2)}, u32[]{:S(2)}) collective-permute-start(bf16[1024,512]{1,0:T(8,128)(2,1)} %param.5), channel_id=1, source_target_pairs={{0,1},{1,2},{2,3},{3,0},{4,5},{5,6},{6,7},{7,4},{8,9},{9,10},{10,1... | collective-permute-start | bytes 3145736 | tf_op jit(solution)/shard_map/ppermute | solution.py:277
  5.7 27.4 %collective-permute-start.10 = (bf16[1024,512]{1,0:T(8,128)(2,1)}, bf16[1024,512]{1,0:T(8,128)(2,1)}, u32[]{:S(2)}, u32[]{:S(2)}) collective-permute-start(bf16[1024,512]{1,0:T(8,128)(2,1)} %param.5), channel_id=1, source_target_pairs={{1,0},{2,1},{3,2},{0,3},{5,4},{6,5},{7,6},{4,7},{9,8},{10,9},{11,1... | collective-permute-start | bytes 3145736 | tf_op jit(solution)/shard_map/ppermute | solution.py:278
  7.2 29.7 %slice-start = ((s8[6291456]{0:T(1024)(128)(4,1)}), s8[2097152]{0:T(1024)(128)(4,1)S(1)}, s32[]{:S(2)}) async-start(s8[6291456]{0:T(1024)(128)(4,1)} %bitcast.56), calls=%async_computation.2 | async-start | bytes 4194304
  10.3 3.8 %collective-permute-start.5 = (bf16[128,512]{1,0:T(8,128)(2,1)S(1)}, bf16[128,512]{1,0:T(8,128)(2,1)S(1)}, u32[]{:S(2)}, u32[]{:S(2)}) collective-permute-start(bf16[128,512]{1,0:T(8,128)(2,1)S(1)} %add_add_fusion.2), channel_id=1, source_target_pairs={{0,48},{64,112},{128,176},{192,240},{1,49},{65,113},{129,177},{193... | collective-permute-start | bytes 393224 | tf_op jit(solution)/shard_map/ppermute | solution.py:269
  11.0 3.1 collective-permute-start.4
  11.6 2.5 collective-permute-start.3
  14.1 2.7 collective-permute-start.8
  14.8 2.0 collective-permute-start.7
  15.5 14.4 %collective-permute-start.6 = (bf16[128,512]{1,0:T(8,128)(2,1)S(1)}, bf16[128,512]{1,0:T(8,128)(2,1)S(1)}, u32[]{:S(2)}, u32[]{:S(2)}) collective-permute-start(bf16[128,512]{1,0:T(8,128)(2,1)S(1)} %add_add_fusion.1), channel_id=1, source_target_pairs={{0,4},{16,20},{32,36},{48,52},{64,68},{80,84},{96,100},{112,116},{... | collective-permute-start | bytes 393224 | tf_op jit(solution)/shard_map/ppermute | solution.py:269
  29.9 6.9 %slice-start.1 = ((s8[6291456]{0:T(1024)(128)(4,1)}), s8[4194304]{0:T(1024)(128)(4,1)S(1)}, s32[]{:S(2)}) async-start(s8[6291456]{0:T(1024)(128)(4,1)} %bitcast.56), calls=%async_computation.3 | async-start | bytes 8388608
  32.9 14.3 %collective-permute-start.11 = (bf16[512,512]{1,0:T(8,128)(2,1)S(1)}, bf16[512,512]{1,0:T(8,128)(2,1)S(1)}, u32[]{:S(2)}, u32[]{:S(2)}) collective-permute-start(bf16[512,512]{1,0:T(8,128)(2,1)S(1)} %slice.29), channel_id=1, source_target_pairs={{0,1},{1,2},{2,3},{3,0},{4,5},{5,6},{6,7},{7,4},{8,9},{9,10},{10,1... | collective-permute-start | bytes 1572872 | tf_op jit(solution)/shard_map/ppermute | solution.py:282
  34.2 13.2 %collective-permute-start.12 = (bf16[512,512]{1,0:T(8,128)(2,1)S(1)}, bf16[512,512]{1,0:T(8,128)(2,1)S(1)}, u32[]{:S(2)}, u32[]{:S(2)}) collective-permute-start(bf16[512,512]{1,0:T(8,128)(2,1)S(1)} %slice.30), channel_id=1, source_target_pairs={{1,0},{2,1},{3,2},{0,3},{5,4},{6,5},{7,6},{4,7},{9,8},{10,9},{11,1... | collective-permute-start | bytes 1572872 | tf_op jit(solution)/shard_map/ppermute | solution.py:283
  47.3 1.6 copy-start.9
  47.4 1.5 copy-start.11
  48.1 1.0 copy-start.3
  49.1 5.2 %copy-start.5 = (bf16[512,1024]{1,0:T(8,128)(2,1)}, bf16[512,1024]{1,0:T(8,128)(2,1)S(1)}, u32[]{:S(2)}) copy-start(bf16[512,1024]{1,0:T(8,128)(2,1)S(1)} %fusion.1) | copy-start | bytes 3145732
  49.9 14.5 %collective-permute-start.13 = (bf16[128,1024]{1,0:T(8,128)(2,1)}, bf16[128,1024]{1,0:T(8,128)(2,1)S(1)}, u32[]{:S(2)}, u32[]{:S(2)}) collective-permute-start(bf16[128,1024]{1,0:T(8,128)(2,1)} %slice.32), channel_id=1, source_target_pairs={{0,4},{4,8},{8,12},{12,16},{16,20},{20,24},{24,28},{28,32},{32,36}... | collective-permute-start | bytes 786440 | tf_op jit(solution)/shard_map/ppermute | solution.py:296
  55.0 9.4 %collective-permute-start.14 = (bf16[128,1024]{1,0:T(8,128)(2,1)}, bf16[128,1024]{1,0:T(8,128)(2,1)S(1)}, u32[]{:S(2)}, u32[]{:S(2)}) collective-permute-start(bf16[128,1024]{1,0:T(8,128)(2,1)} %slice.33), channel_id=1, source_target_pairs={{4,0},{8,4},{12,8},{16,12},{20,16},{24,20},{28,24},{32,28},{36,32}... | collective-permute-start | bytes 786440 | tf_op jit(solution)/shard_map/ppermute | solution.py:297
  64.3 11.8 %copy-start.8 = (s32[4,64,8,4]{2,1,3,0:T(8,128)S(1)}, s32[4,64,8,4]{2,1,3,0:T(8,128)}, u32[]{:S(2)}) copy-start(s32[4,64,8,4]{2,1,3,0:T(8,128)} %reshape.216) | copy-start | bytes 98308
  64.3 12.7 %copy-start.13 = (s32[1,2048]{1,0:T(1,128)S(1)}, s32[1,2048]{1,0:T(1,128)}, u32[]{:S(2)}) copy-start(s32[1,2048]{1,0:T(1,128)} %param.7) | copy-start | bytes 24580
  64.3 12.9 %copy-start.7 = (bf16[1024,512]{1,0:T(8,128)(2,1)S(1)}, bf16[1024,512]{1,0:T(8,128)(2,1)}, u32[]{:S(2)}) copy-start(bf16[1024,512]{1,0:T(8,128)(2,1)} %param.5) | copy-start | bytes 3145732
  64.4 197.5 %all-to-all-start = ((bf16[128,128,256]{2,1,0:T(8,128)(2,1)}), bf16[128,128,256]{2,1,0:T(8,128)(2,1)}, u32[]{:S(2)}, u32[]{:S(2)}) async-start(bf16[128,128,256]{2,1,0:T(8,128)(2,1)} %pack_tiles.1), calls=%async_computation | async-start | bytes 16777216 | tf_op jit(solution)/shard_map/all_to_all | solution.py:302
  77.3 9.7 %slice-start.2 = ((s8[6291456]{0:T(1024)(128)(4,1)}), s8[4194304]{0:T(1024)(128)(4,1)S(1)}, s32[]{:S(2)}) async-start(s8[6291456]{0:T(1024)(128)(4,1)} %bitcast.58), calls=%async_computation.4 | async-start | bytes 8388608
  79.2 6.0 %copy-start.10 = (bf16[512,512]{1,0:T(8,128)(2,1)S(1)}, bf16[512,512]{1,0:T(8,128)(2,1)}, u32[]{:S(2)}) copy-start(bf16[512,512]{1,0:T(8,128)(2,1)} %copy-done.9) | copy-start | bytes 1572868
  79.2 6.0 %copy-start.12 = (bf16[512,512]{1,0:T(8,128)(2,1)S(1)}, bf16[512,512]{1,0:T(8,128)(2,1)}, u32[]{:S(2)}) copy-start(bf16[512,512]{1,0:T(8,128)(2,1)} %copy-done.11) | copy-start | bytes 1572868
  79.2 7.8 %slice-start.3 = ((s8[6291456]{0:T(1024)(128)(4,1)}), s8[2097152]{0:T(1024)(128)(4,1)S(1)}, s32[]{:S(2)}) async-start(s8[6291456]{0:T(1024)(128)(4,1)} %bitcast.58), calls=%async_computation.5 | async-start | bytes 4194304
  81.1 8.4 %collective-permute-start.17 = (bf16[128,512]{1,0:T(8,128)(2,1)S(1)}, bf16[128,512]{1,0:T(8,128)(2,1)S(1)}, u32[]{:S(2)}, u32[]{:S(2)}) collective-permute-start(bf16[128,512]{1,0:T(8,128)(2,1)S(1)} %add_add_fusion), channel_id=1, source_target_pairs={{0,2},{1,3},{2,0},{3,1},{4,6},{5,7},{6,4},{7,5},{8,10},{9,11},{10,... | collective-permute-start | bytes 393224 | tf_op jit(solution)/shard_map/ppermute | solution.py:306
  83.4 7.6 %collective-permute-start.16 = (bf16[128,512]{1,0:T(8,128)(2,1)S(1)}, bf16[128,512]{1,0:T(8,128)(2,1)S(1)}, u32[]{:S(2)}, u32[]{:S(2)}) collective-permute-start(bf16[128,512]{1,0:T(8,128)(2,1)S(1)} %add_add_fusion), channel_id=1, source_target_pairs={{1,0},{2,1},{3,2},{0,3},{5,4},{6,5},{7,6},{4,7},{9,8},{10,9},{11,1... | collective-permute-start | bytes 393224 | tf_op jit(solution)/shard_map/ppermute | solution.py:305
  84.7 6.7 %collective-permute-start.15 = (bf16[128,512]{1,0:T(8,128)(2,1)S(1)}, bf16[128,512]{1,0:T(8,128)(2,1)S(1)}, u32[]{:S(2)}, u32[]{:S(2)}) collective-permute-start(bf16[128,512]{1,0:T(8,128)(2,1)S(1)} %add_add_fusion), channel_id=1, source_target_pairs={{0,1},{1,2},{2,3},{3,0},{4,5},{5,6},{6,7},{7,4},{8,9},{9,10},{10,1... | collective-permute-start | bytes 393224 | tf_op jit(solution)/shard_map/ppermute | solution.py:304
  87.0 2.2 copy-start.4
  87.0 2.2 copy-start.6
  261.9 71.6 %copy-start.1 = (s32[4,512]{1,0:T(4,128)S(1)}, s32[4,512]{1,0:T(4,128)}, u32[]{:S(2)}) copy-start(s32[4,512]{1,0:T(4,128)} %param.9) | copy-start | bytes 24580
  273.1 1.4 copy-start.2
  274.5 57.1 %all-to-all-start.1 = ((bf16[64,128,128]{2,1,0:T(8,128)(2,1)}), bf16[64,128,128]{2,1,0:T(8,128)(2,1)S(1)}, u32[]{:S(2)}, u32[]{:S(2)}) async-start(bf16[64,128,128]{2,1,0:T(8,128)(2,1)} %copy-done.2), calls=%async_computation.1 | async-start | bytes 4194304 | tf_op jit(solution)/shard_map/all_to_all | solution.py:317

commit v6 on v5

--- a/solution.py
+++ b/solution.py
@@ -25,16 +25,17 @@
     return pltpu.CompilerParams(vmem_limit_bytes=VMEM_BYTES)
 
 
-def pack_tiles(index, pair, slots, rows, heads, blk, hd):
+def pack_tiles(index, halves, slots, rows, heads, blk, hd):
     width = heads * hd
 
-    def kernel(index_ref, pair_ref, out_ref, tiles, sems):
+    def kernel(index_ref, top_ref, bottom_ref, out_ref, tiles, sems):
         def copy(s):
             return pltpu.make_async_copy(tiles.at[index_ref[s]], out_ref.at[s], sems.at[s])
 
         for e in range(heads):
             for r in range(rows):
-                at = slice(r * blk, (r + 1) * blk)
+                pair_ref, place = (top_ref, r) if r < rows // 2 else (bottom_ref, r - rows // 2)
+                at = slice(place * blk, (place + 1) * blk)
                 tiles[e * rows + r, :, :hd] = pair_ref[at, e * hd : (e + 1) * hd]
                 tiles[e * rows + r, :, hd:] = pair_ref[at, width + e * hd : width + (e + 1) * hd].T
         for s in range(slots):
@@ -48,7 +49,7 @@
         grid_spec=pltpu.PrefetchScalarGridSpec(
             num_scalar_prefetch=1,
             grid=(1,),
-            in_specs=[pl.BlockSpec(memory_space=pltpu.VMEM)],
+            in_specs=[pl.BlockSpec(memory_space=pltpu.VMEM)] * 2,
             out_specs=pl.BlockSpec(memory_space=pl.ANY),
             scratch_shapes=[
                 pltpu.VMEM((rows * heads, blk, 2 * hd), BF),
@@ -57,7 +58,7 @@
         ),
         compiler_params=params(),
         name="pack_tiles",
-    )(index, pair)
+    )(index, *halves)
 
 
 def take_tiles(index, tiles):
@@ -195,12 +196,12 @@
     anywhere = pl.BlockSpec(memory_space=pl.ANY)
     return pl.pallas_call(
         kernel,
-        out_shape=jax.ShapeDtypeStruct((peers, blk, hd), BF),
+        out_shape=pltpu.HBM((peers, blk, hd), BF),
         grid_spec=pltpu.PrefetchScalarGridSpec(
             num_scalar_prefetch=3,
             grid=(1,),
             in_specs=[vmem, vmem, vmem, anywhere],
-            out_specs=anywhere,
+            out_specs=pl.BlockSpec(memory_space=pltpu.HBM),
             scratch_shapes=[
                 pltpu.VMEM((slots, blk, 2 * hd), BF),
                 pltpu.VMEM((items, blk, hd), BF),
@@ -281,21 +282,15 @@
     zero = spread(spread(spread(zero, peers // 4), peers // 16), peers // 64)
     far_top = lax.ppermute(from_low[:middle], "head", onward)
     far_bottom = lax.ppermute(from_high[middle:], "head", backward)
-    own, zero = lax.optimization_barrier((tokens, zero))
+    own, from_low = lax.optimization_barrier((tokens, from_low))
     total = dot(own, w_pair(0)) + dot(from_low, w_pair(3)) + dot(from_high, w_pair(1))
-    far_top, far_bottom, zero = lax.optimization_barrier((far_top, far_bottom, zero))
-    pair = jnp.concatenate(
-        [
-            (total[:middle] + dot(far_top, w_pair(2))).astype(BF),
-            (total[middle:] + dot(far_bottom, w_pair(2))).astype(BF),
-        ],
-        axis=0,
-    )
+    top = (total[:middle] + dot(far_top, w_pair(2))).astype(BF)
+    bottom = (total[middle:] + dot(far_bottom, w_pair(2))).astype(BF)
     up = [(i, i + 1) for i in range(peers - 1)]
     down = [(b, a) for a, b in up]
-    before = lax.ppermute(pair[-blk:], "seq", up)
-    after = lax.ppermute(pair[:blk], "seq", down)
-    sent = pack_tiles(send_tile, pair, 2 * peers, rows, heads, blk, hd)
+    before = lax.ppermute(bottom[-blk:], "seq", up)
+    after = lax.ppermute(top[:blk], "seq", down)
+    sent = pack_tiles(send_tile, (top, bottom), 2 * peers, rows, heads, blk, hd)
     sent, before, after, far_top, far_bottom, zero = lax.optimization_barrier(
         (sent, before, after, far_top, far_bottom, zero)
     )
@@ -304,7 +299,7 @@
     zero_low = lax.ppermute(zero, "head", onward)
     zero_high = lax.ppermute(zero, "head", backward)
     zero_far = lax.ppermute(zero, "head", across)
-    around = jnp.concatenate([before, pair, after], axis=0)
+    around = jnp.concatenate([before, top, bottom, after], axis=0)
     far = jnp.concatenate([far_top, far_bottom], axis=0)
     query = dot(far, w_query(2)) + dot(tokens, w_query(0))
     query = (query + dot(from_low, w_query(3)) + dot(from_high, w_query(1))).astype(BF)

time: 334 us -> 327 us (0.979)
  waiting for transfers between devices: 233 us -> 220 us
  starting transfers between devices: 41.6 us -> 50.6 us
    ppermute x9, waiting for transfers between devices: 13.1 us -> 0.02 us  [spread(): lax.ppermute(block, 'seq', [(h, h + k * stride) for h in holders])]
    ppermute x1, waiting for transfers between devices: 0.01 us -> 7.01 us  [local(): from_low = lax.ppermute(tokens, 'head', onward)]
    ppermute x1, waiting for transfers between devices: 6.68 us -> 0.01 us  [local(): far_top = lax.ppermute(from_low[:middle], 'head', onward)]
    ppermute x2, starting transfers between devices: 6.25 us -> 12.4 us  [the longest x1 10.5 us: local(): before = lax.ppermute(bottom[-blk:], 'seq', up)]
  transfers between devices with their start and end apart: 20 -> 20, of which waited for: 6 -> 5; matrix products, arithmetic and copies ran while one was open for 8% -> 8% of each run, Pallas kernels for 4% -> 5%
where the time goes in v6:
time: 327 us; the launch traced here: 326 us
  waiting for transfers between devices  220 us (67%)
  starting transfers between devices  50.6 us (15%)
  Pallas kernels  27 us (8%)
  matrix products  14.3 us (4%)
  other arithmetic  6.97 us (2%)
  local copies, waits for them, and re-layouts  5.86 us (2%)
    all_to_all x1, waiting for transfers between devices, local(): tiles = lax.all_to_all(sent, 'seq', split_axis=0, concat_axis=0, tiled=True)  159 us
    all_to_all x1, waiting for transfers between devices, local(): back = lax.all_to_all(done, 'seq', split_axis=0, concat_axis=0, tiled=True)  51.2 us
    dot_general x13, matrix products, dot(): return jnp.dot(a, b, preferred_element_type=F32)  14.3 us
    all_to_all x1, starting transfers between devices, local(): tiles = lax.all_to_all(sent, 'seq', split_axis=0, concat_axis=0, tiled=True)  13.1 us
    pallas_call x1, Pallas kernels, rand_attend(): pl.pallas_call(kernel, out_shape=pltpu.HBM((peers, blk, hd), BF), grid_sp...  10.5 us
    ppermute x1, starting transfers between devices, local(): before = lax.ppermute(bottom[-blk:], 'seq', up)  10.5 us
    pallas_call x1, Pallas kernels, near_attend(): pl.pallas_call(kernel, out_shape=(jax.ShapeDtypeStruct((rows * heads, hd,...  9.37 us
    ppermute x9, starting transfers between devices, spread(): lax.ppermute(block, 'seq', [(h, h + k * stride) for h in holders])  8.2 us
  transfers between devices with their start and end apart: 20, of which 5 were waited for; matrix products, arithmetic and copies ran while one was open for 8% of the time, Pallas kernels for 5%

profile of v6, /device:TPU:1, one launch (start us, length us, event | category | flops | bytes accessed | tf_op | source)
XLA Modules:
  0.0 325.8 jit_solution(11806608654971683556)
XLA Ops:
  0.0 2.1 collective-permute-start
  2.1 1.5 collective-permute-start.1
  3.7 0.9 slice_select_fusion
  4.6 0.7 collective-permute-start.8
  5.3 0.7 collective-permute-start.7
  6.0 1.3 collective-permute-start.6
  7.3 1.9 reshape.216
  9.2 1.8 select_reduce_fusion.1
  11.0 1.0 add_add_fusion.2
  12.0 0.7 collective-permute-start.11
  12.7 0.7 collective-permute-start.10
  13.3 0.7 collective-permute-start.9
  14.1 0.8 collective-permute-start.14
  14.9 1.5 collective-permute-start.13
  16.4 1.3 collective-permute-start.12
  17.7 7.0 %collective-permute-done = bf16[1024,512]{1,0:T(8,128)(2,1)S(1)} collective-permute-done((bf16[1024,512]{1,0:T(8,128)(2,1)}, bf16[1024,512]{1,0:T(8,128)(2,1)S(1)}, u32[]{:S(2)}, u32[]{:S(2)}) %collective-permute-start) | collective-permute-done | bytes 1048608 | tf_op jit(solution)/shard_map/ppermute | solution.py:278
  24.7 1.5 collective-permute-start.2
  26.3 1.8 collective-permute-start.3
  28.1 2.5 fusion.19
  30.6 1.3 fusion.16
  31.8 1.3 bitcast_add_fusion
  33.1 1.4 collective-permute-done.3
  34.5 0.7 fusion.bottom_ref
  35.2 0.7 slice.32
  35.9 10.5 %collective-permute-start.4 = (bf16[128,1024]{1,0:T(8,128)(2,1)}, bf16[128,1024]{1,0:T(8,128)(2,1)}, u32[]{:S(2)}, u32[]{:S(2)}) collective-permute-start(bf16[128,1024]{1,0:T(8,128)(2,1)} %slice.32), channel_id=1, source_target_pairs={{0,4},{4,8},{8,12},{12,16},{16,20},{20,24},{24,28},{28,32},{32,36}... | collective-permute-start | bytes 786440 | tf_op jit(solution)/shard_map/ppermute | solution.py:291
  46.4 0.7 fusion.1.top_ref
  47.2 0.1 copy-done.5
  47.2 0.7 slice.33
  48.0 1.9 collective-permute-start.5
  49.9 0.1 copy.23
  50.0 0.1 reshape.219.index_ref
  50.2 0.6 copy-done.9
  50.8 1.1 add_add_fusion
  51.9 5.4 %pack_tiles.1 = bf16[128,128,256]{2,1,0:T(8,128)(2,1)} custom-call(s32[128]{0:T(128)S(1)} %reshape.219.index_ref, bf16[512,1024]{1,0:T(8,128)(2,1)S(1)} %fusion.1.top_ref, bf16[512,1024]{1,0:T(8,128)(2,1)S(1)} %fusion.bottom_ref), custom_call_target="tpu_custom_call" | custom-call | tf_op jit(solution)/shard_map/pack_tiles/pallas_call | solution.py:46
  57.3 13.1 %all-to-all-start = ((bf16[128,128,256]{2,1,0:T(8,128)(2,1)}), bf16[128,128,256]{2,1,0:T(8,128)(2,1)}, u32[]{:S(2)}, u32[]{:S(2)}) async-start(bf16[128,128,256]{2,1,0:T(8,128)(2,1)} %pack_tiles.1), calls=%async_computation | async-start | bytes 16777216 | tf_op jit(solution)/shard_map/all_to_all | solution.py:297
  70.4 1.2 copy.21
  71.7 0.1 dynamic-slice_bitcast_fusion
  71.8 0.1 copy.22
  71.8 0.1 reshape.218.count_ref
  71.9 0.2 dynamic-slice_reduce_fusion
  72.1 0.1 add_convert_fusion.edge_ref
  72.2 0.2 convert_reduce_fusion
  72.4 0.2 select_reduce_fusion.2.target_ref
  72.6 2.2 fusion.30
  74.9 0.0 slice-start.1
  74.9 1.9 fusion.28
  76.8 2.1 collective-permute-start.17
  78.9 1.5 collective-permute-start.16
  80.4 0.5 collective-permute-start.15
  80.9 1.7 fusion.7
  82.7 0.8 fusion.2.q_ref
  83.4 1.3 pad_maximum_fusion.kv_ref
  84.8 0.3 fusion.21
  85.1 1.7 collective-permute-done.16
  86.8 0.3 fusion.11
  87.1 0.3 fusion.14
  87.4 0.3 fusion.6.first_ref
  87.7 9.4 %near_attend.1 = (f32[32,128,128]{2,1,0:T(8,128)S(1)}, f32[32,8,128]{2,1,0:T(8,128)S(1)}) custom-call(s32[2]{0:T(128)S(1)} %add_convert_fusion.edge_ref, bf16[1024,512]{1,0:T(8,128)(2,1)S(1)} %fusion.2.q_ref, bf16[1280,1024]{1,0:T(8,128)(2,1)S(1)} %pad_maximum_fusion.kv_ref, bf16[128,1024]{1,0:T(8,128)(2,1)S(1)} %fusion.6.first_ref), custom_call_target="tpu_custom_call" | custom-call | tf_op jit(solution)/shard_map/near_attend/pallas_call | solution.py:119
  97.1 159.1 %all-to-all-done.tiles_ref = bf16[128,128,256]{2,1,0:T(8,128)(2,1)} async-done(((bf16[128,128,256]{2,1,0:T(8,128)(2,1)}), bf16[128,128,256]{2,1,0:T(8,128)(2,1)}, u32[]{:S(2)}, u32[]{:S(2)}) %all-to-all-start) | async-done | bytes 8388640 | tf_op jit(solution)/shard_map/all_to_all | solution.py:297
  256.2 10.5 %rand_attend.1 = bf16[64,128,128]{2,1,0:T(8,128)(2,1)} custom-call(s32[128]{0:T(128)S(1)} %multiply_add_fusion.1.slot_ref, s32[32]{0:T(128)S(1)} %reshape.218.count_ref, s32[32]{0:T(128)S(1)} %select_reduce_fusion.2.target_ref, bf16[1024,512]{1,0:T(8,128)(2,1)S(1)} %fusion.2.q_ref, f32[32,128,128]{2,1,0:T(8,128)S(1)} %get-tuple-element.22.acc_ref, ...), custom_call_target="tpu_custom_call" | custom-call | tf_op jit(solution)/shard_map/rand_attend/pallas_call | solution.py:197
  266.7 5.9 %all-to-all-start.1 = ((bf16[64,128,128]{2,1,0:T(8,128)(2,1)}), bf16[64,128,128]{2,1,0:T(8,128)(2,1)S(1)}, u32[]{:S(2)}, u32[]{:S(2)}) async-start(bf16[64,128,128]{2,1,0:T(8,128)(2,1)} %rand_attend.1), calls=%async_computation.1 | async-start | bytes 4194304 | tf_op jit(solution)/shard_map/all_to_all | solution.py:312
  272.6 0.1 and_select_fusion.5.index_ref
  272.7 51.2 %all-to-all-done.1.in_ref = bf16[64,128,128]{2,1,0:T(8,128)(2,1)S(1)} async-done(((bf16[64,128,128]{2,1,0:T(8,128)(2,1)}), bf16[64,128,128]{2,1,0:T(8,128)(2,1)S(1)}, u32[]{:S(2)}, u32[]{:S(2)}) %all-to-all-start.1) | async-done | bytes 2097184 | tf_op jit(solution)/shard_map/all_to_all | solution.py:312
  323.9 1.8 take_tiles.1
  (49 shorter events, 0.3 us)
Async XLA Ops:
  0.0 71.7 %copy-start = (s32[4,512]{1,0:T(4,128)S(1)}, s32[4,512]{1,0:T(4,128)}, u32[]{:S(2)}) copy-start(s32[4,512]{1,0:T(4,128)} %param.9) | copy-start | bytes 24580
  0.0 28.1 %copy-start.2 = (bf16[1024,512]{1,0:T(8,128)(2,1)S(1)}, bf16[1024,512]{1,0:T(8,128)(2,1)}, u32[]{:S(2)}) copy-start(bf16[1024,512]{1,0:T(8,128)(2,1)} %param.5) | copy-start | bytes 3145732
  0.0 24.7 %collective-permute-start = (bf16[1024,512]{1,0:T(8,128)(2,1)}, bf16[1024,512]{1,0:T(8,128)(2,1)S(1)}, u32[]{:S(2)}, u32[]{:S(2)}) collective-permute-start(bf16[1024,512]{1,0:T(8,128)(2,1)} %param.5), channel_id=1, source_target_pairs={{0,1},{1,2},{2,3},{3,0},{4,5},{5,6},{6,7},{7,4},{8,9},{9,10},{10,1... | collective-permute-start | bytes 3145736 | tf_op jit(solution)/shard_map/ppermute | solution.py:278
  2.1 24.1 %collective-permute-start.1 = (bf16[1024,512]{1,0:T(8,128)(2,1)}, bf16[1024,512]{1,0:T(8,128)(2,1)S(1)}, u32[]{:S(2)}, u32[]{:S(2)}) collective-permute-start(bf16[1024,512]{1,0:T(8,128)(2,1)} %param.5), channel_id=1, source_target_pairs={{1,0},{2,1},{3,2},{0,3},{5,4},{6,5},{7,6},{4,7},{9,8},{10,9},{11,1... | collective-permute-start | bytes 3145736 | tf_op jit(solution)/shard_map/ppermute | solution.py:279
  4.6 6.3 %collective-permute-start.8 = (bf16[128,512]{1,0:T(8,128)(2,1)S(1)}, bf16[128,512]{1,0:T(8,128)(2,1)S(1)}, u32[]{:S(2)}, u32[]{:S(2)}) collective-permute-start(bf16[128,512]{1,0:T(8,128)(2,1)S(1)} %slice_select_fusion), channel_id=1, source_target_pairs={{0,192},{1,193},{2,194},{3,195}} | collective-permute-start | bytes 393224 | tf_op jit(solution)/shard_map/ppermute | solution.py:270
  5.3 5.7 %collective-permute-start.7 = (bf16[128,512]{1,0:T(8,128)(2,1)S(1)}, bf16[128,512]{1,0:T(8,128)(2,1)S(1)}, u32[]{:S(2)}, u32[]{:S(2)}) collective-permute-start(bf16[128,512]{1,0:T(8,128)(2,1)S(1)} %slice_select_fusion), channel_id=1, source_target_pairs={{0,128},{1,129},{2,130},{3,131}} | collective-permute-start | bytes 393224 | tf_op jit(solution)/shard_map/ppermute | solution.py:270
  6.0 5.0 %collective-permute-start.6 = (bf16[128,512]{1,0:T(8,128)(2,1)S(1)}, bf16[128,512]{1,0:T(8,128)(2,1)}, u32[]{:S(2)}, u32[]{:S(2)}) collective-permute-start(bf16[128,512]{1,0:T(8,128)(2,1)S(1)} %slice_select_fusion), channel_id=1, source_target_pairs={{0,64},{1,65},{2,66},{3,67}} | collective-permute-start | bytes 393224 | tf_op jit(solution)/shard_map/ppermute | solution.py:270
  12.0 2.0 collective-permute-start.11
  12.7 1.4 collective-permute-start.10
  13.3 0.7 collective-permute-start.9
  14.1 16.5 %copy-start.1 = (bf16[2048,1536]{1,0:T(8,128)(2,1)S(1)}, bf16[2048,1536]{1,0:T(8,128)(2,1)}, u32[]{:S(2)}) copy-start(bf16[2048,1536]{1,0:T(8,128)(2,1)} %param.6) | copy-start | bytes 18874372
  14.1 36.0 %collective-permute-start.14 = (bf16[128,512]{1,0:T(8,128)(2,1)S(1)}, bf16[128,512]{1,0:T(8,128)(2,1)S(1)}, u32[]{:S(2)}, u32[]{:S(2)}) collective-permute-start(bf16[128,512]{1,0:T(8,128)(2,1)S(1)} %add_add_fusion.1), channel_id=1, source_target_pairs={{0,12},{16,28},{32,44},{48,60},{64,76},{80,92},{96,108},{112,124},... | collective-permute-start | bytes 393224 | tf_op jit(solution)/shard_map/ppermute | solution.py:270
  14.9 35.2 %collective-permute-start.13 = (bf16[128,512]{1,0:T(8,128)(2,1)S(1)}, bf16[128,512]{1,0:T(8,128)(2,1)}, u32[]{:S(2)}, u32[]{:S(2)}) collective-permute-start(bf16[128,512]{1,0:T(8,128)(2,1)S(1)} %add_add_fusion.1), channel_id=1, source_target_pairs={{0,8},{16,24},{32,40},{48,56},{64,72},{80,88},{96,104},{112,120},{... | collective-permute-start | bytes 393224 | tf_op jit(solution)/shard_map/ppermute | solution.py:270
  16.4 34.4 %collective-permute-start.12 = (bf16[128,512]{1,0:T(8,128)(2,1)S(1)}, bf16[128,512]{1,0:T(8,128)(2,1)}, u32[]{:S(2)}, u32[]{:S(2)}) collective-permute-start(bf16[128,512]{1,0:T(8,128)(2,1)S(1)} %add_add_fusion.1), channel_id=1, source_target_pairs={{0,4},{16,20},{32,36},{48,52},{64,68},{80,84},{96,100},{112,116},{... | collective-permute-start | bytes 393224 | tf_op jit(solution)/shard_map/ppermute | solution.py:270
  24.7 21.7 %collective-permute-start.2 = (bf16[512,512]{1,0:T(8,128)(2,1)S(1)}, bf16[512,512]{1,0:T(8,128)(2,1)S(1)}, u32[]{:S(2)}, u32[]{:S(2)}) collective-permute-start(bf16[512,512]{1,0:T(8,128)(2,1)S(1)} %slice.29), channel_id=1, source_target_pairs={{0,1},{1,2},{2,3},{3,0},{4,5},{5,6},{6,7},{7,4},{8,9},{9,10},{10,1... | collective-permute-start | bytes 1572872 | tf_op jit(solution)/shard_map/ppermute | solution.py:283
  26.3 5.6 %copy-start.3 = (bf16[1024,512]{1,0:T(8,128)(2,1)}, bf16[1024,512]{1,0:T(8,128)(2,1)S(1)}, u32[]{:S(2)}) copy-start(bf16[1024,512]{1,0:T(8,128)(2,1)S(1)} %collective-permute-done.1) | copy-start | bytes 3145732
  26.3 8.2 %collective-permute-start.3 = (bf16[512,512]{1,0:T(8,128)(2,1)S(1)}, bf16[512,512]{1,0:T(8,128)(2,1)S(1)}, u32[]{:S(2)}, u32[]{:S(2)}) collective-permute-start(bf16[512,512]{1,0:T(8,128)(2,1)S(1)} %slice.31), channel_id=1, source_target_pairs={{1,0},{2,1},{3,2},{0,3},{5,4},{6,5},{7,6},{4,7},{9,8},{10,9},{11,1... | collective-permute-start | bytes 1572872 | tf_op jit(solution)/shard_map/ppermute | solution.py:284
  34.5 12.7 %copy-start.7 = (bf16[512,512]{1,0:T(8,128)(2,1)}, bf16[512,512]{1,0:T(8,128)(2,1)S(1)}, u32[]{:S(2)}) copy-start(bf16[512,512]{1,0:T(8,128)(2,1)S(1)} %collective-permute-done.3) | copy-start | bytes 1572868
  35.9 21.4 %collective-permute-start.4 = (bf16[128,1024]{1,0:T(8,128)(2,1)}, bf16[128,1024]{1,0:T(8,128)(2,1)}, u32[]{:S(2)}, u32[]{:S(2)}) collective-permute-start(bf16[128,1024]{1,0:T(8,128)(2,1)} %slice.32), channel_id=1, source_target_pairs={{0,4},{4,8},{8,12},{12,16},{16,20},{20,24},{24,28},{28,32},{32,36}... | collective-permute-start | bytes 786440 | tf_op jit(solution)/shard_map/ppermute | solution.py:291
  46.4 0.8 copy-start.5
  48.0 9.3 %collective-permute-start.5 = (bf16[128,1024]{1,0:T(8,128)(2,1)}, bf16[128,1024]{1,0:T(8,128)(2,1)}, u32[]{:S(2)}, u32[]{:S(2)}) collective-permute-start(bf16[128,1024]{1,0:T(8,128)(2,1)} %slice.33), channel_id=1, source_target_pairs={{4,0},{8,4},{12,8},{16,12},{20,16},{24,20},{28,24},{32,28},{36,32}... | collective-permute-start | bytes 786440 | tf_op jit(solution)/shard_map/ppermute | solution.py:292
  50.1 0.6 copy-start.9
  57.3 15.1 %copy-start.10 = (s32[1,2048]{1,0:T(1,128)S(1)}, s32[1,2048]{1,0:T(1,128)}, u32[]{:S(2)}) copy-start(s32[1,2048]{1,0:T(1,128)} %param.7) | copy-start | bytes 24580
  57.3 198.9 %all-to-all-start = ((bf16[128,128,256]{2,1,0:T(8,128)(2,1)}), bf16[128,128,256]{2,1,0:T(8,128)(2,1)}, u32[]{:S(2)}, u32[]{:S(2)}) async-start(bf16[128,128,256]{2,1,0:T(8,128)(2,1)} %pack_tiles.1), calls=%async_computation | async-start | bytes 16777216 | tf_op jit(solution)/shard_map/all_to_all | solution.py:297
  72.6 10.0 %slice-start = ((s8[6291456]{0:T(1024)(128)(4,1)}), s8[4194304]{0:T(1024)(128)(4,1)S(1)}, s32[]{:S(2)}) async-start(s8[6291456]{0:T(1024)(128)(4,1)} %bitcast.54), calls=%async_computation.2 | async-start | bytes 8388608
  74.9 6.0 %copy-start.6 = (bf16[512,512]{1,0:T(8,128)(2,1)S(1)}, bf16[512,512]{1,0:T(8,128)(2,1)}, u32[]{:S(2)}) copy-start(bf16[512,512]{1,0:T(8,128)(2,1)} %copy-done.5) | copy-start | bytes 1572868
  74.9 6.0 %copy-start.8 = (bf16[512,512]{1,0:T(8,128)(2,1)S(1)}, bf16[512,512]{1,0:T(8,128)(2,1)}, u32[]{:S(2)}) copy-start(bf16[512,512]{1,0:T(8,128)(2,1)} %copy-done.7) | copy-start | bytes 1572868
  74.9 7.8 %slice-start.1 = ((s8[6291456]{0:T(1024)(128)(4,1)}), s8[2097152]{0:T(1024)(128)(4,1)S(1)}, s32[]{:S(2)}) async-start(s8[6291456]{0:T(1024)(128)(4,1)} %bitcast.54), calls=%async_computation.3 | async-start | bytes 4194304
  74.9 7.8 %copy-start.4 = (bf16[1024,512]{1,0:T(8,128)(2,1)S(1)}, bf16[1024,512]{1,0:T(8,128)(2,1)}, u32[]{:S(2)}) copy-start(bf16[1024,512]{1,0:T(8,128)(2,1)} %copy-done.3) | copy-start | bytes 3145732
  76.8 7.9 %collective-permute-start.17 = (bf16[128,512]{1,0:T(8,128)(2,1)S(1)}, bf16[128,512]{1,0:T(8,128)(2,1)S(1)}, u32[]{:S(2)}, u32[]{:S(2)}) collective-permute-start(bf16[128,512]{1,0:T(8,128)(2,1)S(1)} %add_add_fusion), channel_id=1, source_target_pairs={{0,2},{1,3},{2,0},{3,1},{4,6},{5,7},{6,4},{7,5},{8,10},{9,11},{10,... | collective-permute-start | bytes 393224 | tf_op jit(solution)/shard_map/ppermute | solution.py:301
  78.9 7.8 %collective-permute-start.16 = (bf16[128,512]{1,0:T(8,128)(2,1)S(1)}, bf16[128,512]{1,0:T(8,128)(2,1)S(1)}, u32[]{:S(2)}, u32[]{:S(2)}) collective-permute-start(bf16[128,512]{1,0:T(8,128)(2,1)S(1)} %add_add_fusion), channel_id=1, source_target_pairs={{1,0},{2,1},{3,2},{0,3},{5,4},{6,5},{7,6},{4,7},{9,8},{10,9},{11,1... | collective-permute-start | bytes 393224 | tf_op jit(solution)/shard_map/ppermute | solution.py:300
  80.4 6.7 %collective-permute-start.15 = (bf16[128,512]{1,0:T(8,128)(2,1)S(1)}, bf16[128,512]{1,0:T(8,128)(2,1)S(1)}, u32[]{:S(2)}, u32[]{:S(2)}) collective-permute-start(bf16[128,512]{1,0:T(8,128)(2,1)S(1)} %add_add_fusion), channel_id=1, source_target_pairs={{0,1},{1,2},{2,3},{3,0},{4,5},{5,6},{6,7},{7,4},{8,9},{9,10},{10,1... | collective-permute-start | bytes 393224 | tf_op jit(solution)/shard_map/ppermute | solution.py:299
  266.7 57.2 %all-to-all-start.1 = ((bf16[64,128,128]{2,1,0:T(8,128)(2,1)}), bf16[64,128,128]{2,1,0:T(8,128)(2,1)S(1)}, u32[]{:S(2)}, u32[]{:S(2)}) async-start(bf16[64,128,128]{2,1,0:T(8,128)(2,1)} %rand_attend.1), calls=%async_computation.1 | async-start | bytes 4194304 | tf_op jit(solution)/shard_map/all_to_all | solution.py:312

commit v7 on v6

--- a/solution.py
+++ b/solution.py
@@ -183,7 +183,7 @@
             ]
             summed = [acc_ref[first + e] * keep[e] + dot(values[e], expo[e].astype(BF)) for e in each]
             for e in each:
-                done[first + e] = (summed[e] / total[e]).T.astype(BF)
+                done[first + e] = (summed[e] * (1.0 / total[e])).T.astype(BF)
             for e in each:
                 deliver(first + e).start()
             return carry
@@ -264,12 +264,14 @@
     def w_query(shift):
         return weight(shift, 0, width)
 
-    def spread(block, stride):
+    def spread_parts(block, stride):
         holders = range(0, peers, 4 * stride)
-        got = [
+        return [
             lax.ppermute(block, "seq", [(h, h + k * stride) for h in holders]) for k in (1, 2, 3)
         ]
-        return block + got[0] + got[1] + got[2]
+
+    def spread(block, stride):
+        return sum(spread_parts(block, stride), block)
 
     onward = [(i, (i + 1) % groups) for i in range(groups)]
     backward = [(b, a) for a, b in onward]
@@ -279,7 +281,8 @@
     from_high = lax.ppermute(tokens, "head", backward)
     zero = tokens[:blk]
     zero = jnp.where(me == 0, zero, jnp.zeros_like(zero))
-    zero = spread(spread(spread(zero, peers // 4), peers // 16), peers // 64)
+    zero = spread(spread(zero, peers // 4), peers // 16)
+    zero = [zero, *spread_parts(zero, peers // 64)]
     far_top = lax.ppermute(from_low[:middle], "head", onward)
     far_bottom = lax.ppermute(from_high[middle:], "head", backward)
     own, from_low = lax.optimization_barrier((tokens, from_low))
@@ -296,6 +299,7 @@
     )
     tiles = lax.all_to_all(sent, "seq", split_axis=0, concat_axis=0, tiled=True)
 
+    zero = sum(zero[1:], zero[0])
     zero_low = lax.ppermute(zero, "head", onward)
     zero_high = lax.ppermute(zero, "head", backward)
     zero_far = lax.ppermute(zero, "head", across)

time: 327 us -> 325 us (level)
  transfers between devices with their start and end apart: 20 -> 20, of which waited for: 5 -> 6; matrix products, arithmetic and copies ran while one was open for 8% -> 8% of each run, Pallas kernels for 5% -> 5%
where the time goes in v7:
time: 325 us; the launch traced here: 324 us
  waiting for transfers between devices  219 us (67%)
  starting transfers between devices  51.2 us (16%)
  Pallas kernels  27 us (8%)
  matrix products  14.3 us (4%)
  other arithmetic  6.9 us (2%)
  local copies, waits for them, and re-layouts  5.24 us (2%)
    all_to_all x1, waiting for transfers between devices, local(): tiles = lax.all_to_all(sent, 'seq', split_axis=0, concat_axis=0, tiled=True)  158 us
    all_to_all x1, waiting for transfers between devices, local(): back = lax.all_to_all(done, 'seq', split_axis=0, concat_axis=0, tiled=True)  51.2 us
    dot_general x13, matrix products, dot(): return jnp.dot(a, b, preferred_element_type=F32)  14.3 us
    all_to_all x1, starting transfers between devices, local(): tiles = lax.all_to_all(sent, 'seq', split_axis=0, concat_axis=0, tiled=True)  12.8 us
    pallas_call x1, Pallas kernels, rand_attend(): pl.pallas_call(kernel, out_shape=pltpu.HBM((peers, blk, hd), BF), grid_sp...  10.4 us
    ppermute x1, starting transfers between devices, local(): before = lax.ppermute(bottom[-blk:], 'seq', up)  9.85 us
    pallas_call x1, Pallas kernels, near_attend(): pl.pallas_call(kernel, out_shape=(jax.ShapeDtypeStruct((rows * heads, hd,...  9.37 us
    ppermute x9, starting transfers between devices, spread_parts(): lax.ppermute(block, 'seq', [(h, h + k * stride) for h in holders])  8.97 us
  transfers between devices with their start and end apart: 20, of which 6 were waited for; matrix products, arithmetic and copies ran while one was open for 8% of the time, Pallas kernels for 5%

profile of v7, /device:TPU:1, one launch (start us, length us, event | category | flops | bytes accessed | tf_op | source)
XLA Modules:
  0.0 324.1 jit_solution(12807471051122282099)
XLA Ops:
  0.0 2.1 collective-permute-start
  2.1 1.5 collective-permute-start.1
  3.7 0.9 slice_select_fusion
  4.6 0.7 collective-permute-start.8
  5.3 0.7 collective-permute-start.7
  6.0 1.3 collective-permute-start.6
  7.3 1.9 reshape.216
  9.2 1.0 add_add_fusion.2
  10.2 0.7 collective-permute-start.11
  10.9 0.7 collective-permute-start.10
  11.6 0.7 collective-permute-start.9
  12.3 1.8 select_reduce_fusion.1
  14.1 1.6 collective-permute-start.12
  15.7 1.4 collective-permute-start.13
  17.1 1.3 collective-permute-start.14
  18.4 6.3 %collective-permute-done = bf16[1024,512]{1,0:T(8,128)(2,1)S(1)} collective-permute-done((bf16[1024,512]{1,0:T(8,128)(2,1)}, bf16[1024,512]{1,0:T(8,128)(2,1)S(1)}, u32[]{:S(2)}, u32[]{:S(2)}) %collective-permute-start) | collective-permute-done | bytes 1048608 | tf_op jit(solution)/shard_map/ppermute | solution.py:280
  24.7 1.5 collective-permute-start.2
  26.3 1.8 collective-permute-start.3
  28.1 2.5 fusion.17
  30.6 1.3 fusion.14
  31.8 1.3 bitcast_add_fusion
  33.1 2.0 collective-permute-done.3
  35.1 0.7 fusion.bottom_ref
  35.8 0.7 slice.32
  36.6 9.9 %collective-permute-start.4 = (bf16[128,1024]{1,0:T(8,128)(2,1)}, bf16[128,1024]{1,0:T(8,128)(2,1)}, u32[]{:S(2)}, u32[]{:S(2)}) collective-permute-start(bf16[128,1024]{1,0:T(8,128)(2,1)} %slice.32), channel_id=1, source_target_pairs={{0,4},{4,8},{8,12},{12,16},{16,20},{20,24},{24,28},{28,32},{32,36}... | collective-permute-start | bytes 786440 | tf_op jit(solution)/shard_map/ppermute | solution.py:294
  46.4 0.7 fusion.1.top_ref
  47.2 0.1 copy-done.5
  47.2 0.7 slice.33
  48.0 1.9 collective-permute-start.5
  49.9 0.1 copy.23
  50.0 0.1 reshape.219.index_ref
  50.2 5.4 %pack_tiles.1 = bf16[128,128,256]{2,1,0:T(8,128)(2,1)} custom-call(s32[128]{0:T(128)S(1)} %reshape.219.index_ref, bf16[512,1024]{1,0:T(8,128)(2,1)S(1)} %fusion.1.top_ref, bf16[512,1024]{1,0:T(8,128)(2,1)S(1)} %fusion.bottom_ref), custom_call_target="tpu_custom_call" | custom-call | tf_op jit(solution)/shard_map/pack_tiles/pallas_call | solution.py:46
  55.6 0.3 collective-permute-done.5
  56.0 12.8 %all-to-all-start = ((bf16[128,128,256]{2,1,0:T(8,128)(2,1)}), bf16[128,128,256]{2,1,0:T(8,128)(2,1)}, u32[]{:S(2)}, u32[]{:S(2)}) async-start(bf16[128,128,256]{2,1,0:T(8,128)(2,1)} %pack_tiles.1), calls=%async_computation | async-start | bytes 16777216 | tf_op jit(solution)/shard_map/all_to_all | solution.py:300
  68.8 1.2 copy.21
  70.0 0.1 dynamic-slice_bitcast_fusion
  70.1 0.1 copy.22
  70.2 0.1 reshape.218.count_ref
  70.2 0.2 dynamic-slice_reduce_fusion
  70.5 0.1 add_convert_fusion.edge_ref
  70.6 0.2 convert_reduce_fusion
  70.7 0.2 select_reduce_fusion.2.target_ref
  71.0 2.2 fusion.28
  73.2 0.0 slice-start.1
  73.2 1.9 fusion.26
  75.1 1.0 add_add_fusion
  76.2 2.1 collective-permute-start.17
  78.3 1.9 collective-permute-start.15
  80.2 0.7 collective-permute-start.16
  81.0 1.7 fusion.6
  82.8 0.8 fusion.2.q_ref
  83.5 1.3 pad_maximum_fusion.kv_ref
  84.8 0.6 collective-permute-done.15
  85.4 0.3 fusion.12
  85.7 0.3 convolution_add_fusion.1
  86.1 0.3 fusion.19
  86.4 0.3 fusion.5.first_ref
  86.7 9.4 %near_attend.1 = (f32[32,128,128]{2,1,0:T(8,128)S(1)}, f32[32,8,128]{2,1,0:T(8,128)S(1)}) custom-call(s32[2]{0:T(128)S(1)} %add_convert_fusion.edge_ref, bf16[1024,512]{1,0:T(8,128)(2,1)S(1)} %fusion.2.q_ref, bf16[1280,1024]{1,0:T(8,128)(2,1)S(1)} %pad_maximum_fusion.kv_ref, bf16[128,1024]{1,0:T(8,128)(2,1)S(1)} %fusion.5.first_ref), custom_call_target="tpu_custom_call" | custom-call | tf_op jit(solution)/shard_map/near_attend/pallas_call | solution.py:119
  96.1 158.4 %all-to-all-done.tiles_ref = bf16[128,128,256]{2,1,0:T(8,128)(2,1)} async-done(((bf16[128,128,256]{2,1,0:T(8,128)(2,1)}), bf16[128,128,256]{2,1,0:T(8,128)(2,1)}, u32[]{:S(2)}, u32[]{:S(2)}) %all-to-all-start) | async-done | bytes 8388640 | tf_op jit(solution)/shard_map/all_to_all | solution.py:300
  254.5 10.4 %rand_attend.1 = bf16[64,128,128]{2,1,0:T(8,128)(2,1)} custom-call(s32[128]{0:T(128)S(1)} %multiply_add_fusion.1.slot_ref, s32[32]{0:T(128)S(1)} %reshape.218.count_ref, s32[32]{0:T(128)S(1)} %select_reduce_fusion.2.target_ref, bf16[1024,512]{1,0:T(8,128)(2,1)S(1)} %fusion.2.q_ref, f32[32,128,128]{2,1,0:T(8,128)S(1)} %get-tuple-element.28.acc_ref, ...), custom_call_target="tpu_custom_call" | custom-call | tf_op jit(solution)/shard_map/rand_attend/pallas_call | solution.py:197
  265.0 5.9 %all-to-all-start.1 = ((bf16[64,128,128]{2,1,0:T(8,128)(2,1)}), bf16[64,128,128]{2,1,0:T(8,128)(2,1)S(1)}, u32[]{:S(2)}, u32[]{:S(2)}) async-start(bf16[64,128,128]{2,1,0:T(8,128)(2,1)} %rand_attend.1), calls=%async_computation.1 | async-start | bytes 4194304 | tf_op jit(solution)/shard_map/all_to_all | solution.py:316
  270.9 0.1 and_select_fusion.5.index_ref
  271.0 51.2 %all-to-all-done.1.in_ref = bf16[64,128,128]{2,1,0:T(8,128)(2,1)S(1)} async-done(((bf16[64,128,128]{2,1,0:T(8,128)(2,1)}), bf16[64,128,128]{2,1,0:T(8,128)(2,1)S(1)}, u32[]{:S(2)}, u32[]{:S(2)}) %all-to-all-start.1) | async-done | bytes 2097184 | tf_op jit(solution)/shard_map/all_to_all | solution.py:316
  322.1 1.8 take_tiles.1
  (47 shorter events, 0.3 us)
Async XLA Ops:
  0.0 70.0 %copy-start = (s32[4,512]{1,0:T(4,128)S(1)}, s32[4,512]{1,0:T(4,128)}, u32[]{:S(2)}) copy-start(s32[4,512]{1,0:T(4,128)} %param.9) | copy-start | bytes 24580
  0.0 28.1 %copy-start.2 = (bf16[1024,512]{1,0:T(8,128)(2,1)S(1)}, bf16[1024,512]{1,0:T(8,128)(2,1)}, u32[]{:S(2)}) copy-start(bf16[1024,512]{1,0:T(8,128)(2,1)} %param.5) | copy-start | bytes 3145732
  0.0 24.7 %collective-permute-start = (bf16[1024,512]{1,0:T(8,128)(2,1)}, bf16[1024,512]{1,0:T(8,128)(2,1)S(1)}, u32[]{:S(2)}, u32[]{:S(2)}) collective-permute-start(bf16[1024,512]{1,0:T(8,128)(2,1)} %param.5), channel_id=1, source_target_pairs={{0,1},{1,2},{2,3},{3,0},{4,5},{5,6},{6,7},{7,4},{8,9},{9,10},{10,1... | collective-permute-start | bytes 3145736 | tf_op jit(solution)/shard_map/ppermute | solution.py:280
  2.1 24.1 %collective-permute-start.1 = (bf16[1024,512]{1,0:T(8,128)(2,1)}, bf16[1024,512]{1,0:T(8,128)(2,1)S(1)}, u32[]{:S(2)}, u32[]{:S(2)}) collective-permute-start(bf16[1024,512]{1,0:T(8,128)(2,1)} %param.5), channel_id=1, source_target_pairs={{1,0},{2,1},{3,2},{0,3},{5,4},{6,5},{7,6},{4,7},{9,8},{10,9},{11,1... | collective-permute-start | bytes 3145736 | tf_op jit(solution)/shard_map/ppermute | solution.py:281
  4.6 4.6 %collective-permute-start.8 = (bf16[128,512]{1,0:T(8,128)(2,1)S(1)}, bf16[128,512]{1,0:T(8,128)(2,1)S(1)}, u32[]{:S(2)}, u32[]{:S(2)}) collective-permute-start(bf16[128,512]{1,0:T(8,128)(2,1)S(1)} %slice_select_fusion), channel_id=1, source_target_pairs={{0,192},{1,193},{2,194},{3,195}} | collective-permute-start | bytes 393224 | tf_op jit(solution)/shard_map/ppermute | solution.py:270
  5.3 3.9 %collective-permute-start.7 = (bf16[128,512]{1,0:T(8,128)(2,1)S(1)}, bf16[128,512]{1,0:T(8,128)(2,1)S(1)}, u32[]{:S(2)}, u32[]{:S(2)}) collective-permute-start(bf16[128,512]{1,0:T(8,128)(2,1)S(1)} %slice_select_fusion), channel_id=1, source_target_pairs={{0,128},{1,129},{2,130},{3,131}} | collective-permute-start | bytes 393224 | tf_op jit(solution)/shard_map/ppermute | solution.py:270
  6.0 3.2 collective-permute-start.6
  10.2 3.8 %collective-permute-start.11 = (bf16[128,512]{1,0:T(8,128)(2,1)S(1)}, bf16[128,512]{1,0:T(8,128)(2,1)S(1)}, u32[]{:S(2)}, u32[]{:S(2)}) collective-permute-start(bf16[128,512]{1,0:T(8,128)(2,1)S(1)} %add_add_fusion.2), channel_id=1, source_target_pairs={{0,48},{64,112},{128,176},{192,240},{1,49},{65,113},{129,177},{193... | collective-permute-start | bytes 393224 | tf_op jit(solution)/shard_map/ppermute | solution.py:270
  10.9 3.1 collective-permute-start.10
  11.6 2.5 collective-permute-start.9
  14.1 16.5 %copy-start.1 = (bf16[2048,1536]{1,0:T(8,128)(2,1)S(1)}, bf16[2048,1536]{1,0:T(8,128)(2,1)}, u32[]{:S(2)}) copy-start(bf16[2048,1536]{1,0:T(8,128)(2,1)} %param.6) | copy-start | bytes 18874372
  14.1 41.5 %collective-permute-start.12 = (bf16[128,512]{1,0:T(8,128)(2,1)S(1)}, bf16[128,512]{1,0:T(8,128)(2,1)S(1)}, u32[]{:S(2)}, u32[]{:S(2)}) collective-permute-start(bf16[128,512]{1,0:T(8,128)(2,1)S(1)} %add_add_fusion.1), channel_id=1, source_target_pairs={{0,4},{16,20},{32,36},{48,52},{64,68},{80,84},{96,100},{112,116},{... | collective-permute-start | bytes 393224 | tf_op jit(solution)/shard_map/ppermute | solution.py:270
  15.7 39.9 %collective-permute-start.13 = (bf16[128,512]{1,0:T(8,128)(2,1)S(1)}, bf16[128,512]{1,0:T(8,128)(2,1)}, u32[]{:S(2)}, u32[]{:S(2)}) collective-permute-start(bf16[128,512]{1,0:T(8,128)(2,1)S(1)} %add_add_fusion.1), channel_id=1, source_target_pairs={{0,8},{16,24},{32,40},{48,56},{64,72},{80,88},{96,104},{112,120},{... | collective-permute-start | bytes 393224 | tf_op jit(solution)/shard_map/ppermute | solution.py:270
  17.1 38.5 %collective-permute-start.14 = (bf16[128,512]{1,0:T(8,128)(2,1)S(1)}, bf16[128,512]{1,0:T(8,128)(2,1)}, u32[]{:S(2)}, u32[]{:S(2)}) collective-permute-start(bf16[128,512]{1,0:T(8,128)(2,1)S(1)} %add_add_fusion.1), channel_id=1, source_target_pairs={{0,12},{16,28},{32,44},{48,60},{64,76},{80,92},{96,108},{112,124},... | collective-permute-start | bytes 393224 | tf_op jit(solution)/shard_map/ppermute | solution.py:270
  24.7 21.7 %collective-permute-start.2 = (bf16[512,512]{1,0:T(8,128)(2,1)S(1)}, bf16[512,512]{1,0:T(8,128)(2,1)S(1)}, u32[]{:S(2)}, u32[]{:S(2)}) collective-permute-start(bf16[512,512]{1,0:T(8,128)(2,1)S(1)} %slice.29), channel_id=1, source_target_pairs={{0,1},{1,2},{2,3},{3,0},{4,5},{5,6},{6,7},{7,4},{8,9},{9,10},{10,1... | collective-permute-start | bytes 1572872 | tf_op jit(solution)/shard_map/ppermute | solution.py:286
  26.3 5.6 %copy-start.3 = (bf16[1024,512]{1,0:T(8,128)(2,1)}, bf16[1024,512]{1,0:T(8,128)(2,1)S(1)}, u32[]{:S(2)}) copy-start(bf16[1024,512]{1,0:T(8,128)(2,1)S(1)} %collective-permute-done.1) | copy-start | bytes 3145732
  26.3 8.8 %collective-permute-start.3 = (bf16[512,512]{1,0:T(8,128)(2,1)S(1)}, bf16[512,512]{1,0:T(8,128)(2,1)S(1)}, u32[]{:S(2)}, u32[]{:S(2)}) collective-permute-start(bf16[512,512]{1,0:T(8,128)(2,1)S(1)} %slice.31), channel_id=1, source_target_pairs={{1,0},{2,1},{3,2},{0,3},{5,4},{6,5},{7,6},{4,7},{9,8},{10,9},{11,1... | collective-permute-start | bytes 1572872 | tf_op jit(solution)/shard_map/ppermute | solution.py:287
  35.1 12.1 %copy-start.7 = (bf16[512,512]{1,0:T(8,128)(2,1)}, bf16[512,512]{1,0:T(8,128)(2,1)S(1)}, u32[]{:S(2)}) copy-start(bf16[512,512]{1,0:T(8,128)(2,1)S(1)} %collective-permute-done.3) | copy-start | bytes 1572868
  36.6 19.1 %collective-permute-start.4 = (bf16[128,1024]{1,0:T(8,128)(2,1)}, bf16[128,1024]{1,0:T(8,128)(2,1)}, u32[]{:S(2)}, u32[]{:S(2)}) collective-permute-start(bf16[128,1024]{1,0:T(8,128)(2,1)} %slice.32), channel_id=1, source_target_pairs={{0,4},{4,8},{8,12},{12,16},{16,20},{20,24},{24,28},{28,32},{32,36}... | collective-permute-start | bytes 786440 | tf_op jit(solution)/shard_map/ppermute | solution.py:294
  46.4 0.8 copy-start.5
  48.0 8.0 %collective-permute-start.5 = (bf16[128,1024]{1,0:T(8,128)(2,1)}, bf16[128,1024]{1,0:T(8,128)(2,1)}, u32[]{:S(2)}, u32[]{:S(2)}) collective-permute-start(bf16[128,1024]{1,0:T(8,128)(2,1)} %slice.33), channel_id=1, source_target_pairs={{4,0},{8,4},{12,8},{16,12},{20,16},{24,20},{28,24},{32,28},{36,32}... | collective-permute-start | bytes 786440 | tf_op jit(solution)/shard_map/ppermute | solution.py:295
  55.6 15.2 %copy-start.9 = (s32[1,2048]{1,0:T(1,128)S(1)}, s32[1,2048]{1,0:T(1,128)}, u32[]{:S(2)}) copy-start(s32[1,2048]{1,0:T(1,128)} %param.7) | copy-start | bytes 24580
  56.0 198.6 %all-to-all-start = ((bf16[128,128,256]{2,1,0:T(8,128)(2,1)}), bf16[128,128,256]{2,1,0:T(8,128)(2,1)}, u32[]{:S(2)}, u32[]{:S(2)}) async-start(bf16[128,128,256]{2,1,0:T(8,128)(2,1)} %pack_tiles.1), calls=%async_computation | async-start | bytes 16777216 | tf_op jit(solution)/shard_map/all_to_all | solution.py:300
  71.0 11.8 %slice-start = ((s8[6291456]{0:T(1024)(128)(4,1)}), s8[4194304]{0:T(1024)(128)(4,1)S(1)}, s32[]{:S(2)}) async-start(s8[6291456]{0:T(1024)(128)(4,1)} %bitcast.54), calls=%async_computation.2 | async-start | bytes 8388608
  73.2 7.8 %copy-start.6 = (bf16[512,512]{1,0:T(8,128)(2,1)S(1)}, bf16[512,512]{1,0:T(8,128)(2,1)}, u32[]{:S(2)}) copy-start(bf16[512,512]{1,0:T(8,128)(2,1)} %copy-done.5) | copy-start | bytes 1572868
  73.2 7.8 %copy-start.8 = (bf16[512,512]{1,0:T(8,128)(2,1)S(1)}, bf16[512,512]{1,0:T(8,128)(2,1)}, u32[]{:S(2)}) copy-start(bf16[512,512]{1,0:T(8,128)(2,1)} %copy-done.7) | copy-start | bytes 1572868
  73.2 9.5 %slice-start.1 = ((s8[6291456]{0:T(1024)(128)(4,1)}), s8[2097152]{0:T(1024)(128)(4,1)S(1)}, s32[]{:S(2)}) async-start(s8[6291456]{0:T(1024)(128)(4,1)} %bitcast.54), calls=%async_computation.3 | async-start | bytes 4194304
  73.2 9.5 %copy-start.4 = (bf16[1024,512]{1,0:T(8,128)(2,1)S(1)}, bf16[1024,512]{1,0:T(8,128)(2,1)}, u32[]{:S(2)}) copy-start(bf16[1024,512]{1,0:T(8,128)(2,1)} %copy-done.3) | copy-start | bytes 3145732
  76.2 9.9 %collective-permute-start.17 = (bf16[128,512]{1,0:T(8,128)(2,1)S(1)}, bf16[128,512]{1,0:T(8,128)(2,1)S(1)}, u32[]{:S(2)}, u32[]{:S(2)}) collective-permute-start(bf16[128,512]{1,0:T(8,128)(2,1)S(1)} %add_add_fusion), channel_id=1, source_target_pairs={{0,2},{1,3},{2,0},{3,1},{4,6},{5,7},{6,4},{7,5},{8,10},{9,11},{10,... | collective-permute-start | bytes 393224 | tf_op jit(solution)/shard_map/ppermute | solution.py:305
  78.3 7.1 %collective-permute-start.15 = (bf16[128,512]{1,0:T(8,128)(2,1)S(1)}, bf16[128,512]{1,0:T(8,128)(2,1)S(1)}, u32[]{:S(2)}, u32[]{:S(2)}) collective-permute-start(bf16[128,512]{1,0:T(8,128)(2,1)S(1)} %add_add_fusion), channel_id=1, source_target_pairs={{0,1},{1,2},{2,3},{3,0},{4,5},{5,6},{6,7},{7,4},{8,9},{9,10},{10,1... | collective-permute-start | bytes 393224 | tf_op jit(solution)/shard_map/ppermute | solution.py:303
  80.2 6.2 %collective-permute-start.16 = (bf16[128,512]{1,0:T(8,128)(2,1)S(1)}, bf16[128,512]{1,0:T(8,128)(2,1)S(1)}, u32[]{:S(2)}, u32[]{:S(2)}) collective-permute-start(bf16[128,512]{1,0:T(8,128)(2,1)S(1)} %add_add_fusion), channel_id=1, source_target_pairs={{1,0},{2,1},{3,2},{0,3},{5,4},{6,5},{7,6},{4,7},{9,8},{10,9},{11,1... | collective-permute-start | bytes 393224 | tf_op jit(solution)/shard_map/ppermute | solution.py:304
  265.0 57.2 %all-to-all-start.1 = ((bf16[64,128,128]{2,1,0:T(8,128)(2,1)}), bf16[64,128,128]{2,1,0:T(8,128)(2,1)S(1)}, u32[]{:S(2)}, u32[]{:S(2)}) async-start(bf16[64,128,128]{2,1,0:T(8,128)(2,1)} %rand_attend.1), calls=%async_computation.1 | async-start | bytes 4194304 | tf_op jit(solution)/shard_map/all_to_all | solution.py:316
